TPU v7x, 32 devices: a whole 2x2x4 slice. The times are simulated.
32 devices in a mesh: expert: 4 (over y, x), hidden: 8 (over z, core).
Axes of the slice: x: 2, y: 2, z: 4, core: 2. Of those that a mesh axis runs over, the one named last changes fastest.
Arguments:
- patches: bfloat16 [32768, 384], P(('expert', 'hidden')), may hold values from -6 to 6
- cotangent: bfloat16 [32768, 384], P(('expert', 'hidden')), may hold values from -6 to 6
- expert_ids: int32 [32768, 4], P(('expert', 'hidden')), may hold values from 0 to 15, all different within a row
- gates: float32 [32768, 4], P(('expert', 'hidden')), may hold values from 0.1 to 0.4
- task_ids: int32 [32768], P(('expert', 'hidden')), may hold values from 0 to 1
- segments: int32 [32, 1024], P(('expert', 'hidden')), may hold values from 0 to 7, never falling along the last dimension, each value on 1 to 512 neighbouring positions
- norm_params: float32 [6, 384], replicated, may hold values from 0.5 to 1.5
- attn_qkv: float32 [384, 1152], replicated, may hold values from -0.3125 to 0.3125
- attn_proj: float32 [384, 384], replicated, may hold values from -1.75 to 1.75
- expert_inner: float32 [1536, 16, 384], P('hidden', 'expert'), may hold values from -0.3125 to 0.3125
- expert_outer: float32 [1536, 16, 384], P('hidden', 'expert'), may hold values from -0.5 to 0.5
- norm_moment: float32 [6, 384], replicated, may hold values from -896 to 896
- qkv_moment: float32 [384, 1152], replicated, may hold values from -512 to 512
- proj_moment: float32 [384, 384], replicated, may hold values from -128 to 128
- inner_moment: float32 [1536, 16, 384], P('hidden', 'expert'), may hold values from -160 to 160
- outer_moment: float32 [1536, 16, 384], P('hidden', 'expert'), may hold values from -80 to 80
- norm_average: float32 [6, 384], replicated, may hold values from 0.5 to 1.5
- qkv_average: float32 [384, 1152], replicated, may hold values from -0.3125 to 0.3125
- proj_average: float32 [384, 384], replicated, may hold values from -1.75 to 1.75
- inner_average: float32 [1536, 16, 384], P('hidden', 'expert'), may hold values from -0.3125 to 0.3125
- outer_average: float32 [1536, 16, 384], P('hidden', 'expert'), may hold values from -0.5 to 0.5
Outputs:
- block_out: bfloat16 [32768, 384], P(('expert', 'hidden'))
- patch_grad: float32 [32768, 384], P(('expert', 'hidden'))
- expert_load: float32 [16], replicated
- norm_new: float32 [6, 384], replicated
- norm_moment_new: float32 [6, 384], replicated
- norm_average_new: float32 [6, 384], replicated
- qkv_new: float32 [384, 1152], replicated
- qkv_moment_new: float32 [384, 1152], replicated
- qkv_average_new: float32 [384, 1152], replicated
- proj_new: float32 [384, 384], replicated
- proj_moment_new: float32 [384, 384], replicated
- proj_average_new: float32 [384, 384], replicated
- inner_new: float32 [1536, 16, 384], P('hidden', 'expert')
- inner_moment_new: float32 [1536, 16, 384], P('hidden', 'expert')
- inner_average_new: float32 [1536, 16, 384], P('hidden', 'expert')
- outer_new: float32 [1536, 16, 384], P('hidden', 'expert')
- outer_moment_new: float32 [1536, 16, 384], P('hidden', 'expert')
- outer_average_new: float32 [1536, 16, 384], P('hidden', 'expert')
Inputs may be any that keep to these rules, and one draw needn't show every extreme that they name: `expert_ids`: each row names 4 different experts. `segments`: in each row the numbers never fall and each image has 1 to 512 slots.
All inputs are finite; a program needn't handle non-finite values.
Results may differ from a plain program's by a relative error of at most 0.012.
The roundings to bfloat16 on the way count: a program that leaves them out, or rounds other values in their place, can miss the bound.
Values may be sent and summed in bfloat16 or wider, within the bound.
No kernel may reach another device: no remote copies, remote signals or barrier semaphores. Data moves between devices by JAX's collectives and lax.ppermute only.
A program may use at most 320 MiB of HBM per device.

v0:
```python
import math

import jax
import jax.numpy as jnp
from jax import lax
from jax.sharding import PartitionSpec as P

D = 384
HEADS = 6
HEAD = 64
EXPERTS = 16
TOP = 4
TASKS = 2
CAP = 320


MOMENT_DECAY = 0.9
AVERAGE_DECAY = 0.9
RATE_NORM = 0.23
RATE_QKV = 0.064
RATE_PROJ = 1.4
RATE_INNER = 0.21
RATE_OUTER = 0.73
NORM_EPS = 1e-06
MASKED = -1e30


def layer_norm(values):
    center = values - jnp.mean(values, axis=-1, keepdims=True)
    spread = jnp.mean(center * center, axis=-1, keepdims=True)
    return center * lax.rsqrt(spread + NORM_EPS)


def first_norm(values, gain_row, offset_row):
    return layer_norm(values) * gain_row + offset_row


def exact_gelu(values):
    return jax.nn.gelu(values, approximate=False)


def routing(expert_ids, groups):
    flat_ids = expert_ids.reshape(-1)
    pair_count = flat_ids.shape[0]
    local_count = EXPERTS // groups
    onehot = (flat_ids[:, None] == jnp.arange(EXPERTS, dtype=jnp.int32)[None, :]).astype(jnp.int32)
    slot_place = jnp.sum(onehot * jnp.cumsum(onehot, axis=0), axis=1) - 1
    is_kept = slot_place < CAP
    slot_total = EXPERTS * CAP
    target = (flat_ids % local_count * groups + flat_ids // local_count) * CAP + slot_place
    target = jnp.where(is_kept, target, slot_total)
    source = jnp.full((slot_total + 1,), pair_count, jnp.int32)
    source = source.at[target].set(jnp.arange(pair_count, dtype=jnp.int32))[:slot_total]
    counts = jnp.sum(onehot * is_kept[:, None].astype(jnp.int32), axis=0)
    return (target, source, counts)


def attend_forward(query_heads, key_heads, value_heads, seg_marks, block_rows):
    score_scale = HEAD ** (-0.5)
    seq_length = query_heads.shape[0]
    outputs = []
    log_sums = []
    for row_start in range(0, seq_length, block_rows):
        query_rows = query_heads[row_start : row_start + block_rows]
        marks_rows = seg_marks[row_start : row_start + block_rows]
        scores = (
            jnp.einsum("qhd,khd->hqk", query_rows, key_heads, preferred_element_type=jnp.float32)
            * score_scale
        )
        scores = jnp.where(marks_rows[None, :, None] == seg_marks[None, None, :], scores, MASKED)
        row_peak = jnp.max(scores, axis=-1, keepdims=True)
        row_exp = jnp.exp(scores - row_peak)
        row_total = jnp.sum(row_exp, axis=-1, keepdims=True)
        weights_low = (row_exp / row_total).astype(jnp.bfloat16)
        mixed_rows = jnp.einsum(
            "hqk,khd->qhd", weights_low, value_heads, preferred_element_type=jnp.float32
        )
        outputs.append(mixed_rows.astype(jnp.bfloat16))
        log_sums.append(row_peak + jnp.log(row_total))
    return (jnp.concatenate(outputs, axis=0), log_sums)


def attend_backward(
    query_heads, key_heads, value_heads, seg_marks, mixed_grad, log_sums, block_rows
):
    score_scale = HEAD ** (-0.5)
    seq_length = query_heads.shape[0]
    key_grad = jnp.zeros(key_heads.shape, jnp.float32)
    value_grad = jnp.zeros(value_heads.shape, jnp.float32)
    query_grads = []
    for block_index in range(seq_length // block_rows):
        row_start = block_index * block_rows
        query_rows = query_heads[row_start : row_start + block_rows]
        marks_rows = seg_marks[row_start : row_start + block_rows]
        grad_rows = mixed_grad[row_start : row_start + block_rows]
        scores = (
            jnp.einsum("qhd,khd->hqk", query_rows, key_heads, preferred_element_type=jnp.float32)
            * score_scale
        )
        scores = jnp.where(marks_rows[None, :, None] == seg_marks[None, None, :], scores, MASKED)
        probs = jnp.exp(scores - log_sums[block_index])
        probs_low = probs.astype(jnp.bfloat16)
        value_grad = value_grad + jnp.einsum(
            "hqk,qhd->khd", probs_low, grad_rows, preferred_element_type=jnp.float32
        )
        prob_grad = jnp.einsum(
            "qhd,khd->hqk", grad_rows, value_heads, preferred_element_type=jnp.float32
        )
        row_dot = jnp.sum(prob_grad * probs, axis=-1, keepdims=True)
        score_grad = (probs * (prob_grad - row_dot)).astype(jnp.bfloat16)
        query_grads.append(
            jnp.einsum("hqk,khd->qhd", score_grad, key_heads, preferred_element_type=jnp.float32)
            * score_scale
        )
        key_grad = (
            key_grad
            + jnp.einsum("hqk,qhd->khd", score_grad, query_rows, preferred_element_type=jnp.float32)
            * score_scale
        )
    return (jnp.concatenate(query_grads, axis=0), key_grad, value_grad)


def expert_forward(rows_in, inner_part, outer_part):
    pre_act = jnp.einsum("erd,fed->erf", rows_in, inner_part, preferred_element_type=jnp.float32)
    act_low = exact_gelu(pre_act).astype(jnp.bfloat16)
    return jnp.einsum("erf,fed->erd", act_low, outer_part, preferred_element_type=jnp.float32)


def expert_backward_parts(rows_in, rows_grad, inner_part, outer_part):
    pre_act = jnp.einsum("erd,fed->erf", rows_in, inner_part, preferred_element_type=jnp.float32)
    act_val, gelu_back = jax.vjp(exact_gelu, pre_act)
    act_low = act_val.astype(jnp.bfloat16)
    act_grad = jnp.einsum("erd,fed->erf", rows_grad, outer_part, preferred_element_type=jnp.float32)
    pre_grad = gelu_back(act_grad)[0].astype(jnp.bfloat16)
    input_grad = jnp.einsum(
        "erf,fed->erd", pre_grad, inner_part, preferred_element_type=jnp.float32
    )
    return (input_grad, pre_grad, act_low)


def nesterov(weight, moment, average, grad, rate):
    moment_new = MOMENT_DECAY * moment + grad
    weight_new = weight - rate * (grad + MOMENT_DECAY * moment_new)
    average_new = AVERAGE_DECAY * average + (1.0 - AVERAGE_DECAY) * weight_new
    return (weight_new, moment_new, average_new)


def body(
    patches,
    cotangent,
    expert_ids,
    gates,
    task_ids,
    segments,
    norm_params,
    attn_qkv,
    attn_proj,
    expert_inner,
    expert_outer,
    norm_moment,
    qkv_moment,
    proj_moment,
    inner_moment,
    outer_moment,
    norm_average,
    qkv_average,
    proj_average,
    inner_average,
    outer_average,
):
    groups = lax.axis_size("expert")
    tok_count = patches.shape[0]
    tokens_all = tok_count * groups * lax.axis_size("hidden")
    local_count = EXPERTS // groups
    block_rows = min(512, tok_count)
    inputs = patches.astype(jnp.float32)
    seg_marks = segments[0]
    normed_one, first_back = jax.vjp(first_norm, inputs, norm_params[0], norm_params[1])
    attn_in = normed_one.astype(jnp.bfloat16)
    qkv_low = attn_qkv.astype(jnp.bfloat16)
    proj_low = attn_proj.astype(jnp.bfloat16)
    joined = jnp.dot(attn_in, qkv_low, preferred_element_type=jnp.float32).astype(jnp.bfloat16)
    joined = joined.reshape(tok_count, 3, HEADS, HEAD)
    query_heads = joined[:, 0]
    key_heads = joined[:, 1]
    value_heads = joined[:, 2]
    mixed, log_sums = attend_forward(query_heads, key_heads, value_heads, seg_marks, block_rows)
    mixed = mixed.reshape(tok_count, D)
    hidden_one = inputs + jnp.dot(mixed, proj_low, preferred_element_type=jnp.float32)
    task_hot = (task_ids[:, None] == jnp.arange(TASKS, dtype=jnp.int32)[None, :]).astype(
        jnp.float32
    )

    def second_norm(values, table):
        gain_rows = jnp.dot(task_hot, table[:TASKS], precision=lax.Precision.HIGHEST)
        bias_rows = jnp.dot(task_hot, table[TASKS:], precision=lax.Precision.HIGHEST)
        return layer_norm(values) * gain_rows + bias_rows

    normed_two, second_back = jax.vjp(second_norm, hidden_one, norm_params[2:])
    moe_in = normed_two.astype(jnp.bfloat16)
    target, source, counts = routing(expert_ids, groups)
    moe_pad = jnp.concatenate([moe_in, jnp.zeros((1, D), jnp.bfloat16)], axis=0)
    slots_out = moe_pad[source // TOP].reshape(local_count, groups, CAP, D)
    rows_in = lax.all_to_all(slots_out, "expert", split_axis=1, concat_axis=1, tiled=True).reshape(
        local_count, groups * CAP, D
    )
    inner_low = expert_inner.astype(jnp.bfloat16)
    outer_low = expert_outer.astype(jnp.bfloat16)
    inner_all, outer_all = (
        lax.all_gather(inner_low, "hidden", axis=0, tiled=True),
        lax.all_gather(outer_low, "hidden", axis=0, tiled=True),
    )
    expert_sum = expert_forward(rows_in, inner_all, outer_all)
    returned = lax.all_to_all(
        expert_sum.astype(jnp.bfloat16).reshape(local_count, groups, CAP, D),
        "expert",
        split_axis=1,
        concat_axis=1,
        tiled=True,
    )
    back_pad = jnp.concatenate(
        [returned.reshape(EXPERTS * CAP, D), jnp.zeros((1, D), jnp.bfloat16)], axis=0
    )
    routed = back_pad[target].reshape(tok_count, TOP, D)
    moe_sum = jnp.sum(gates[:, :, None] * routed.astype(jnp.float32), axis=1)
    block_out = (hidden_one + moe_sum).astype(jnp.bfloat16)
    out_grad = cotangent.astype(jnp.float32)
    pair_grad = (
        (gates[:, :, None] * out_grad[:, None, :]).astype(jnp.bfloat16).reshape(tok_count * TOP, D)
    )
    pair_pad = jnp.concatenate([pair_grad, jnp.zeros((1, D), jnp.bfloat16)], axis=0)
    slots_grad = pair_pad[source].reshape(local_count, groups, CAP, D)
    rows_grad = lax.all_to_all(
        slots_grad, "expert", split_axis=1, concat_axis=1, tiled=True
    ).reshape(local_count, groups * CAP, D)
    input_grad, pre_grad_all, act_all = expert_backward_parts(
        rows_in, rows_grad, inner_all, outer_all
    )
    inner_full = jnp.einsum(
        "erf,erd->fed", pre_grad_all, rows_in, preferred_element_type=jnp.float32
    )
    outer_full = jnp.einsum("erf,erd->fed", act_all, rows_grad, preferred_element_type=jnp.float32)
    inner_grad, outer_grad = (
        lax.psum_scatter(inner_full, "hidden", scatter_dimension=0, tiled=True),
        lax.psum_scatter(outer_full, "hidden", scatter_dimension=0, tiled=True),
    )
    back_rows = lax.all_to_all(
        input_grad.astype(jnp.bfloat16).reshape(local_count, groups, CAP, D),
        "expert",
        split_axis=1,
        concat_axis=1,
        tiled=True,
    )
    grad_pad = jnp.concatenate(
        [back_rows.reshape(EXPERTS * CAP, D), jnp.zeros((1, D), jnp.bfloat16)], axis=0
    )
    moe_grad = jnp.sum(grad_pad[target].reshape(tok_count, TOP, D).astype(jnp.float32), axis=1)
    hidden_grad, table_grad = second_back(moe_grad)
    hidden_grad = hidden_grad + out_grad
    attn_grad_low = hidden_grad.astype(jnp.bfloat16)
    proj_grad = jnp.einsum("td,te->de", mixed, attn_grad_low, preferred_element_type=jnp.float32)
    mixed_grad = jnp.einsum(
        "te,de->td", attn_grad_low, proj_low, preferred_element_type=jnp.float32
    )
    mixed_grad = mixed_grad.astype(jnp.bfloat16).reshape(tok_count, HEADS, HEAD)
    query_grad, key_grad, value_grad = attend_backward(
        query_heads, key_heads, value_heads, seg_marks, mixed_grad, log_sums, block_rows
    )
    joined_grad = (
        jnp.stack([query_grad, key_grad, value_grad], axis=1)
        .reshape(tok_count, 3 * D)
        .astype(jnp.bfloat16)
    )
    qkv_grad = jnp.einsum("td,te->de", attn_in, joined_grad, preferred_element_type=jnp.float32)
    attn_in_grad = jnp.einsum("te,de->td", joined_grad, qkv_low, preferred_element_type=jnp.float32)
    input_first, gain_grad, offset_grad = first_back(attn_in_grad)
    patch_grad = hidden_grad + input_first
    norm_grad = jnp.concatenate([gain_grad[None], offset_grad[None], table_grad], axis=0)
    qkv_sum, proj_sum, norm_sum, count_sum = lax.psum(
        (qkv_grad, proj_grad, norm_grad, counts.astype(jnp.float32)), ("expert", "hidden")
    )
    expert_load = count_sum * (EXPERTS / (tokens_all * TOP))
    root_tokens = math.sqrt(tokens_all)
    norm_new = nesterov(norm_params, norm_moment, norm_average, norm_sum, RATE_NORM / root_tokens)
    qkv_new = nesterov(attn_qkv, qkv_moment, qkv_average, qkv_sum, RATE_QKV / root_tokens)
    proj_new = nesterov(attn_proj, proj_moment, proj_average, proj_sum, RATE_PROJ / root_tokens)
    inner_new = nesterov(
        expert_inner, inner_moment, inner_average, inner_grad, RATE_INNER / root_tokens
    )
    outer_new = nesterov(
        expert_outer, outer_moment, outer_average, outer_grad, RATE_OUTER / root_tokens
    )
    return (
        block_out,
        patch_grad,
        expert_load,
        norm_new[0],
        norm_new[1],
        norm_new[2],
        qkv_new[0],
        qkv_new[1],
        qkv_new[2],
        proj_new[0],
        proj_new[1],
        proj_new[2],
        inner_new[0],
        inner_new[1],
        inner_new[2],
        outer_new[0],
        outer_new[1],
        outer_new[2],
    )


def solution(mesh):
    return jax.shard_map(
        body,
        mesh=mesh,
        in_specs=(
            P(("expert", "hidden"), None),
            P(("expert", "hidden"), None),
            P(("expert", "hidden"), None),
            P(("expert", "hidden"), None),
            P(("expert", "hidden")),
            P(("expert", "hidden"), None),
            P(),
            P(),
            P(),
            P("hidden", "expert", None),
            P("hidden", "expert", None),
            P(),
            P(),
            P(),
            P("hidden", "expert", None),
            P("hidden", "expert", None),
            P(),
            P(),
            P(),
            P("hidden", "expert", None),
            P("hidden", "expert", None),
        ),
        out_specs=(
            P(("expert", "hidden"), None),
            P(("expert", "hidden"), None),
            P(),
            P(),
            P(),
            P(),
            P(),
            P(),
            P(),
            P(),
            P(),
            P(),
            P("hidden", "expert", None),
            P("hidden", "expert", None),
            P("hidden", "expert", None),
            P("hidden", "expert", None),
            P("hidden", "expert", None),
            P("hidden", "expert", None),
        ),
        check_vma=False,
    )
```

profile of v0, /device:TPU:0, one launch (start us, length us, event | category | flops | bytes accessed | tf_op | source)
XLA Modules:
  0.0 1074.7 jit_solution(8279190066428974367)
XLA Ops:
  11.4 4.6 reduce-window.6
  17.2 15.5 %scatter_custom_fusion = s32[5121]{0:T(1024)S(1)} fusion(s32[4096]{0:T(1024)S(1)} %bitcast.146, s32[4096]{0:T(1024)S(1)} %iota.15, s32[]{:T(128)} %constant.65.clone.1), kind=kCustom, calls=%fused_computation.177 | custom fusion | bytes 20488 | tf_op jit(solution)/shard_map/scatter | solution.py:53
  33.3 3.4 mul.351
  36.8 7.8 mul.352
  44.5 3.3 multiply_convert_fusion.3
  48.1 21.2 %gather_fusion.2 = bf16[5120,384]{1,0:T(8,128)(2,1)} fusion(bf16[4097,384]{1,0:T(8,128)(2,1)S(1)} %concatenate.25, s32[5120]{0:T(1024)S(1)} %get-tuple-element.89), kind=kCustom, calls=%fused_computation.2 | custom fusion | bytes 7884800 | tf_op jit(solution)/shard_map/gather | solution.py:232
  69.3 4.4 copy.94
  73.8 5.9 all-to-all-start.2
  81.1 3.0 convolution_convert_fusion.2
  84.1 2.8 copy.82
  87.6 2.4 fusion.91
  90.0 2.4 fusion.92
  92.4 2.8 fusion.7
  95.3 2.8 fusion.6
  98.1 3.2 fusion.47
  101.3 3.3 fusion.46
  110.3 21.2 %gather_fusion = bf16[5120,384]{1,0:T(8,128)(2,1)} fusion(bf16[1025,384]{1,0:T(8,128)(2,1)S(1)} %concatenate.23, s32[5120]{0:T(1024)S(1)} %get-tuple-element.90), kind=kCustom, calls=%fused_computation | custom fusion | bytes 7884800 | tf_op jit(solution)/shard_map/gather | solution.py:203
  131.6 4.4 copy.87
  136.0 4.9 all-to-all-start
  141.9 4.5 copy.95
  146.4 40.3 %all-to-all-done = bf16[4,4,320,384]{3,2,0,1:T(8,128)(2,1)} async-done(((bf16[4,4,320,384]{3,2,0,1:T(8,128)(2,1)}), bf16[4,4,320,384]{3,2,0,1:T(8,128)(2,1)}, u32[]{:S(2)}, u32[]{:S(2)}) %all-to-all-start) | async-done | bytes 3932192 | tf_op jit(solution)/shard_map/all_to_all | solution.py:204
  186.7 4.5 copy.88
  191.2 26.0 %fusion.11 = (u8[1280,1536]{1,0:T(8,128)(4,1)S(1)}, u8[1280,1536]{1,0:T(8,128)(4,1)}, f32[4,1280,1536]{2,1,0:T(8,128)}) fusion(bf16[4,1280,384]{2,1,0:T(8,128)(2,1)} %bitcast.135, bf16[1536,4,384]{2,0,1:T(8,128)(2,1)} %all-gather.3.cloned.1.call-done), kind=kOutput, calls=%fused_computation.43 | convolution fusion | flops 6138101760 | bytes 44040192 | tf_op jit(solution)/shard_map/erd,fed->erf/dot_general | solution.py:124
  217.2 74.1 %multiply_convert_fusion = (bf16[4,1280,1536]{2,1,0:T(8,128)(2,1)}, f32[4,1280,1536]{2,1,0:T(8,128)}) fusion(f32[4,1280,1536]{2,1,0:T(8,128)} %get-tuple-element.101, u8[1280,1536]{1,0:T(8,128)(4,1)} %get-tuple-element.55, u8[1280,1536]{1,0:T(8,128)(4,1)S(1)} %get-tuple-element.54), kind=kLoop, calls=%fused_computation.13 | loop fusion | flops 550502400 | bytes 82575360 | tf_op jit(solution)/shard_map/convert_element_type | solution.py:125
  291.3 13.1 %convolution_convert_fusion.1 = bf16[4,1280,384]{2,1,0:T(8,128)(2,1)S(1)} fusion(bf16[4,1280,1536]{2,1,0:T(8,128)(2,1)} %get-tuple-element.84, bf16[1536,4,384]{2,0,1:T(8,128)(2,1)} %all-gather.5.cloned.1.call-done), kind=kOutput, calls=%fused_computation.55 | convolution fusion | flops 6041763840 | bytes 24379392 | tf_op jit(solution)/shard_map/erf,fed->erd/dot_general | solution.py:126
  304.4 2.4 copy.91
  306.8 5.0 all-to-all-start.1
  311.9 31.4 %add_convert_fusion = bf16[4,1280,1536]{2,1,0:T(8,128)(2,1)} fusion(f32[4,1280,1536]{2,1,0:T(8,128)} %get-tuple-element.85, bf16[4,1280,384]{2,1,0:T(8,128)(2,1)} %bitcast.133, bf16[1536,4,384]{2,0,1:T(8,128)(2,1)} %all-gather.5.cloned.1.call-done, f32[4,1280,1536]{2,1,0:T(8,128)} %get-tuple-element.101), kind=kOutput, calls=%fused_computation.12 | convolution fusion | flops 6149898240 | bytes 87293952 | tf_op jit(solution)/shard_map/erd,fed->erf/dot_general | solution.py:133
  343.3 13.1 %convolution_convert_fusion = bf16[4,1280,384]{2,1,0:T(8,128)(2,1)S(1)} fusion(bf16[4,1280,1536]{2,1,0:T(8,128)(2,1)} %add_convert_fusion, bf16[1536,4,384]{2,0,1:T(8,128)(2,1)} %all-gather.3.cloned.1.call-done), kind=kOutput, calls=%fused_computation.54 | convolution fusion | flops 6041763840 | bytes 24379392 | tf_op jit(solution)/shard_map/erf,fed->erd/dot_general | solution.py:135
  356.4 2.4 copy.96
  358.7 4.9 all-to-all-start.3
  363.8 13.7 %convolution_bitcast_fusion.1 = f32[1536,4,384]{0,2,1:T(8,128)} fusion(bf16[4,1280,384]{2,1,0:T(8,128)(2,1)} %bitcast.136, bf16[4,1280,1536]{2,1,0:T(8,128)(2,1)} %add_convert_fusion), kind=kOutput, calls=%fused_computation.53 | convolution fusion | flops 6039797760 | bytes 29097984 | tf_op jit(solution)/shard_map/erf,erd->fed/dot_general | solution.py:239
  377.5 12.0 %copy.99 = f32[1536,4,384]{2,1,0:T(4,128)} copy(f32[1536,4,384]{0,2,1:T(8,128)} %convolution_bitcast_fusion.1) | data formatting | bytes 18874368 | tf_op jit(solution)/shard_map/erf,erd->fed/transpose | solution.py:239
  389.4 2.5 copy.92
  392.0 2.3 concatenate.24
  394.2 13.8 %all-to-all-done.3 = bf16[4,4,320,384]{3,2,0,1:T(8,128)(2,1)} async-done(((bf16[4,4,320,384]{3,2,0,1:T(8,128)(2,1)}), bf16[4,4,320,384]{3,2,0,1:T(8,128)(2,1)}, u32[]{:S(2)}, u32[]{:S(2)}) %all-to-all-start.3) | async-done | bytes 3932192 | tf_op jit(solution)/shard_map/all_to_all | solution.py:247
  408.1 2.5 copy.97
  410.6 2.3 concatenate.26
  412.9 19.3 %gather_fusion.1 = bf16[4096,384]{1,0:T(8,128)(2,1)} fusion(bf16[5121,384]{1,0:T(8,128)(2,1)} %concatenate.24, s32[4096]{0:T(1024)S(1)} %broadcast_clamp_fusion), kind=kCustom, calls=%fused_computation.1 | custom fusion | bytes 6307840 | tf_op jit(solution)/shard_map/gather | solution.py:224
  432.2 16.7 %gather_fusion.3 = bf16[4096,384]{1,0:T(8,128)(2,1)S(1)} fusion(bf16[5121,384]{1,0:T(8,128)(2,1)} %concatenate.26, s32[4096]{0:T(1024)S(1)} %broadcast_clamp_fusion), kind=kCustom, calls=%fused_computation.3 | custom fusion | bytes 6307840 | tf_op jit(solution)/shard_map/gather | solution.py:257
  448.9 3.7 reshape.408
  452.6 7.8 reduce_sum.194
  460.4 2.4 multiply_reduce_fusion.3
  462.8 6.9 reshape.407
  469.7 17.8 %multiply_reduce_fusion.2 = f32[1024,384]{1,0:T(8,128)S(1)} fusion(f32[1024,4,384]{2,1,0:T(4,128)} %reshape.407, f32[1024,4]{1,0:T(8,128)S(1)} %copy-done.26), kind=kLoop, calls=%fused_computation.49 | loop fusion | flops 2752512 | bytes 7880704 | tf_op jit(solution)/shard_map/reduce_sum | solution.py:225
  493.0 7.3 multiply_reduce_fusion.1
  500.3 10.0 multiply_convert_fusion.2
  510.3 5.8 fusion.45
  516.1 5.2 fusion.61
  521.3 3.5 fusion.12
  524.8 8.0 multiply_reduce_fusion
  532.8 4.5 fusion.36
  537.4 6.5 multiply_convert_fusion.1
  549.1 2.8 fusion.83
  552.0 13.4 %convolution_bitcast_fusion = f32[1536,4,384]{0,2,1:T(8,128)} fusion(bf16[4,1280,384]{2,1,0:T(8,128)(2,1)} %bitcast.134, bf16[4,1280,1536]{2,1,0:T(8,128)(2,1)} %get-tuple-element.84), kind=kOutput, calls=%fused_computation.52 | convolution fusion | flops 6039797760 | bytes 29097984 | tf_op jit(solution)/shard_map/erf,erd->fed/dot_general | solution.py:242
  565.4 12.0 %copy.101 = f32[1536,4,384]{2,1,0:T(4,128)} copy(f32[1536,4,384]{0,2,1:T(8,128)} %convolution_bitcast_fusion) | data formatting | bytes 18874368 | tf_op jit(solution)/shard_map/erf,erd->fed/transpose | solution.py:242
  579.4 4.2 fusion.30
  588.0 39.8 %all-reduce.8 = (f32[16]{0:T(128)S(1)}, f32[6,384]{1,0:T(8,128)S(1)}) all-reduce(f32[16]{0:T(128)} %convert_element_type.150, f32[6,384]{1,0:T(8,128)S(1)} %pad_maximum_fusion.2), channel_id=1, replica_groups=mesh['expert'=4,'hidden'=8] {'expert','hidden'}, use_global_device_ids=true, to_apply=%region_21.22 | all-reduce | flops 2320 | bytes 18560 | tf_op jit(solution)/shard_map/psum | solution.py:279
  630.4 3.4 add_add_fusion.2
  633.8 54.2 %all-reduce.14.cloned.1.call-done = (f32[384,1152]{1,0:T(8,128)}, f32[384,384]{1,0:T(8,128)}) async-done(((f32[384,1152]{1,0:T(8,128)}, f32[384,384]{1,0:T(8,128)}), (f32[384,1152]{1,0:T(8,128)}, f32[384,384]{1,0:T(8,128)})) %all-reduce.14.cloned.1.call-update) | async-done | bytes 2359312 | tf_op jit(solution)/shard_map/psum | solution.py:279
  688.0 2.5 multiply_add_fusion.6
  690.6 5.8 multiply_add_fusion
  696.3 365.3 %all-reduce.16.cloned.1.call-done = (f32[1536,4,384]{2,1,0:T(4,128)}, f32[1536,4,384]{2,1,0:T(4,128)}) async-done(((f32[1536,4,384]{2,1,0:T(4,128)}, f32[1536,4,384]{2,1,0:T(4,128)}), (f32[1536,4,384]{2,1,0:T(4,128)}, f32[1536,4,384]{2,1,0:T(4,128)})) %all-reduce.16.cloned.1.call-update) | async-done | bytes 18874384
  1061.6 6.1 multiply_add_fusion.2
  (235 shorter events, 33.4 us)
Async XLA Ops:
  7.2 25.6 %copy-start.70 = (f32[1024,4]{0,1:T(4,128)S(1)}, f32[1024,4]{0,1:T(4,128)}, u32[]{:S(2)}) copy-start(f32[1024,4]{0,1:T(4,128)} %param.24) | copy-start | bytes 49156
  7.2 26.1 %copy-start.15 = (bf16[1024,384]{1,0:T(8,128)(2,1)S(1)}, bf16[1024,384]{1,0:T(8,128)(2,1)}, u32[]{:S(2)}) copy-start(bf16[1024,384]{1,0:T(8,128)(2,1)} %param.22) | copy-start | bytes 2359300
  7.2 184.0 %all-gather.3.cloned.1.call-start = ((), (), s32[]{:S(2)}) async-start(), calls=%async_computation.4 | async-start | bytes 5308416 | tf_op jit(solution)/shard_map/all_gather | solution.py:210
  10.7 26.0 %copy-start.37 = (s32[4096]{0:T(1024)}, s32[4096]{0:T(1024)S(1)}, u32[]{:S(2)}) copy-start(s32[4096]{0:T(1024)S(1)} %eq.102) | copy-start | bytes 49156
  17.0 15.8 %copy-start.39 = (s32[4096]{0:T(1024)}, s32[4096]{0:T(1024)S(1)}, u32[]{:S(2)}) copy-start(s32[4096]{0:T(1024)S(1)} %fusion.63) | copy-start | bytes 49156
  17.2 15.6 %copy-start.52 = (s32[4096,1]{0,1:T(1,128)}, s32[4096,1]{0,1:T(1,128)S(1)}, u32[]{:S(2)}) copy-start(s32[4096,1]{0,1:T(1,128)S(1)} %compare_select_fusion) | copy-start | bytes 49156
  33.0 11.5 %copy-start.25 = (f32[1024,4]{1,0:T(8,128)}, f32[1024,4]{1,0:T(8,128)S(1)}, u32[]{:S(2)}) copy-start(f32[1024,4]{1,0:T(8,128)S(1)} %copy.83) | copy-start | bytes 49156
  73.8 5.9 copy-start.12
  73.8 6.7 copy-start.69
  73.8 6.7 copy-start.46
  73.8 7.3 copy-start.31
  73.8 62.2 %all-to-all-start.2 = ((bf16[4,4,320,384]{3,2,0,1:T(8,128)(2,1)}), bf16[4,4,320,384]{3,2,0,1:T(8,128)(2,1)}, u32[]{:S(2)}, u32[]{:S(2)}) async-start(bf16[4,4,320,384]{3,2,0,1:T(8,128)(2,1)} %copy.94), calls=%async_computation.2 | async-start | bytes 7864320 | tf_op jit(solution)/shard_map/all_to_all | solution.py:233
  86.9 14.3 %copy-start.6 = (bf16[1024,1152]{0,1:T(8,128)(2,1)}, bf16[1024,1152]{0,1:T(8,128)(2,1)S(1)}, u32[]{:S(2)}) copy-start(bf16[1024,1152]{0,1:T(8,128)(2,1)S(1)} %copy.82) | copy-start | bytes 7077892
  90.0 8.1 copy-start.1
  90.0 8.1 copy-start.44
  92.4 8.9 copy-start
  95.3 2.9 copy-start.50
  101.3 3.5 copy-start.20
  105.6 4.7 copy-start.2
  105.6 4.7 copy-start.41
  106.7 3.6 copy-start.56
  136.0 5.0 copy-start.23
  136.0 50.7 %all-to-all-start = ((bf16[4,4,320,384]{3,2,0,1:T(8,128)(2,1)}), bf16[4,4,320,384]{3,2,0,1:T(8,128)(2,1)}, u32[]{:S(2)}, u32[]{:S(2)}) async-start(bf16[4,4,320,384]{3,2,0,1:T(8,128)(2,1)} %copy.87), calls=%async_computation | async-start | bytes 7864320 | tf_op jit(solution)/shard_map/all_to_all | solution.py:204
  140.9 150.4 %all-gather.5.cloned.1.call-start = ((), (), s32[]{:S(2)}) async-start(), calls=%async_computation.5 | async-start | bytes 5308416 | tf_op jit(solution)/shard_map/all_gather | solution.py:211
  306.8 51.9 %all-to-all-start.1 = ((bf16[4,4,320,384]{3,2,0,1:T(8,128)(2,1)}), bf16[4,4,320,384]{3,2,0,1:T(8,128)(2,1)}, u32[]{:S(2)}, u32[]{:S(2)}) async-start(bf16[4,4,320,384]{3,2,0,1:T(8,128)(2,1)} %copy.91), calls=%async_computation.1 | async-start | bytes 7864320 | tf_op jit(solution)/shard_map/all_to_all | solution.py:214
  358.7 5.0 copy-start.53
  358.7 5.0 copy-start.45
  358.7 5.0 copy-start.51
  358.7 49.3 %all-to-all-start.3 = ((bf16[4,4,320,384]{3,2,0,1:T(8,128)(2,1)}), bf16[4,4,320,384]{3,2,0,1:T(8,128)(2,1)}, u32[]{:S(2)}, u32[]{:S(2)}) async-start(bf16[4,4,320,384]{3,2,0,1:T(8,128)(2,1)} %copy.96), calls=%async_computation.3 | async-start | bytes 7864320 | tf_op jit(solution)/shard_map/all_to_all | solution.py:247
  363.7 324.3 %all-reduce.14.cloned.1.call-start = ((), (), s32[]{:S(2)}) async-start(), calls=%async_computation.6 | async-start | bytes 4718592 | tf_op jit(solution)/shard_map/psum | solution.py:279
  452.6 7.8 copy-start.3
  452.6 7.8 copy-start.42
  460.4 2.4 copy-start.66
  462.8 6.9 copy-start.26
  469.7 17.8 %copy-start.4 = (f32[1024,384]{1,0:T(8,128)S(1)}, f32[1024,384]{1,0:T(8,128)}, u32[]{:S(2)}) copy-start(f32[1024,384]{1,0:T(8,128)} %reduce_sum.194) | copy-start | bytes 4718596
  469.7 17.8 %copy-start.11 = (f32[1024,384]{1,0:T(8,128)S(1)}, f32[1024,384]{1,0:T(8,128)}, u32[]{:S(2)}) copy-start(f32[1024,384]{1,0:T(8,128)} %copy-done.10) | copy-start | bytes 4718596
  469.7 17.8 %copy-start.57 = (f32[1024]{0:T(1024)S(1)}, f32[1024]{0:T(1024)}, u32[]{:S(2)}) copy-start(f32[1024]{0:T(1024)} %copy-done.56) | copy-start | bytes 12292
  469.7 23.2 %slice-start = ((s8[12582912]{0:T(1024)(128)(4,1)}), s8[4194304]{0:T(1024)(128)(4,1)S(1)}, s32[]{:S(2)}) async-start(s8[12582912]{0:T(1024)(128)(4,1)} %bitcast.113), calls=%async_computation.8 | async-start | bytes 8388608
  487.6 5.4 slice-start.1
  489.2 3.7 copy-start.9
  489.2 3.7 copy-start.59
  489.3 3.7 slice-start.2
  493.0 7.4 copy-start.27
  500.3 10.0 copy-start.7
  500.3 21.0 %slice-start.3 = ((s8[12582912]{0:T(1024)(128)(4,1)}), s8[4194304]{0:T(1024)(128)(4,1)S(1)}, s32[]{:S(2)}) async-start(s8[12582912]{0:T(1024)(128)(4,1)} %bitcast.115), calls=%async_computation.11 | async-start | bytes 8388608
  500.3 21.0 %slice-start.4 = ((s8[12582912]{0:T(1024)(128)(4,1)}), s8[4194304]{0:T(1024)(128)(4,1)S(1)}, s32[]{:S(2)}) async-start(s8[12582912]{0:T(1024)(128)(4,1)} %bitcast.115), calls=%async_computation.12 | async-start | bytes 8388608
  510.3 11.0 %slice-start.5 = ((s8[12582912]{0:T(1024)(128)(4,1)}), s8[4194304]{0:T(1024)(128)(4,1)S(1)}, s32[]{:S(2)}) async-start(s8[12582912]{0:T(1024)(128)(4,1)} %bitcast.115), calls=%async_computation.13 | async-start | bytes 8388608
  516.1 5.2 copy-start.28
  537.4 6.6 copy-start.8
  551.9 509.7 %all-reduce.16.cloned.1.call-start = ((), (), s32[]{:S(2)}) async-start(), calls=%async_computation.7 | async-start | bytes 37748736
  579.4 4.3 copy-start.64
  579.4 5.9 copy-start.5
  579.4 5.9 copy-start.55
  583.6 3.7 copy-start.19
  583.6 2.5 copy-start.43
  583.6 2.5 copy-start.58
  583.6 45.4 %copy-start.47 = (f32[6,384]{1,0:T(8,128)S(1)}, f32[6,384]{1,0:T(8,128)}, u32[]{:S(2)}) copy-start(f32[6,384]{1,0:T(8,128)} %param.27) | copy-start | bytes 27652
  583.6 46.7 %copy-start.60 = (f32[1024]{0:T(1024)S(1)}, f32[1024]{0:T(1024)}, u32[]{:S(2)}) copy-start(f32[1024]{0:T(1024)} %copy-done.59) | copy-start | bytes 12292
  587.3 100.7 %copy-start.35 = (f32[384,384]{1,0:T(8,128)S(1)}, f32[384,384]{1,0:T(8,128)}, u32[]{:S(2)}) copy-start(f32[384,384]{1,0:T(8,128)} %param.39) | copy-start | bytes 1769476
  587.3 100.7 %copy-start.36 = (f32[384,384]{1,0:T(8,128)S(1)}, f32[384,384]{1,0:T(8,128)}, u32[]{:S(2)}) copy-start(f32[384,384]{1,0:T(8,128)} %param.34) | copy-start | bytes 1769476
  688.0 2.6 copy-start.32
  690.5 371.1 %copy-start.22 = (f32[192,4,384]{2,1,0:T(4,128)S(1)}, f32[192,4,384]{2,1,0:T(4,128)}, u32[]{:S(2)}) copy-start(f32[192,4,384]{2,1,0:T(4,128)} %param.30) | copy-start | bytes 3538948
  690.5 371.1 %copy-start.24 = (f32[192,4,384]{2,1,0:T(4,128)S(1)}, f32[192,4,384]{2,1,0:T(4,128)}, u32[]{:S(2)}) copy-start(f32[192,4,384]{2,1,0:T(4,128)} %param.31) | copy-start | bytes 3538948
  690.6 371.1 %copy-start.34 = (f32[192,4,384]{2,1,0:T(4,128)S(1)}, f32[192,4,384]{2,1,0:T(4,128)}, u32[]{:S(2)}) copy-start(f32[192,4,384]{2,1,0:T(4,128)} %param.41) | copy-start | bytes 3538948
  (24 other events, 31.5 us)
Sparse Core Ops, SparseCore 0:
  10.2 53.9 all-gather.2
  143.9 53.9 all-gather.4
  552.0 135.8 all-reduce.13
  690.4 371.1 all-reduce.15
where the time goes:
time: 1080 us; the launch traced here: 1070 us
  waiting for transfers between devices  474 us (44%)
  local copies, waits for them, and re-layouts  188 us (17%)
  matrix products  177 us (16%)
  other arithmetic  159 us (15%)
  blocking collectives  39.8 us (4%)
  starting transfers between devices  21 us (2%)
  between operations  16.1 us (1%)
    unnamed x5, waiting for transfers between devices  365 us
    convert_element_type x1, other arithmetic, expert_forward(): act_low = exact_gelu(pre_act).astype(jnp.bfloat16)  74.1 us
    psum x1, waiting for transfers between devices, body(): lax.psum((qkv_grad, proj_grad, norm_grad, counts.astype(jnp.float32)), ('...  54.2 us
    all_to_all x1, waiting for transfers between devices, body(): lax.all_to_all(slots_out, 'expert', split_axis=1, concat_axis=1, tiled=True)  40.3 us
    psum x1, blocking collectives, body(): lax.psum((qkv_grad, proj_grad, norm_grad, counts.astype(jnp.float32)), ('...  39.8 us
    dot_general x1, matrix products, expert_backward_parts(): jnp.einsum('erd,fed->erf', rows_grad, outer_part, preferred_element_type=...  31.4 us
    dot_general x1, matrix products, expert_forward(): jnp.einsum('erd,fed->erf', rows_in, inner_part, preferred_element_type=jn...  26 us
  transfers between devices with their start and end apart: 8, of which 4 were waited for; matrix products, arithmetic and copies ran while one was open for 33% of the time, Pallas kernels for 0%

commit v1 on v0

--- a/solution.py
+++ b/solution.py
@@ -136,6 +136,41 @@
         "erf,fed->erd", pre_grad, inner_part, preferred_element_type=jnp.float32
     )
     return (input_grad, pre_grad, act_low)
+
+
+def butterfly_sum(value, wire):
+    sizes = [("hidden", lax.axis_size("hidden")), ("expert", lax.axis_size("expert"))]
+    steps = []
+    for axis, size in sizes:
+        bit = 1
+        while bit < size:
+            steps.append((axis, size, bit))
+            bit *= 2
+    steps = steps[:1] + [s for s in steps if s[0] == "expert"] + [s for s in steps[1:] if s[0] == "hidden"]
+    value = value.astype(jnp.float32)
+    done = []
+    for axis, size, bit in steps:
+        half = value.shape[0] // 2
+        if value.shape[0] % 2 or half % 8:
+            break
+        done.append((axis, size, bit))
+        upper = (lax.axis_index(axis) & bit) > 0
+        low_half, high_half = value[:half], value[half:]
+        keep = jnp.where(upper, high_half, low_half)
+        send = jnp.where(upper, low_half, high_half).astype(wire)
+        got = lax.ppermute(send, axis, [(i, i ^ bit) for i in range(size)])
+        value = keep + got.astype(jnp.float32)
+    for axis, size, bit in steps[len(done):]:
+        got = lax.ppermute(value.astype(wire), axis, [(i, i ^ bit) for i in range(size)])
+        value = value + got.astype(jnp.float32)
+    value = value.astype(wire)
+    for axis, size, bit in done[::-1]:
+        upper = (lax.axis_index(axis) & bit) > 0
+        got = lax.ppermute(value, axis, [(i, i ^ bit) for i in range(size)])
+        first = jnp.where(upper, got, value)
+        second = jnp.where(upper, value, got)
+        value = jnp.concatenate([first, second], axis=0)
+    return value.astype(jnp.float32)
 
 
 def nesterov(weight, moment, average, grad, rate):
@@ -204,11 +239,12 @@
     rows_in = lax.all_to_all(slots_out, "expert", split_axis=1, concat_axis=1, tiled=True).reshape(
         local_count, groups * CAP, D
     )
-    inner_low = expert_inner.astype(jnp.bfloat16)
-    outer_low = expert_outer.astype(jnp.bfloat16)
+    own_units = expert_inner.shape[0]
+    inner_low = expert_inner.astype(jnp.bfloat16).reshape(own_units, local_count * D)
+    outer_low = expert_outer.astype(jnp.bfloat16).reshape(own_units, local_count * D)
     inner_all, outer_all = (
-        lax.all_gather(inner_low, "hidden", axis=0, tiled=True),
-        lax.all_gather(outer_low, "hidden", axis=0, tiled=True),
+        lax.all_gather(inner_low, "hidden", axis=0, tiled=True).reshape(-1, local_count, D),
+        lax.all_gather(outer_low, "hidden", axis=0, tiled=True).reshape(-1, local_count, D),
     )
     expert_sum = expert_forward(rows_in, inner_all, outer_all)
     returned = lax.all_to_all(
@@ -236,14 +272,17 @@
     input_grad, pre_grad_all, act_all = expert_backward_parts(
         rows_in, rows_grad, inner_all, outer_all
     )
-    inner_full = jnp.einsum(
-        "erf,erd->fed", pre_grad_all, rows_in, preferred_element_type=jnp.float32
-    )
-    outer_full = jnp.einsum("erf,erd->fed", act_all, rows_grad, preferred_element_type=jnp.float32)
-    inner_grad, outer_grad = (
-        lax.psum_scatter(inner_full, "hidden", scatter_dimension=0, tiled=True),
-        lax.psum_scatter(outer_full, "hidden", scatter_dimension=0, tiled=True),
-    )
+    def weight_sums(left, right):
+        parts = [
+            jnp.einsum("rf,rd->fd", left[e], right[e], preferred_element_type=jnp.float32).astype(jnp.bfloat16)
+            for e in range(local_count)
+        ]
+        full = jnp.concatenate(parts, axis=1)
+        mine = lax.psum_scatter(full, "hidden", scatter_dimension=0, tiled=True)
+        return mine.astype(jnp.float32).reshape(own_units, local_count, D)
+
+    inner_grad = weight_sums(pre_grad_all, rows_in)
+    outer_grad = weight_sums(act_all, rows_grad)
     back_rows = lax.all_to_all(
         input_grad.astype(jnp.bfloat16).reshape(local_count, groups, CAP, D),
         "expert",
@@ -276,9 +315,15 @@
     input_first, gain_grad, offset_grad = first_back(attn_in_grad)
     patch_grad = hidden_grad + input_first
     norm_grad = jnp.concatenate([gain_grad[None], offset_grad[None], table_grad], axis=0)
-    qkv_sum, proj_sum, norm_sum, count_sum = lax.psum(
-        (qkv_grad, proj_grad, norm_grad, counts.astype(jnp.float32)), ("expert", "hidden")
-    )
+    big = jnp.concatenate([qkv_grad, proj_grad], axis=1)
+    pad_rows = -big.shape[0] % 512
+    big = jnp.concatenate([big, jnp.zeros((pad_rows, big.shape[1]), jnp.float32)], axis=0)
+    big_sum = butterfly_sum(big, jnp.bfloat16)[:D]
+    qkv_sum, proj_sum = big_sum[:, : 3 * D], big_sum[:, 3 * D :]
+    count_row = jnp.pad(counts.astype(jnp.float32), (0, D - EXPERTS))[None]
+    small = jnp.concatenate([norm_grad, count_row, jnp.zeros((1, D), jnp.float32)], axis=0)
+    small_sum = butterfly_sum(small, jnp.float32)
+    norm_sum, count_sum = small_sum[:6], small_sum[6, :EXPERTS]
     expert_load = count_sum * (EXPERTS / (tokens_all * TOP))
     root_tokens = math.sqrt(tokens_all)
     norm_new = nesterov(norm_params, norm_moment, norm_average, norm_sum, RATE_NORM / root_tokens)

time: 1080 us -> 821 us (0.76)
  waiting for transfers between devices: 474 us -> 216 us
  blocking collectives: 39.8 us -> 0 us
  local copies, waits for them, and re-layouts: 188 us -> 212 us
  matrix products: 177 us -> 166 us
  other arithmetic: 159 us -> 170 us
    unnamed x5 -> x6, waiting for transfers between devices: 365 us -> 55.4 us
    psum x1 -> x0, waiting for transfers between devices: 54.2 us -> none  [body(): lax.psum((qkv_grad, proj_grad, norm_grad, counts.astype(jnp.float32)), ('...]
    all_gather x1, waiting for transfers between devices: 0.02 us -> 45.3 us  [body(): lax.all_gather(outer_low, 'hidden', axis=0, tiled=True)]
    all_to_all x1, waiting for transfers between devices: 0.01 us -> 39.8 us  [body(): lax.all_to_all(slots_grad, 'expert', split_axis=1, concat_axis=1, tiled=T...]
    psum x1 -> x0, blocking collectives: 39.8 us -> none  [body(): lax.psum((qkv_grad, proj_grad, norm_grad, counts.astype(jnp.float32)), ('...]
    ppermute x0 -> x15, waiting for transfers between devices: none -> 39.2 us  [the longest x5 15.5 us: butterfly_sum(): got = lax.ppermute(value, axis, [(i, i ^ bit) for i in range(size)])]
    all_to_all x1, waiting for transfers between devices: 40.3 us -> 4.81 us  [body(): lax.all_to_all(slots_out, 'expert', split_axis=1, concat_axis=1, tiled=True)]
    transpose x2 -> x0, local copies, waits for them, and re-layouts: 24 us -> none  [the longest x1 12 us: body(): jnp.einsum('erf,erd->fed', pre_grad_all, rows_in, preferred_element_type=...]
  transfers between devices with their start and end apart: 8 -> 23, of which waited for: 4 -> 16; matrix products, arithmetic and copies ran while one was open for 33% -> 29% of each run, Pallas kernels for 0% -> 0%
where the time goes in v1:
time: 821 us; the launch traced here: 809 us
  waiting for transfers between devices  216 us (26%)
  local copies, waits for them, and re-layouts  212 us (26%)
  other arithmetic  170 us (21%)
  matrix products  166 us (20%)
  starting transfers between devices  29.5 us (4%)
  between operations  15.7 us (2%)
    convert_element_type x1, other arithmetic, expert_forward(): act_low = exact_gelu(pre_act).astype(jnp.bfloat16)  74.8 us
    unnamed x6, waiting for transfers between devices  55.4 us
    all_gather x1, waiting for transfers between devices, body(): lax.all_gather(outer_low, 'hidden', axis=0, tiled=True)  45.3 us
    all_to_all x1, waiting for transfers between devices, body(): lax.all_to_all(slots_grad, 'expert', split_axis=1, concat_axis=1, tiled=T...  39.8 us
    unnamed x218, local copies, waits for them, and re-layouts  32.7 us
    dot_general x1, matrix products, expert_backward_parts(): jnp.einsum('erd,fed->erf', rows_grad, outer_part, preferred_element_type=...  31.5 us
    all_to_all x1, waiting for transfers between devices, body(): lax.all_to_all(input_grad.astype(jnp.bfloat16).reshape(local_count, group...  31.1 us
    dot_general x1, matrix products, expert_forward(): jnp.einsum('erd,fed->erf', rows_in, inner_part, preferred_element_type=jn...  25.9 us
  transfers between devices with their start and end apart: 23, of which 16 were waited for; matrix products, arithmetic and copies ran while one was open for 29% of the time, Pallas kernels for 0%

profile of v1, /device:TPU:0, one launch (start us, length us, event | category | flops | bytes accessed | tf_op | source)
XLA Modules:
  0.0 809.3 jit_solution(2842359674718050048)
XLA Ops:
  12.4 4.6 reduce-window.6
  19.7 3.0 convolution_convert_fusion.2
  22.7 2.8 copy.66
  28.6 2.8 fusion.7
  33.3 3.1 fusion.64
  38.9 2.8 fusion.6
  43.6 3.6 fusion.63
  52.1 15.5 %scatter_custom_fusion = s32[5121]{0:T(1024)S(1)} fusion(s32[4096]{0:T(1024)S(1)} %bitcast.223, s32[4096]{0:T(1024)S(1)} %iota.15, s32[]{:T(128)} %constant.67.clone.1), kind=kCustom, calls=%fused_computation.231 | custom fusion | bytes 20488 | tf_op jit(solution)/shard_map/scatter | solution.py:53
  67.7 21.2 %gather_fusion = bf16[5120,384]{1,0:T(8,128)(2,1)} fusion(bf16[1025,384]{1,0:T(8,128)(2,1)S(1)} %concatenate.50, s32[5120]{0:T(1024)S(1)} %get-tuple-element.68), kind=kCustom, calls=%fused_computation | custom fusion | bytes 7884800 | tf_op jit(solution)/shard_map/gather | solution.py:238
  88.9 4.5 copy.71
  93.4 5.3 all-to-all-start
  99.2 3.4 mul.354
  102.7 7.8 mul.355
  110.5 3.2 multiply_convert_fusion.3
  114.0 21.2 %gather_fusion.2 = bf16[5120,384]{1,0:T(8,128)(2,1)} fusion(bf16[4097,384]{1,0:T(8,128)(2,1)S(1)} %concatenate.52, s32[5120]{0:T(1024)S(1)} %get-tuple-element.67), kind=kCustom, calls=%fused_computation.2 | custom fusion | bytes 7884800 | tf_op jit(solution)/shard_map/gather | solution.py:268
  135.2 4.4 copy.80
  139.6 4.8 all-to-all-done
  144.5 4.8 all-to-all-start.2
  149.3 4.4 copy.72
  153.7 39.8 %all-to-all-done.2 = bf16[4,4,320,384]{3,2,0,1:T(8,128)(2,1)} async-done(((bf16[4,4,320,384]{3,2,0,1:T(8,128)(2,1)}), bf16[4,4,320,384]{3,2,0,1:T(8,128)(2,1)}, u32[]{:S(2)}, u32[]{:S(2)}) %all-to-all-start.2) | async-done | bytes 3932192 | tf_op jit(solution)/shard_map/all_to_all | solution.py:269
  193.6 3.8 fusion.111
  197.3 6.8 copy.73
  204.1 25.9 %fusion.11 = (u8[1280,1536]{1,0:T(8,128)(4,1)S(1)}, u8[1280,1536]{1,0:T(8,128)(4,1)}, f32[4,1280,1536]{2,1,0:T(8,128)}) fusion(bf16[4,1280,384]{2,1,0:T(8,128)(2,1)} %bitcast.198, bf16[1536,4,384]{0,2,1:T(8,128)(2,1)} %bitcast.194), kind=kOutput, calls=%fused_computation.43 | convolution fusion | flops 6138101760 | bytes 44040192 | tf_op jit(solution)/shard_map/erd,fed->erf/dot_general | solution.py:124
  230.0 74.8 %multiply_convert_fusion = (bf16[4,1280,1536]{2,1,0:T(8,128)(2,1)S(1)}, f32[4,1280,1536]{2,1,0:T(8,128)}) fusion(f32[4,1280,1536]{2,1,0:T(8,128)} %get-tuple-element.79, u8[1280,1536]{1,0:T(8,128)(4,1)} %get-tuple-element.19, u8[1280,1536]{1,0:T(8,128)(4,1)S(1)} %get-tuple-element.18), kind=kLoop, calls=%fused_computation.13 | loop fusion | flops 550502400 | bytes 82575360 | tf_op jit(solution)/shard_map/convert_element_type | solution.py:125
  314.8 6.6 copy.98
  321.5 55.4 %reduce-scatter.9.cloned.1.call-done = bf16[192,1536]{1,0:T(8,128)(2,1)} async-done(((bf16[1536,1536]{1,0:T(8,128)(2,1)}), bf16[192,1536]{1,0:T(8,128)(2,1)}) %reduce-scatter.9.cloned.1.call-update) | async-done | bytes 589840
  378.9 4.9 multiply_add_fusion.2
  384.8 4.5 copy.81
  389.2 45.3 %all-gather.5.cloned.1.call-done = bf16[1536,1536]{1,0:T(8,128)(2,1)} async-done(((bf16[192,1536]{1,0:T(8,128)(2,1)}), bf16[1536,1536]{1,0:T(8,128)(2,1)}) %all-gather.5.cloned.1.call-update) | async-done | bytes 4718608 | tf_op jit(solution)/shard_map/all_gather | solution.py:247
  434.6 6.6 copy.75
  441.2 13.1 %convolution_convert_fusion.1 = bf16[4,1280,384]{2,1,0:T(8,128)(2,1)S(1)} fusion(bf16[4,1280,1536]{2,1,0:T(8,128)(2,1)} %copy-done.17, bf16[1536,4,384]{0,2,1:T(8,128)(2,1)} %bitcast.196), kind=kOutput, calls=%fused_computation.55 | convolution fusion | flops 6041763840 | bytes 24379392 | tf_op jit(solution)/shard_map/erf,fed->erd/dot_general | solution.py:126
  456.6 5.3 all-to-all-start.1
  461.9 31.5 %add_convert_fusion = bf16[4,1280,1536]{2,1,0:T(8,128)(2,1)} fusion(f32[4,1280,1536]{2,1,0:T(8,128)} %get-tuple-element.44, bf16[4,1280,384]{2,1,0:T(8,128)(2,1)} %bitcast.199, bf16[1536,4,384]{0,2,1:T(8,128)(2,1)} %bitcast.197, f32[4,1280,1536]{2,1,0:T(8,128)} %get-tuple-element.79), kind=kOutput, calls=%fused_computation.12 | convolution fusion | flops 6149898240 | bytes 87293952 | tf_op jit(solution)/shard_map/erd,fed->erf/dot_general | solution.py:133
  493.5 13.1 %convolution_convert_fusion = bf16[4,1280,384]{2,1,0:T(8,128)(2,1)S(1)} fusion(bf16[4,1280,1536]{2,1,0:T(8,128)(2,1)} %add_convert_fusion, bf16[1536,4,384]{0,2,1:T(8,128)(2,1)} %bitcast.195), kind=kOutput, calls=%fused_computation.54 | convolution fusion | flops 6041763840 | bytes 24379392 | tf_op jit(solution)/shard_map/erf,fed->erd/dot_general | solution.py:135
  509.0 4.9 all-to-all-start.3
  514.7 3.8 fusion.112
  518.5 4.9 fusion.31
  528.1 31.1 %all-to-all-done.3 = bf16[4,4,320,384]{3,2,0,1:T(8,128)(2,1)} async-done(((bf16[4,4,320,384]{3,2,0,1:T(8,128)(2,1)}), bf16[4,4,320,384]{3,2,0,1:T(8,128)(2,1)}, u32[]{:S(2)}, u32[]{:S(2)}) %all-to-all-start.3) | async-done | bytes 3932192 | tf_op jit(solution)/shard_map/all_to_all | solution.py:286
  564.0 19.5 %gather_fusion.1 = bf16[4096,384]{1,0:T(8,128)(2,1)} fusion(bf16[5121,384]{1,0:T(8,128)(2,1)} %concatenate.51, s32[4096]{0:T(1024)S(1)} %broadcast_clamp_fusion), kind=kCustom, calls=%fused_computation.1 | custom fusion | bytes 6307840 | tf_op jit(solution)/shard_map/gather | solution.py:260
  583.5 16.7 %gather_fusion.3 = bf16[4096,384]{1,0:T(8,128)(2,1)S(1)} fusion(bf16[5121,384]{1,0:T(8,128)(2,1)} %concatenate.53, s32[4096]{0:T(1024)S(1)} %broadcast_clamp_fusion), kind=kCustom, calls=%fused_computation.3 | custom fusion | bytes 6307840 | tf_op jit(solution)/shard_map/gather | solution.py:296
  600.2 3.6 reshape.458
  603.8 7.8 reduce_sum.194
  614.0 6.7 reshape.457
  620.8 17.8 %multiply_reduce_fusion.2 = f32[1024,384]{1,0:T(8,128)S(1)} fusion(f32[1024,4,384]{2,1,0:T(4,128)} %reshape.457, f32[1024,4]{1,0:T(8,128)S(1)} %copy-done.31), kind=kLoop, calls=%fused_computation.49 | loop fusion | flops 2752512 | bytes 7880704 | tf_op jit(solution)/shard_map/reduce_sum | solution.py:261
  643.9 7.4 multiply_reduce_fusion.1
  651.2 9.9 %multiply_convert_fusion.2 = bf16[6,512,1024]{2,1,0:T(8,128)(2,1)} fusion(f32[6,512,1024]{2,1,0:T(8,128)} %get-tuple-element.81, f32[6,512,1024]{2,1,0:T(8,128)S(1)} %bitcast.175, f32[6,512]{1,0:T(8,128)S(1)} %get-tuple-element.80, f32[6,512]{1,0:T(8,128)S(1)} %log_add_fusion.1), kind=kLoop, calls=%fused_computation.29 | loop fusion | flops 12582912 | bytes 31481856 | tf_op jit(solution)/shard_map/convert_element_type | solution.py:110
  661.2 5.8 fusion.62
  666.9 5.2 fusion.80
  672.2 3.2 fusion.12
  675.4 8.0 multiply_reduce_fusion
  683.4 4.5 fusion.53
  687.9 6.9 multiply_convert_fusion.1
  712.1 7.2 collective-permute-done.6
  724.3 6.8 copy.96
  733.2 3.8 collective-permute-done.8
  738.5 4.0 fusion.107
  742.5 2.9 collective-permute-done.9
  746.7 5.0 collective-permute-done.10
  751.9 6.8 collective-permute-done.11
  760.8 3.7 collective-permute-done.12
  780.5 3.5 collective-permute-done.3
  785.5 2.6 add_add_fusion.2
  793.2 2.8 multiply_add_fusion
  798.2 4.4 multiply_add_fusion.4
  (361 shorter events, 111.4 us)
Async XLA Ops:
  7.2 10.5 %copy-start.74 = (s32[1024]{0:T(1024)S(1)}, s32[1024]{0:T(1024)}, u32[]{:S(2)}) copy-start(s32[1024]{0:T(1024)} %param.25) | copy-start | bytes 12292
  7.2 190.1 %all-gather.3.cloned.1.call-start = ((), (), s32[]{:S(2)}) async-start(), calls=%async_computation.6 | async-start | bytes 5308416 | tf_op jit(solution)/shard_map/all_gather | solution.py:246
  8.8 10.9 %copy-start.37 = (f32[384,1152]{1,0:T(8,128)S(1)}, f32[384,1152]{1,0:T(8,128)}, u32[]{:S(2)}) copy-start(f32[384,1152]{1,0:T(8,128)} %param.28) | copy-start | bytes 5308420
  11.0 40.1 %copy-start.52 = (s32[4096]{0:T(1024)}, s32[4096]{0:T(1024)S(1)}, u32[]{:S(2)}) copy-start(s32[4096]{0:T(1024)S(1)} %eq.102) | copy-start | bytes 49156
  11.8 7.9 copy-start.65
  12.3 7.4 copy-start.83
  12.3 7.4 copy-start.81
  12.4 7.3 copy-start.87
  12.4 7.3 copy-start.93
  25.5 16.2 %copy-start.6 = (bf16[1024,1152]{0,1:T(8,128)(2,1)}, bf16[1024,1152]{0,1:T(8,128)(2,1)S(1)}, u32[]{:S(2)}) copy-start(bf16[1024,1152]{0,1:T(8,128)(2,1)S(1)} %copy.66) | copy-start | bytes 7077892
  51.3 37.6 %copy-start.54 = (s32[4096]{0:T(1024)}, s32[4096]{0:T(1024)S(1)}, u32[]{:S(2)}) copy-start(s32[4096]{0:T(1024)S(1)} %fusion.82) | copy-start | bytes 49156
  93.4 51.1 %all-to-all-start = ((bf16[4,4,320,384]{3,2,0,1:T(8,128)(2,1)}), bf16[4,4,320,384]{3,2,0,1:T(8,128)(2,1)}, u32[]{:S(2)}, u32[]{:S(2)}) async-start(bf16[4,4,320,384]{3,2,0,1:T(8,128)(2,1)} %copy.71), calls=%async_computation | async-start | bytes 7864320 | tf_op jit(solution)/shard_map/all_to_all | solution.py:239
  98.9 11.5 %copy-start.30 = (f32[1024,4]{1,0:T(8,128)}, f32[1024,4]{1,0:T(8,128)S(1)}, u32[]{:S(2)}) copy-start(f32[1024,4]{1,0:T(8,128)S(1)} %copy.67) | copy-start | bytes 49156
  144.5 49.1 %all-to-all-start.2 = ((bf16[4,4,320,384]{3,2,0,1:T(8,128)(2,1)}), bf16[4,4,320,384]{3,2,0,1:T(8,128)(2,1)}, u32[]{:S(2)}, u32[]{:S(2)}) async-start(bf16[4,4,320,384]{3,2,0,1:T(8,128)(2,1)} %copy.80), calls=%async_computation.2 | async-start | bytes 7864320 | tf_op jit(solution)/shard_map/all_to_all | solution.py:269
  149.3 227.6 %reduce-scatter.9.cloned.1.call-start = ((), (), s32[]{:S(2)}) async-start(), calls=%async_computation.9 | async-start | bytes 5308416
  230.0 74.8 %copy-start.49 = (bf16[1,4,320,384]{3,2,0,1:T(8,128)(2,1)S(1)}, bf16[1,4,320,384]{3,2,0,1:T(8,128)(2,1)}, u32[]{:S(2)}) copy-start(bf16[1,4,320,384]{3,2,0,1:T(8,128)(2,1)} %get-tuple-element.46) | copy-start | bytes 2949124
  321.4 57.5 %copy-start.42 = (f32[192,4,384]{2,1,0:T(4,128)S(1)}, f32[192,4,384]{2,1,0:T(4,128)}, u32[]{:S(2)}) copy-start(f32[192,4,384]{2,1,0:T(4,128)} %param.41) | copy-start | bytes 3538948
  321.4 113.1 %all-gather.5.cloned.1.call-start = ((), (), s32[]{:S(2)}) async-start(), calls=%async_computation.7 | async-start | bytes 5308416 | tf_op jit(solution)/shard_map/all_gather | solution.py:247
  456.6 52.3 %all-to-all-start.1 = ((bf16[4,4,320,384]{3,2,0,1:T(8,128)(2,1)}), bf16[4,4,320,384]{3,2,0,1:T(8,128)(2,1)}, u32[]{:S(2)}, u32[]{:S(2)}) async-start(bf16[4,4,320,384]{3,2,0,1:T(8,128)(2,1)} %copy.77), calls=%async_computation.1 | async-start | bytes 7864320 | tf_op jit(solution)/shard_map/all_to_all | solution.py:250
  509.0 50.2 %all-to-all-start.3 = ((bf16[4,4,320,384]{3,2,0,1:T(8,128)(2,1)}), bf16[4,4,320,384]{3,2,0,1:T(8,128)(2,1)}, u32[]{:S(2)}, u32[]{:S(2)}) async-start(bf16[4,4,320,384]{3,2,0,1:T(8,128)(2,1)} %copy.84), calls=%async_computation.3 | async-start | bytes 7864320 | tf_op jit(solution)/shard_map/all_to_all | solution.py:286
  513.9 282.2 %reduce-scatter.7.cloned.1.call-start = ((), (), s32[]{:S(2)}) async-start(), calls=%async_computation.8 | async-start | bytes 5308416
  603.8 7.8 copy-start.3
  603.8 7.8 copy-start.57
  614.0 6.8 copy-start.31
  620.8 17.8 %copy-start.4 = (f32[1024,384]{1,0:T(8,128)S(1)}, f32[1024,384]{1,0:T(8,128)}, u32[]{:S(2)}) copy-start(f32[1024,384]{1,0:T(8,128)} %reduce_sum.194) | copy-start | bytes 4718596
  620.8 17.8 %copy-start.12 = (f32[1024,384]{1,0:T(8,128)S(1)}, f32[1024,384]{1,0:T(8,128)}, u32[]{:S(2)}) copy-start(f32[1024,384]{1,0:T(8,128)} %fusion.71) | copy-start | bytes 4718596
  620.8 17.8 %copy-start.77 = (f32[1024]{0:T(1024)S(1)}, f32[1024]{0:T(1024)}, u32[]{:S(2)}) copy-start(f32[1024]{0:T(1024)} %copy-done.76) | copy-start | bytes 12292
  620.8 23.0 %slice-start = ((s8[12582912]{0:T(1024)(128)(4,1)}), s8[4194304]{0:T(1024)(128)(4,1)S(1)}, s32[]{:S(2)}) async-start(s8[12582912]{0:T(1024)(128)(4,1)} %bitcast.174), calls=%async_computation.10 | async-start | bytes 8388608
  643.8 7.4 copy-start.33
  651.2 9.9 %copy-start.7 = (bf16[1024,1152]{0,1:T(8,128)(2,1)S(1)}, bf16[1024,1152]{0,1:T(8,128)(2,1)}, u32[]{:S(2)}) copy-start(bf16[1024,1152]{0,1:T(8,128)(2,1)} %copy-done.6) | copy-start | bytes 7077892
  651.2 20.9 %slice-start.3 = ((s8[12582912]{0:T(1024)(128)(4,1)}), s8[4194304]{0:T(1024)(128)(4,1)S(1)}, s32[]{:S(2)}) async-start(s8[12582912]{0:T(1024)(128)(4,1)} %bitcast.176), calls=%async_computation.13 | async-start | bytes 8388608
  651.2 20.9 %slice-start.4 = ((s8[12582912]{0:T(1024)(128)(4,1)}), s8[4194304]{0:T(1024)(128)(4,1)S(1)}, s32[]{:S(2)}) async-start(s8[12582912]{0:T(1024)(128)(4,1)} %bitcast.176), calls=%async_computation.14 | async-start | bytes 8388608
  661.2 11.0 %slice-start.5 = ((s8[12582912]{0:T(1024)(128)(4,1)}), s8[4194304]{0:T(1024)(128)(4,1)S(1)}, s32[]{:S(2)}) async-start(s8[12582912]{0:T(1024)(128)(4,1)} %bitcast.176), calls=%async_computation.15 | async-start | bytes 8388608
  687.9 7.0 copy-start.8
  697.0 6.1 slice-start.6
  697.0 6.1 slice-start.7
  703.0 5.5 collective-permute-start.5
  708.8 10.4 %collective-permute-start.6 = (bf16[128,1536]{1,0:T(8,128)(2,1)S(1)}, bf16[128,1536]{1,0:T(8,128)(2,1)S(1)}, u32[]{:S(2)}, u32[]{:S(2)}) collective-permute-start(bf16[128,1536]{1,0:T(8,128)(2,1)S(1)} %select_convert_fusion.1), channel_id=1, source_target_pairs={{0,8},{8,0},{16,24},{24,16},{1,9},{9,1},{17,25},{25,17},{2,10},{10... | collective-permute-start | bytes 1179656 | tf_op jit(solution)/shard_map/ppermute | solution.py:161
  712.1 9.8 %copy-start.43 = (bf16[1536,384]{0,1:T(8,128)(2,1)S(1)}, bf16[1536,384]{0,1:T(8,128)(2,1)}, u32[]{:S(2)}) copy-start(bf16[1536,384]{0,1:T(8,128)(2,1)} %fusion.31) | copy-start | bytes 3538948
  720.3 10.8 %collective-permute-start.7 = (bf16[64,1536]{1,0:T(8,128)(2,1)S(1)}, bf16[64,1536]{1,0:T(8,128)(2,1)S(1)}, u32[]{:S(2)}, u32[]{:S(2)}) collective-permute-start(bf16[64,1536]{1,0:T(8,128)(2,1)S(1)} %select_convert_fusion.2), channel_id=1, source_target_pairs={{0,16},{8,24},{16,0},{24,8},{1,17},{9,25},{17,1},{25,9},{2,18},{10... | collective-permute-start | bytes 589832 | tf_op jit(solution)/shard_map/ppermute | solution.py:161
  732.3 4.7 collective-permute-start.8
  737.1 8.5 %copy-start.5 = (f32[1024,384]{1,0:T(8,128)S(1)}, f32[1024,384]{1,0:T(8,128)}, u32[]{:S(2)}) copy-start(f32[1024,384]{1,0:T(8,128)} %reduce_sum.194) | copy-start | bytes 4718596
  737.1 8.5 %copy-start.58 = (f32[1024]{0:T(1024)S(1)}, f32[1024]{0:T(1024)}, u32[]{:S(2)}) copy-start(f32[1024]{0:T(1024)} %copy-done.56) | copy-start | bytes 12292
  737.1 8.5 %copy-start.75 = (s32[1024]{0:T(1024)S(1)}, s32[1024]{0:T(1024)}, u32[]{:S(2)}) copy-start(s32[1024]{0:T(1024)} %param.25) | copy-start | bytes 12292
  737.1 8.5 %copy-start.78 = (f32[1024]{0:T(1024)S(1)}, f32[1024]{0:T(1024)}, u32[]{:S(2)}) copy-start(f32[1024]{0:T(1024)} %copy-done.76) | copy-start | bytes 12292
  737.1 14.7 %copy-start.84 = (f32[1024]{0:T(1024)S(1)}, f32[1024]{0:T(1024)}, u32[]{:S(2)}) copy-start(f32[1024]{0:T(1024)} %copy-done.83) | copy-start | bytes 12292
  737.1 8.3 %collective-permute-start.9 = (bf16[16,1536]{1,0:T(8,128)(2,1)S(1)}, bf16[16,1536]{1,0:T(8,128)(2,1)S(1)}, u32[]{:S(2)}, u32[]{:S(2)}) collective-permute-start(bf16[16,1536]{1,0:T(8,128)(2,1)S(1)} %select_convert_fusion.4), channel_id=1, source_target_pairs={{0,4},{1,5},{2,6},{3,7},{4,0},{5,1},{6,2},{7,3},{8,12},{9,13},{10,... | collective-permute-start | bytes 147464 | tf_op jit(solution)/shard_map/ppermute | solution.py:161
  742.5 22.8 %copy-start.24 = (f32[1024,384]{1,0:T(8,128)}, f32[1024,384]{1,0:T(8,128)S(1)}, u32[]{:S(2)}) copy-start(f32[1024,384]{1,0:T(8,128)S(1)} %get-tuple-element.84) | copy-start | bytes 4718596
  742.5 16.8 %copy-start.15 = (bf16[1024,384]{1,0:T(8,128)(2,1)S(1)}, bf16[1024,384]{1,0:T(8,128)(2,1)}, u32[]{:S(2)}) copy-start(bf16[1024,384]{1,0:T(8,128)(2,1)} %param.21) | copy-start | bytes 2359300
  745.5 6.2 collective-permute-start.10
  751.8 6.9 collective-permute-start.11
  758.8 5.7 collective-permute-start.12
  759.4 26.1 %copy-start.10 = (f32[1024,384]{1,0:T(8,128)S(1)}, f32[1024,384]{1,0:T(8,128)}, u32[]{:S(2)}) copy-start(f32[1024,384]{1,0:T(8,128)} %copy-done.9) | copy-start | bytes 4718596
  759.4 26.1 %copy-start.16 = (bf16[1024,384]{1,0:T(8,128)(2,1)S(1)}, bf16[1024,384]{1,0:T(8,128)(2,1)}, u32[]{:S(2)}) copy-start(bf16[1024,384]{1,0:T(8,128)(2,1)} %param.21) | copy-start | bytes 2359300
  759.4 26.1 %copy-start.21 = (bf16[1024,384]{1,0:T(8,128)(2,1)S(1)}, bf16[1024,384]{1,0:T(8,128)(2,1)}, u32[]{:S(2)}) copy-start(bf16[1024,384]{1,0:T(8,128)(2,1)} %param.22) | copy-start | bytes 2359300
  759.4 26.1 %copy-start.80 = (f32[1024]{0:T(1024)S(1)}, f32[1024]{0:T(1024)}, u32[]{:S(2)}) copy-start(f32[1024]{0:T(1024)} %copy-done.79) | copy-start | bytes 12292
  765.3 18.8 %collective-permute-start.13 = (bf16[128,1536]{1,0:T(8,128)(2,1)}, bf16[128,1536]{1,0:T(8,128)(2,1)}, u32[]{:S(2)}, u32[]{:S(2)}) collective-permute-start(bf16[128,1536]{1,0:T(8,128)(2,1)} %pad_maximum_fusion.6), channel_id=1, source_target_pairs={{0,8},{8,0},{16,24},{24,16},{1,9},{9,1},{17,25},{25,17},{2,10},{10... | collective-permute-start | bytes 1179656 | tf_op jit(solution)/shard_map/ppermute | solution.py:169
  770.3 15.2 %copy-start.25 = (f32[1024,384]{1,0:T(8,128)S(1)}, f32[1024,384]{1,0:T(8,128)}, u32[]{:S(2)}) copy-start(f32[1024,384]{1,0:T(8,128)} %copy-done.24) | copy-start | bytes 4718596
  770.3 1.4 collective-permute-start
  772.4 3.7 collective-permute-start.1
  776.1 3.7 collective-permute-start.2
  779.8 4.2 collective-permute-start.3
  784.0 4.6 collective-permute-start.4
  785.4 4.4 collective-permute-start.14
  (64 other events, 212.8 us)
Sparse Core Ops, SparseCore 0:
  10.3 54.0 all-gather.2
  321.6 55.2 reduce-scatter.8
  384.9 49.6 all-gather.4
  731.2 56.9 reduce-scatter.6

commit v2 on v1

--- a/solution.py
+++ b/solution.py
@@ -1,8 +1,11 @@
+import functools
 import math
 
 import jax
 import jax.numpy as jnp
 from jax import lax
+from jax.experimental import pallas as pl
+from jax.experimental.pallas import tpu as pltpu
 from jax.sharding import PartitionSpec as P
 
 D = 384
@@ -23,6 +26,7 @@
 RATE_OUTER = 0.73
 NORM_EPS = 1e-06
 MASKED = -1e30
+VMEM_MOST = 67043328
 
 
 def layer_norm(values):
@@ -33,26 +37,6 @@
 
 def first_norm(values, gain_row, offset_row):
     return layer_norm(values) * gain_row + offset_row
-
-
-def exact_gelu(values):
-    return jax.nn.gelu(values, approximate=False)
-
-
-def routing(expert_ids, groups):
-    flat_ids = expert_ids.reshape(-1)
-    pair_count = flat_ids.shape[0]
-    local_count = EXPERTS // groups
-    onehot = (flat_ids[:, None] == jnp.arange(EXPERTS, dtype=jnp.int32)[None, :]).astype(jnp.int32)
-    slot_place = jnp.sum(onehot * jnp.cumsum(onehot, axis=0), axis=1) - 1
-    is_kept = slot_place < CAP
-    slot_total = EXPERTS * CAP
-    target = (flat_ids % local_count * groups + flat_ids // local_count) * CAP + slot_place
-    target = jnp.where(is_kept, target, slot_total)
-    source = jnp.full((slot_total + 1,), pair_count, jnp.int32)
-    source = source.at[target].set(jnp.arange(pair_count, dtype=jnp.int32))[:slot_total]
-    counts = jnp.sum(onehot * is_kept[:, None].astype(jnp.int32), axis=0)
-    return (target, source, counts)
 
 
 def attend_forward(query_heads, key_heads, value_heads, seg_marks, block_rows):
@@ -120,22 +104,201 @@
     return (jnp.concatenate(query_grads, axis=0), key_grad, value_grad)
 
 
-def expert_forward(rows_in, inner_part, outer_part):
-    pre_act = jnp.einsum("erd,fed->erf", rows_in, inner_part, preferred_element_type=jnp.float32)
-    act_low = exact_gelu(pre_act).astype(jnp.bfloat16)
-    return jnp.einsum("erf,fed->erd", act_low, outer_part, preferred_element_type=jnp.float32)
-
-
-def expert_backward_parts(rows_in, rows_grad, inner_part, outer_part):
-    pre_act = jnp.einsum("erd,fed->erf", rows_in, inner_part, preferred_element_type=jnp.float32)
-    act_val, gelu_back = jax.vjp(exact_gelu, pre_act)
-    act_low = act_val.astype(jnp.bfloat16)
-    act_grad = jnp.einsum("erd,fed->erf", rows_grad, outer_part, preferred_element_type=jnp.float32)
-    pre_grad = gelu_back(act_grad)[0].astype(jnp.bfloat16)
-    input_grad = jnp.einsum(
-        "erf,fed->erd", pre_grad, inner_part, preferred_element_type=jnp.float32
-    )
-    return (input_grad, pre_grad, act_low)
+def route_kernel(first_expert, ids_ref, gates_ref, rows_ref, gate_rows_ref, cols_ref):
+    slots, _, tokens = ids_ref.shape
+    count = rows_ref.shape[1]
+    before = (
+        lax.broadcasted_iota(jnp.int32, (tokens, tokens), 0)
+        <= lax.broadcasted_iota(jnp.int32, (tokens, tokens), 1)
+    )
+    before = jnp.where(before, 1.0, 0.0).astype(jnp.bfloat16)
+    hot_rows = []
+    for slot in range(slots):
+        for expert in range(count):
+            hot = jnp.zeros((1, tokens), jnp.float32)
+            gate = jnp.zeros((1, tokens), jnp.float32)
+            name = (first_expert[0] + expert).astype(jnp.float32)
+            for choice in range(TOP):
+                same = ids_ref[slot, choice : choice + 1, :] == name
+                hot = jnp.where(same, 1.0, hot)
+                gate = jnp.where(same, gates_ref[slot, choice : choice + 1, :], gate)
+            hot_rows.append(hot)
+            gate_rows_ref[slot, expert : expert + 1, :] = gate
+    hot_all = jnp.concatenate(hot_rows, axis=0)
+    place = jnp.dot(hot_all.astype(jnp.bfloat16), before, preferred_element_type=jnp.float32) - 1.0
+    place = jnp.where((hot_all > 0.5) & (place < CAP), place, -1.0)
+    for slot in range(slots):
+        rows_ref[slot] = place[slot * count : (slot + 1) * count].astype(jnp.int32)
+    wide = jnp.concatenate([place, jnp.full((128 - place.shape[0], tokens), -1.0, jnp.float32)], axis=0)
+    cols_ref[...] = jnp.transpose(wide).astype(jnp.int32)
+
+
+def route(first_expert, ids_all, gates_all, count):
+    slots, _, tokens = ids_all.shape
+    vmem = pl.BlockSpec(memory_space=pltpu.VMEM)
+    return pl.pallas_call(
+        route_kernel,
+        out_shape=(
+            jax.ShapeDtypeStruct((slots, count, tokens), jnp.int32),
+            jax.ShapeDtypeStruct((slots, count, tokens), jnp.float32),
+            jax.ShapeDtypeStruct((tokens, 128), jnp.int32),
+        ),
+        in_specs=[pl.BlockSpec(memory_space=pltpu.SMEM), vmem, vmem],
+        out_specs=(vmem, vmem, vmem),
+        name="route",
+    )(first_expert, ids_all, gates_all)
+
+
+NT = (((1,), (1,)), ((), ()))
+NN = (((1,), (0,)), ((), ()))
+TN = (((0,), (0,)), ((), ()))
+
+
+def mxu(left, right, dims=NN):
+    return lax.dot_general(left, right, dims, preferred_element_type=jnp.float32)
+
+
+def moe_kernel(
+    offset, count, has_start, last, chunk, rows_ref, gate_rows_ref, cols_ref, *rest
+):
+    slots, _, tokens = rows_ref.shape
+    rest = list(rest)
+    u_refs, g_refs, rest = rest[:slots], rest[slots : 2 * slots], rest[2 * slots :]
+    inner_ref, outer_ref, rest = rest[0], rest[1], rest[2:]
+    if has_start:
+        start_ref, rest = rest[0], rest[1:]
+    out_count = 2 * slots if last else 1
+    sums_refs, grads_ref, rest = rest[:out_count], rest[out_count], rest[out_count + 1 :]
+    x_buf, dy_buf, act_buf, dpre_buf, gate_buf, sum_buf = rest[:6]
+    step = pl.program_id(0)
+    width = u_refs[0].shape[1]
+    units = inner_ref.shape[0]
+    for slot in range(slots):
+        place = rows_ref[slot, pl.ds(offset + step, 1), :]
+        same = lax.broadcasted_iota(jnp.int32, (CAP, tokens), 0) == place
+        pick = jnp.where(same, 1.0, 0.0).astype(jnp.bfloat16)
+        gate = jnp.sum(
+            jnp.where(same, gate_rows_ref[slot, pl.ds(offset + step, 1), :], 0.0), axis=1, keepdims=True
+        )
+        span = pl.ds(slot * CAP, CAP)
+        x_buf[span, :] = mxu(pick, u_refs[slot][...]).astype(jnp.bfloat16)
+        dy_buf[span, :] = (gate * mxu(pick, g_refs[slot][...])).astype(jnp.bfloat16)
+        gate_buf[span, :] = jnp.broadcast_to(gate, (CAP, 128))
+
+    def part(index, carry):
+        at = pl.multiple_of(index * chunk, chunk)
+        span = pl.ds(at, chunk)
+        rows_in = x_buf[...]
+        rows_grad = dy_buf[...]
+        pre = mxu(rows_in, inner_ref[span, :], NT)
+        act_grad = mxu(rows_grad, outer_ref[span, :], NT)
+        phi = 0.5 + 0.5 * lax.erf(pre * math.sqrt(0.5))
+        bell = jnp.exp(pre * pre * -0.5) * (1.0 / math.sqrt(2.0 * math.pi))
+        act = (pre * phi).astype(jnp.bfloat16)
+        dpre = (act_grad * (phi + pre * bell)).astype(jnp.bfloat16)
+        act_buf[:, span] = act
+        dpre_buf[:, span] = dpre
+        grads_ref[span, :width] = mxu(dpre, rows_in, TN).astype(jnp.bfloat16)
+        grads_ref[span, width:] = mxu(act, rows_grad, TN).astype(jnp.bfloat16)
+        return carry
+
+    lax.fori_loop(0, units // chunk, part, 0)
+    result = mxu(act_buf[...], outer_ref[...])
+    gate_wide = jnp.concatenate([gate_buf[...]] * (width // 128), axis=1)
+    x_buf[...] = (gate_wide * result).astype(jnp.bfloat16)
+    dy_buf[...] = mxu(dpre_buf[...], inner_ref[...]).astype(jnp.bfloat16)
+
+    if has_start:
+        @pl.when(step == 0)
+        def _():
+            copy = pltpu.make_async_copy(start_ref, sum_buf, rest[6])
+            copy.start()
+            copy.wait()
+
+    for slot in range(slots):
+        lane = slot * count + offset + step
+        wide = lax.broadcasted_iota(jnp.int32, (tokens, 128), 1) == lane
+        column = jnp.sum(jnp.where(wide, cols_ref[...], 0), axis=1, keepdims=True)
+        same = lax.broadcasted_iota(jnp.int32, (tokens, CAP), 1) == column
+        spread = jnp.where(same, 1.0, 0.0).astype(jnp.bfloat16)
+        span = pl.ds(slot * CAP, CAP)
+        for side, buf in enumerate((x_buf, dy_buf)):
+            add = mxu(spread, buf[span, :])
+            lanes = slice(side * width, (side + 1) * width)
+            if has_start:
+                sum_buf[slot, :, lanes] = sum_buf[slot, :, lanes] + add
+            else:
+                first = jnp.where(step == 0, 0.0, 1.0)
+                old = sum_buf[slot, :, lanes]
+                sum_buf[slot, :, lanes] = jnp.where(first > 0.5, old, 0.0) + add
+
+    @pl.when(step == pl.num_programs(0) - 1)
+    def _():
+        if last:
+            for slot in range(slots):
+                sums_refs[slot][...] = sum_buf[slot, :, width:].astype(jnp.bfloat16)
+                sums_refs[slots + slot][...] = sum_buf[slot, :, :width].astype(jnp.bfloat16)
+        else:
+            sums_refs[0][...] = sum_buf[...]
+
+
+def moe(rows, gate_rows, cols, u_all, g_all, weights, offset, start, last):
+    slots, count, tokens = rows.shape
+    width = u_all[0].shape[1]
+    units = weights.shape[0]
+    steps = weights.shape[1] // (2 * width)
+    pairs = slots * CAP
+    once = pl.Buffered(1)
+
+    def whole(array):
+        return pl.BlockSpec(array.shape, lambda e: (0,) * array.ndim, pipeline_mode=once)
+
+    sums_shape = (slots, tokens, 2 * width)
+    scratch = [
+        pltpu.VMEM((pairs, width), jnp.bfloat16),
+        pltpu.VMEM((pairs, width), jnp.bfloat16),
+        pltpu.VMEM((pairs, units), jnp.bfloat16),
+        pltpu.VMEM((pairs, units), jnp.bfloat16),
+        pltpu.VMEM((pairs, 128), jnp.float32),
+        pltpu.VMEM(sums_shape, jnp.float32),
+    ]
+    operands = [rows, gate_rows, cols, *u_all, *g_all, weights, weights]
+    in_specs = [whole(a) for a in operands[:-2]] + [
+        pl.BlockSpec((units, width), lambda e: (0, 2 * e)),
+        pl.BlockSpec((units, width), lambda e: (0, 2 * e + 1)),
+    ]
+    if start is not None:
+        operands.append(start)
+        in_specs.append(pl.BlockSpec(memory_space=pl.ANY))
+        scratch.append(pltpu.SemaphoreType.DMA)
+    if last:
+        sums_out = (jax.ShapeDtypeStruct((tokens, width), jnp.bfloat16),) * (2 * slots)
+    else:
+        sums_out = (jax.ShapeDtypeStruct(sums_shape, jnp.float32),)
+    flops = steps * pairs * width * (12 * units + 8 * tokens)
+    return pl.pallas_call(
+        functools.partial(moe_kernel, offset, count, start is not None, last, units // 3),
+        out_shape=sums_out + (jax.ShapeDtypeStruct((units, steps * 2 * width), jnp.bfloat16),),
+        grid_spec=pltpu.PrefetchScalarGridSpec(
+            num_scalar_prefetch=0,
+            grid=(steps,),
+            in_specs=in_specs,
+            out_specs=tuple(whole(s) for s in sums_out)
+            + (pl.BlockSpec((units, 2 * width), lambda e: (0, e)),),
+            scratch_shapes=scratch,
+        ),
+        compiler_params=pltpu.CompilerParams(
+            dimension_semantics=("arbitrary",), vmem_limit_bytes=VMEM_MOST
+        ),
+        cost_estimate=pl.CostEstimate(flops=flops, bytes_accessed=40 << 20, transcendentals=0),
+        name="moe",
+    )(*operands)
+
+
+def to_peers(arrays, groups):
+    return [arrays[0]] + [
+        lax.ppermute(arrays[k], "expert", [(i, i ^ k) for i in range(groups)]) for k in range(1, groups)
+    ]
 
 
 def butterfly_sum(value, wire):
@@ -208,6 +371,23 @@
     tokens_all = tok_count * groups * lax.axis_size("hidden")
     local_count = EXPERTS // groups
     block_rows = min(512, tok_count)
+    own_units = expert_inner.shape[0]
+    half = local_count // 2 * 2 * D
+    both = jnp.stack([expert_inner, expert_outer], axis=2).astype(jnp.bfloat16)
+    both = both.reshape(own_units, local_count * 2 * D)
+    weights = [
+        lax.all_gather(both[:, :half], "hidden", axis=0, tiled=True),
+        lax.all_gather(both[:, half:], "hidden", axis=0, tiled=True),
+    ]
+    table = jnp.concatenate([expert_ids.astype(jnp.float32).T, gates.T], axis=0)
+    tables = jnp.stack(to_peers([table] * groups, groups))
+    g_all = to_peers([cotangent] * groups, groups)
+    first_expert = (lax.axis_index("expert") * local_count).astype(jnp.int32).reshape(1)
+    rows, gate_rows, cols = route(first_expert, tables[:, :TOP], tables[:, TOP:], local_count)
+    named = jnp.sum(
+        (expert_ids[:, :, None] == jnp.arange(EXPERTS, dtype=jnp.int32)).astype(jnp.float32), axis=(0, 1)
+    )
+    counts = jnp.minimum(named, float(CAP))
     inputs = patches.astype(jnp.float32)
     seg_marks = segments[0]
     normed_one, first_back = jax.vjp(first_norm, inputs, norm_params[0], norm_params[1])
@@ -233,67 +413,24 @@
 
     normed_two, second_back = jax.vjp(second_norm, hidden_one, norm_params[2:])
     moe_in = normed_two.astype(jnp.bfloat16)
-    target, source, counts = routing(expert_ids, groups)
-    moe_pad = jnp.concatenate([moe_in, jnp.zeros((1, D), jnp.bfloat16)], axis=0)
-    slots_out = moe_pad[source // TOP].reshape(local_count, groups, CAP, D)
-    rows_in = lax.all_to_all(slots_out, "expert", split_axis=1, concat_axis=1, tiled=True).reshape(
-        local_count, groups * CAP, D
-    )
-    own_units = expert_inner.shape[0]
-    inner_low = expert_inner.astype(jnp.bfloat16).reshape(own_units, local_count * D)
-    outer_low = expert_outer.astype(jnp.bfloat16).reshape(own_units, local_count * D)
-    inner_all, outer_all = (
-        lax.all_gather(inner_low, "hidden", axis=0, tiled=True).reshape(-1, local_count, D),
-        lax.all_gather(outer_low, "hidden", axis=0, tiled=True).reshape(-1, local_count, D),
-    )
-    expert_sum = expert_forward(rows_in, inner_all, outer_all)
-    returned = lax.all_to_all(
-        expert_sum.astype(jnp.bfloat16).reshape(local_count, groups, CAP, D),
-        "expert",
-        split_axis=1,
-        concat_axis=1,
-        tiled=True,
-    )
-    back_pad = jnp.concatenate(
-        [returned.reshape(EXPERTS * CAP, D), jnp.zeros((1, D), jnp.bfloat16)], axis=0
-    )
-    routed = back_pad[target].reshape(tok_count, TOP, D)
-    moe_sum = jnp.sum(gates[:, :, None] * routed.astype(jnp.float32), axis=1)
+    u_all = to_peers([moe_in] * groups, groups)
+    sums, grads_first = moe(rows, gate_rows, cols, u_all, g_all, weights[0], 0, None, False)
+    *parts, grads_second = moe(
+        rows, gate_rows, cols, u_all, g_all, weights[1], local_count // 2, sums, True
+    )
+    du_parts = to_peers(parts[:groups], groups)
+    y_parts = to_peers(parts[groups:], groups)
+    moe_grad = sum(p.astype(jnp.float32) for p in du_parts)
+    moe_sum = sum(p.astype(jnp.float32) for p in y_parts)
     block_out = (hidden_one + moe_sum).astype(jnp.bfloat16)
     out_grad = cotangent.astype(jnp.float32)
-    pair_grad = (
-        (gates[:, :, None] * out_grad[:, None, :]).astype(jnp.bfloat16).reshape(tok_count * TOP, D)
-    )
-    pair_pad = jnp.concatenate([pair_grad, jnp.zeros((1, D), jnp.bfloat16)], axis=0)
-    slots_grad = pair_pad[source].reshape(local_count, groups, CAP, D)
-    rows_grad = lax.all_to_all(
-        slots_grad, "expert", split_axis=1, concat_axis=1, tiled=True
-    ).reshape(local_count, groups * CAP, D)
-    input_grad, pre_grad_all, act_all = expert_backward_parts(
-        rows_in, rows_grad, inner_all, outer_all
-    )
-    def weight_sums(left, right):
-        parts = [
-            jnp.einsum("rf,rd->fd", left[e], right[e], preferred_element_type=jnp.float32).astype(jnp.bfloat16)
-            for e in range(local_count)
-        ]
-        full = jnp.concatenate(parts, axis=1)
-        mine = lax.psum_scatter(full, "hidden", scatter_dimension=0, tiled=True)
-        return mine.astype(jnp.float32).reshape(own_units, local_count, D)
-
-    inner_grad = weight_sums(pre_grad_all, rows_in)
-    outer_grad = weight_sums(act_all, rows_grad)
-    back_rows = lax.all_to_all(
-        input_grad.astype(jnp.bfloat16).reshape(local_count, groups, CAP, D),
-        "expert",
-        split_axis=1,
-        concat_axis=1,
-        tiled=True,
-    )
-    grad_pad = jnp.concatenate(
-        [back_rows.reshape(EXPERTS * CAP, D), jnp.zeros((1, D), jnp.bfloat16)], axis=0
-    )
-    moe_grad = jnp.sum(grad_pad[target].reshape(tok_count, TOP, D).astype(jnp.float32), axis=1)
+    owned = [
+        lax.psum_scatter(g, "hidden", scatter_dimension=0, tiled=True)
+        for g in (grads_first, grads_second)
+    ]
+    owned = jnp.concatenate(owned, axis=1).astype(jnp.float32)
+    owned = owned.reshape(own_units, local_count, 2, D)
+    inner_grad, outer_grad = owned[:, :, 0], owned[:, :, 1]
     hidden_grad, table_grad = second_back(moe_grad)
     hidden_grad = hidden_grad + out_grad
     attn_grad_low = hidden_grad.astype(jnp.bfloat16)
@@ -320,7 +457,7 @@
     big = jnp.concatenate([big, jnp.zeros((pad_rows, big.shape[1]), jnp.float32)], axis=0)
     big_sum = butterfly_sum(big, jnp.bfloat16)[:D]
     qkv_sum, proj_sum = big_sum[:, : 3 * D], big_sum[:, 3 * D :]
-    count_row = jnp.pad(counts.astype(jnp.float32), (0, D - EXPERTS))[None]
+    count_row = jnp.pad(counts, (0, D - EXPERTS))[None]
     small = jnp.concatenate([norm_grad, count_row, jnp.zeros((1, D), jnp.float32)], axis=0)
     small_sum = butterfly_sum(small, jnp.float32)
     norm_sum, count_sum = small_sum[:6], small_sum[6, :EXPERTS]

time: 821 us -> 469 us (0.57)
  local copies, waits for them, and re-layouts: 212 us -> 25.4 us
  Pallas kernels: 0 us -> 110 us
  other arithmetic: 170 us -> 61.9 us
  matrix products: 166 us -> 63.3 us
  waiting for transfers between devices: 216 us -> 149 us
  starting transfers between devices: 29.5 us -> 38.3 us
    pallas_call x0 -> x3, Pallas kernels: none -> 110 us  [the longest x2 108 us: moe(): pl.pallas_call(functools.partial(moe_kernel, offset, count, start is not...]
    ppermute x0 -> x15, waiting for transfers between devices: none -> 103 us  [to_peers(): lax.ppermute(arrays[k], 'expert', [(i, i ^ k) for i in range(groups)])]
    dot_general x12 -> x0, matrix products: 101 us -> none  [the longest x1 31.5 us: expert_backward_parts(): jnp.einsum('erd,fed->erf', rows_grad, outer_part, preferred_element_type=...]
    gather x4 -> x0, local copies, waits for them, and re-layouts: 78.5 us -> none  [the longest x1 21.2 us: body(): slots_grad = pair_pad[source].reshape(local_count, groups, CAP, D)]
    convert_element_type x6 -> x2, other arithmetic: 80.1 us -> 3.28 us  [the longest x1 2.21 us: body(): attn_grad_low = hidden_grad.astype(jnp.bfloat16)]
    all_to_all x4 -> x0, waiting for transfers between devices: 75.7 us -> none  [the longest x1 39.8 us: body(): lax.all_to_all(slots_grad, 'expert', split_axis=1, concat_axis=1, tiled=T...]
    unnamed x6 -> x4, waiting for transfers between devices: 55.4 us -> 0.07 us
    all_gather x2, waiting for transfers between devices: 45.3 us -> 0.02 us  [the longest x1 0.02 us: body(): lax.all_gather(both[:, half:], 'hidden', axis=0, tiled=True)]
  transfers between devices with their start and end apart: 23 -> 34, of which waited for: 16 -> 20; matrix products, arithmetic and copies ran while one was open for 29% -> 27% of each run, Pallas kernels for 0% -> 12%
where the time goes in v2:
time: 469 us; the launch traced here: 463 us
  waiting for transfers between devices  149 us (32%)
  Pallas kernels  110 us (23%)
  matrix products  63.3 us (13%)
  other arithmetic  61.9 us (13%)
  starting transfers between devices  38.3 us (8%)
  local copies, waits for them, and re-layouts  25.4 us (5%)
  between operations  15.4 us (3%)
    pallas_call x2, Pallas kernels, moe(): pl.pallas_call(functools.partial(moe_kernel, offset, count, start is not...  108 us
    ppermute x15, waiting for transfers between devices, to_peers(): lax.ppermute(arrays[k], 'expert', [(i, i ^ k) for i in range(groups)])  103 us
    ppermute x5, waiting for transfers between devices, butterfly_sum(): got = lax.ppermute(send, axis, [(i, i ^ bit) for i in range(size)])  22.8 us
    ppermute x15, starting transfers between devices, to_peers(): lax.ppermute(arrays[k], 'expert', [(i, i ^ k) for i in range(groups)])  18.8 us
    convert_element_type x2, other arithmetic, attend_backward(): score_grad = (probs * (prob_grad - row_dot)).astype(jnp.bfloat16)  18.4 us
    dot_general x2, matrix products, attend_backward(): jnp.einsum('qhd,khd->hqk', grad_rows, value_heads, preferred_element_type...  14.8 us
    ppermute x5, waiting for transfers between devices, butterfly_sum(): got = lax.ppermute(value, axis, [(i, i ^ bit) for i in range(size)])  12.7 us
    unnamed x178, local copies, waits for them, and re-layouts  12.1 us
  transfers between devices with their start and end apart: 34, of which 20 were waited for; matrix products, arithmetic and copies ran while one was open for 27% of the time, Pallas kernels for 12%

profile of v2, /device:TPU:0, one launch (start us, length us, event | category | flops | bytes accessed | tf_op | source)
XLA Modules:
  0.0 463.4 jit_solution(8772920381485749526)
XLA Ops:
  7.2 2.0 convert_bitcast_fusion
  10.1 1.8 copy.63
  14.1 3.1 collective-permute-start.1
  18.7 2.9 collective-permute-start.8
  23.6 3.0 convolution_convert_fusion
  26.5 3.0 copy.60
  30.2 2.4 fusion.78
  32.6 2.4 fusion.79
  35.0 2.8 fusion.1
  37.8 2.8 fusion
  40.7 3.2 fusion.40
  43.9 3.2 fusion.39
  51.1 1.5 add_convert_fusion.2.rest_0_
  53.0 2.7 collective-permute-start.5
  57.2 2.2 route.1
  59.4 14.0 %collective-permute-done.6.rest_5_ = bf16[1024,384]{1,0:T(8,128)(2,1)S(1)} collective-permute-done((bf16[1024,384]{1,0:T(8,128)(2,1)}, bf16[1024,384]{1,0:T(8,128)(2,1)S(1)}, u32[]{:S(2)}, u32[]{:S(2)}) %collective-permute-start.6) | collective-permute-done | bytes 786464 | tf_op jit(solution)/shard_map/ppermute | solution.py:300
  73.3 17.8 %collective-permute-done.5.rest_3_ = bf16[1024,384]{1,0:T(8,128)(2,1)S(1)} collective-permute-done((bf16[1024,384]{1,0:T(8,128)(2,1)S(1)}, bf16[1024,384]{1,0:T(8,128)(2,1)S(1)}, u32[]{:S(2)}, u32[]{:S(2)}) %collective-permute-start.5) | collective-permute-done | bytes 786464 | tf_op jit(solution)/shard_map/ppermute | solution.py:300
  91.2 13.7 %collective-permute-done.3.rest_1_ = bf16[1024,384]{1,0:T(8,128)(2,1)} collective-permute-done((bf16[1024,384]{1,0:T(8,128)(2,1)S(1)}, bf16[1024,384]{1,0:T(8,128)(2,1)}, u32[]{:S(2)}, u32[]{:S(2)}) %collective-permute-start.3) | collective-permute-done | bytes 786464 | tf_op jit(solution)/shard_map/ppermute | solution.py:300
  104.9 52.8 %moe.2 = (f32[4,1024,768]{2,1,0:T(8,128)}, bf16[1536,1536]{1,0:T(8,128)(2,1)}) custom-call(s32[4,4,1024]{2,1,0:T(4,128)} %get-tuple-element.32.rows_ref, f32[4,4,1024]{2,1,0:T(4,128)} %get-tuple-element.33.gate_rows_ref, s32[1024,128]{1,0:T(8,128)} %get-tuple-element.34.cols_ref, bf16[1024,384]{1,0:T(8,128)(2,1)} %copy-done.45, ...), custom_call_target="tpu_custom_call" | custom-call | flops 26172456960 | bytes 41943040 | tf_op jit(solution)/shard_map/moe/pallas_call | solution.py:279
  157.7 55.0 %moe.3 = (bf16[1024,384]{1,0:T(8,128)(2,1)}, bf16[1024,384]{1,0:T(8,128)(2,1)}, bf16[1024,384]{1,0:T(8,128)(2,1)}, bf16[1024,384]{1,0:T(8,128)(2,1)}, bf16[1024,...) custom-call(s32[4,4,1024]{2,1,0:T(4,128)} %get-tuple-element.32.rows, ...), custom_call_target="tpu_custom_call" | custom-call | flops 26172456960 | bytes 41943040 | tf_op jit(solution)/shard_map/moe/pallas_call | solution.py:279
  213.2 1.5 collective-permute-start.13
  214.7 1.5 collective-permute-start.14
  217.5 1.5 collective-permute-start.10
  219.0 14.4 %collective-permute-done.12 = bf16[1024,384]{1,0:T(8,128)(2,1)S(1)} collective-permute-done((bf16[1024,384]{1,0:T(8,128)(2,1)}, bf16[1024,384]{1,0:T(8,128)(2,1)S(1)}, u32[]{:S(2)}, u32[]{:S(2)}) %collective-permute-start.12) | collective-permute-done | bytes 786464 | tf_op jit(solution)/shard_map/ppermute | solution.py:300
  235.7 14.7 %collective-permute-done.13 = bf16[1024,384]{1,0:T(8,128)(2,1)} collective-permute-done((bf16[1024,384]{1,0:T(8,128)(2,1)}, bf16[1024,384]{1,0:T(8,128)(2,1)}, u32[]{:S(2)}, u32[]{:S(2)}) %collective-permute-start.13) | collective-permute-done | bytes 786464 | tf_op jit(solution)/shard_map/ppermute | solution.py:300
  251.3 3.0 multiply_reduce_fusion.2
  254.3 12.9 %collective-permute-done.9 = bf16[1024,384]{1,0:T(8,128)(2,1)} collective-permute-done((bf16[1024,384]{1,0:T(8,128)(2,1)}, bf16[1024,384]{1,0:T(8,128)(2,1)}, u32[]{:S(2)}, u32[]{:S(2)}) %collective-permute-start.9) | collective-permute-done | bytes 786464 | tf_op jit(solution)/shard_map/ppermute | solution.py:300
  267.3 14.4 %collective-permute-done.11 = bf16[1024,384]{1,0:T(8,128)(2,1)} collective-permute-done((bf16[1024,384]{1,0:T(8,128)(2,1)}, bf16[1024,384]{1,0:T(8,128)(2,1)}, u32[]{:S(2)}, u32[]{:S(2)}) %collective-permute-start.11) | collective-permute-done | bytes 786464 | tf_op jit(solution)/shard_map/ppermute | solution.py:300
  281.7 3.3 fusion.73
  284.9 2.2 fusion.42
  288.6 7.5 %multiply_reduce_fusion.1 = (f32[6,512]{1,0:T(8,128)S(1)}, f32[6,512,1024]{2,1,0:T(8,128)}) fusion(f32[6,512,1024]{2,1,0:T(8,128)S(1)} %bitcast.105, f32[6,512]{1,0:T(8,128)S(1)} %log_add_fusion.1, bf16[512,6,64]{0,2,1:T(8,128)(2,1)S(1)} %bitcast.122, bf16[1024,3,6,64]{0,3,2,1:T(8,128)(2,1)} %bitcast.114), kind=kOutput, calls=%fused_computation.4 | convolution fusion | flops 412087296 | bytes 26370048 | tf_op jit(solution)/shard_map/qhd,khd->hqk/dot_general | solution.py:90
  296.1 9.3 %multiply_convert_fusion.1 = bf16[6,512,1024]{2,1,0:T(8,128)(2,1)} fusion(f32[6,512,1024]{2,1,0:T(8,128)} %get-tuple-element.104, f32[6,512,1024]{2,1,0:T(8,128)S(1)} %bitcast.105, f32[6,512]{1,0:T(8,128)S(1)} %get-tuple-element.103, f32[6,512]{1,0:T(8,128)S(1)} %log_add_fusion.1), kind=kLoop, calls=%fused_computation.3 | loop fusion | flops 12582912 | bytes 31481856 | tf_op jit(solution)/shard_map/convert_element_type | solution.py:94
  305.4 5.8 %fusion.38 = bf16[512,6,64]{0,2,1:T(8,128)(2,1)} fusion(bf16[6,512,1024]{2,1,0:T(8,128)(2,1)} %multiply_convert_fusion.1, bf16[1024,3,6,64]{0,3,2,1:T(8,128)(2,1)} %bitcast.115), kind=kOutput, calls=%fused_computation.73 | convolution fusion | flops 403046400 | bytes 7471104 | tf_op jit(solution)/shard_map/hqk,khd->qhd/dot_general | solution.py:96
  311.2 7.4 %multiply_reduce_fusion = (f32[6,512]{1,0:T(8,128)S(1)}, f32[6,512,1024]{2,1,0:T(8,128)}) fusion(f32[6,512,1024]{2,1,0:T(8,128)S(1)} %bitcast.107, f32[6,512]{1,0:T(8,128)S(1)} %log_add_fusion, bf16[512,6,64]{0,2,1:T(8,128)(2,1)} %bitcast.124, bf16[1024,3,6,64]{0,3,2,1:T(8,128)(2,1)} %bitcast.116), kind=kOutput, calls=%fused_computation.1 | convolution fusion | flops 412087296 | bytes 26370048 | tf_op jit(solution)/shard_map/qhd,khd->hqk/dot_general | solution.py:90
  318.6 9.1 %multiply_convert_fusion = bf16[6,512,1024]{2,1,0:T(8,128)(2,1)} fusion(f32[6,512,1024]{2,1,0:T(8,128)} %get-tuple-element.106, f32[6,512,1024]{2,1,0:T(8,128)S(1)} %bitcast.107, f32[6,512]{1,0:T(8,128)S(1)} %get-tuple-element.105, f32[6,512]{1,0:T(8,128)S(1)} %log_add_fusion), kind=kLoop, calls=%fused_computation | loop fusion | flops 12582912 | bytes 31481856 | tf_op jit(solution)/shard_map/convert_element_type | solution.py:94
  327.7 4.9 %fusion.37 = bf16[512,6,64]{0,2,1:T(8,128)(2,1)S(1)} fusion(bf16[6,512,1024]{2,1,0:T(8,128)(2,1)} %multiply_convert_fusion, bf16[1024,3,6,64]{0,3,2,1:T(8,128)(2,1)S(1)} %bitcast.117), kind=kOutput, calls=%fused_computation.72 | convolution fusion | flops 403046400 | bytes 7471104 | tf_op jit(solution)/shard_map/hqk,khd->qhd/dot_general | solution.py:96
  333.6 4.6 fusion.54
  338.3 2.1 fusion.32
  340.4 2.5 fusion.4
  342.9 2.5 fusion.29
  348.6 1.6 fusion.67
  353.1 2.6 collective-permute-done.20
  355.7 2.0 convert_add_fusion.1
  360.0 10.2 %collective-permute-done.21 = bf16[128,1536]{1,0:T(8,128)(2,1)S(1)} collective-permute-done((bf16[128,1536]{1,0:T(8,128)(2,1)S(1)}, bf16[128,1536]{1,0:T(8,128)(2,1)S(1)}, u32[]{:S(2)}, u32[]{:S(2)}) %collective-permute-start.21) | collective-permute-done | bytes 393248 | tf_op jit(solution)/shard_map/ppermute | solution.py:324
  373.7 5.0 %collective-permute-done.22 = bf16[64,1536]{1,0:T(8,128)(2,1)S(1)} collective-permute-done((bf16[64,1536]{1,0:T(8,128)(2,1)S(1)}, bf16[64,1536]{1,0:T(8,128)(2,1)S(1)}, u32[]{:S(2)}, u32[]{:S(2)}) %collective-permute-start.22) | collective-permute-done | bytes 196640 | tf_op jit(solution)/shard_map/ppermute | solution.py:324
  379.9 2.0 collective-permute-start.23
  382.0 4.8 %collective-permute-done.23 = bf16[32,1536]{1,0:T(8,128)(2,1)S(1)} collective-permute-done((bf16[32,1536]{1,0:T(8,128)(2,1)S(1)}, bf16[32,1536]{1,0:T(8,128)(2,1)S(1)}, u32[]{:S(2)}, u32[]{:S(2)}) %collective-permute-start.23) | collective-permute-done | bytes 98336 | tf_op jit(solution)/shard_map/ppermute | solution.py:324
  386.8 3.0 collective-permute-start.24
  389.8 4.1 fusion.71
  394.1 2.4 collective-permute-start.25
  397.6 3.2 collective-permute-done.25
  400.9 2.9 collective-permute-start.26
  403.7 5.3 %collective-permute-done.26 = bf16[32,1536]{1,0:T(8,128)(2,1)S(1)} collective-permute-done((bf16[32,1536]{1,0:T(8,128)(2,1)S(1)}, bf16[32,1536]{1,0:T(8,128)(2,1)S(1)}, u32[]{:S(2)}, u32[]{:S(2)}) %collective-permute-start.26) | collective-permute-done | bytes 98336 | tf_op jit(solution)/shard_map/ppermute | solution.py:332
  410.6 4.3 collective-permute-done.27
  419.1 3.9 collective-permute-done.16
  423.6 3.1 collective-permute-done.17
  426.7 1.6 collective-permute-start.18
  428.3 2.7 collective-permute-done.18
  431.0 2.0 collective-permute-start.19
  433.3 3.1 add_add_fusion.2
  442.4 2.8 multiply_add_fusion
  445.3 1.9 concatenate.54
  447.7 2.0 concatenate.53
  452.3 4.3 multiply_add_fusion.2
  (298 shorter events, 50.2 us)
Async XLA Ops:
  7.2 97.7 %all-gather.5.cloned.1.call-start = ((), (), s32[]{:S(2)}) async-start(), calls=%async_computation.3 | async-start | bytes 5308416 | tf_op jit(solution)/shard_map/all_gather | solution.py:379
  12.9 9.3 %copy-start.11 = (bf16[1024,384]{1,0:T(8,128)(2,1)S(1)}, bf16[1024,384]{1,0:T(8,128)(2,1)}, u32[]{:S(2)}) copy-start(bf16[1024,384]{1,0:T(8,128)(2,1)} %param.21) | copy-start | bytes 2359300
  14.0 8.9 %copy-start.72 = (s32[1,1024]{1,0:T(1,128)S(1)}, s32[1,1024]{1,0:T(1,128)}, u32[]{:S(2)}) copy-start(s32[1,1024]{1,0:T(1,128)} %param.26) | copy-start | bytes 12292
  14.0 9.0 %copy-start.52 = (f32[6,384]{1,0:T(8,128)S(1)}, f32[6,384]{1,0:T(8,128)}, u32[]{:S(2)}) copy-start(f32[6,384]{1,0:T(8,128)} %param.27) | copy-start | bytes 27652
  14.0 9.6 %copy-start.33 = (f32[384,1152]{1,0:T(8,128)S(1)}, f32[384,1152]{1,0:T(8,128)}, u32[]{:S(2)}) copy-start(f32[384,1152]{1,0:T(8,128)} %param.28) | copy-start | bytes 5308420
  14.0 143.7 %all-gather.3.cloned.1.call-start = ((), (), s32[]{:S(2)}) async-start(), calls=%async_computation.2 | async-start | bytes 5308416 | tf_op jit(solution)/shard_map/all_gather | solution.py:380
  14.1 38.5 %collective-permute-start.1 = (f32[8,1024]{1,0:T(8,128)S(1)}, f32[8,1024]{1,0:T(8,128)S(1)}, u32[]{:S(2)}, u32[]{:S(2)}) collective-permute-start(f32[8,1024]{1,0:T(8,128)S(1)} %get-tuple-element.92), channel_id=1, source_target_pairs={{0,16},{8,24},{16,0},{24,8},{1,17},{9,25},{17,1},{25,9},{2,18},{10... | collective-permute-start | bytes 98312 | tf_op jit(solution)/shard_map/ppermute | solution.py:300
  17.2 35.9 %collective-permute-start = (f32[8,1024]{1,0:T(8,128)S(1)}, f32[8,1024]{1,0:T(8,128)S(1)}, u32[]{:S(2)}, u32[]{:S(2)}) collective-permute-start(f32[8,1024]{1,0:T(8,128)S(1)} %get-tuple-element.92), channel_id=1, source_target_pairs={{0,8},{8,0},{16,24},{24,16},{1,9},{9,1},{17,25},{25,17},{2,10},{10... | collective-permute-start | bytes 98312 | tf_op jit(solution)/shard_map/ppermute | solution.py:300
  18.7 37.0 %collective-permute-start.2 = (f32[8,1024]{1,0:T(8,128)S(1)}, f32[8,1024]{1,0:T(8,128)S(1)}, u32[]{:S(2)}, u32[]{:S(2)}) collective-permute-start(f32[8,1024]{1,0:T(8,128)S(1)} %get-tuple-element.92), channel_id=1, source_target_pairs={{0,24},{8,16},{16,8},{24,0},{1,25},{9,17},{17,9},{25,1},{2,26},{10... | collective-permute-start | bytes 98312 | tf_op jit(solution)/shard_map/ppermute | solution.py:300
  18.7 37.5 %collective-permute-start.8 = (bf16[1024,384]{1,0:T(8,128)(2,1)}, bf16[1024,384]{1,0:T(8,128)(2,1)}, u32[]{:S(2)}, u32[]{:S(2)}) collective-permute-start(bf16[1024,384]{1,0:T(8,128)(2,1)} %rest_4_.3), channel_id=1, source_target_pairs={{0,24},{8,16},{16,8},{24,0},{1,25},{9,17},{17,9},{25,1},{2,26},{10... | collective-permute-start | bytes 2359304 | tf_op jit(solution)/shard_map/ppermute | solution.py:300
  21.6 37.8 %collective-permute-start.7 = (bf16[1024,384]{1,0:T(8,128)(2,1)}, bf16[1024,384]{1,0:T(8,128)(2,1)}, u32[]{:S(2)}, u32[]{:S(2)}) collective-permute-start(bf16[1024,384]{1,0:T(8,128)(2,1)} %rest_4_.3), channel_id=1, source_target_pairs={{0,16},{8,24},{16,0},{24,8},{1,17},{9,25},{17,1},{25,9},{2,18},{10... | collective-permute-start | bytes 2359304 | tf_op jit(solution)/shard_map/ppermute | solution.py:300
  22.1 423.2 %reduce-scatter.5.cloned.1.call-start = ((), (), s32[]{:S(2)}) async-start(), calls=%async_computation.5 | async-start | bytes 5308416 | tf_op jit(solution)/shard_map/reduce_scatter | solution.py:428
  29.5 14.4 %copy-start.4 = (bf16[1024,1152]{0,1:T(8,128)(2,1)}, bf16[1024,1152]{0,1:T(8,128)(2,1)S(1)}, u32[]{:S(2)}) copy-start(bf16[1024,1152]{0,1:T(8,128)(2,1)S(1)} %copy.60) | copy-start | bytes 7077892
  32.6 8.1 %copy-start.1 = (f32[6,512,1024]{2,1,0:T(8,128)}, f32[6,512,1024]{2,1,0:T(8,128)S(1)}, u32[]{:S(2)}) copy-start(f32[6,512,1024]{2,1,0:T(8,128)S(1)} %get-tuple-element.98) | copy-start | bytes 37748740
  32.6 8.1 %copy-start.51 = (f32[6,512]{1,0:T(8,128)}, f32[6,512]{1,0:T(8,128)S(1)}, u32[]{:S(2)}) copy-start(f32[6,512]{1,0:T(8,128)S(1)} %get-tuple-element.97) | copy-start | bytes 36868
  35.0 8.9 %copy-start = (f32[6,512,1024]{2,1,0:T(8,128)}, f32[6,512,1024]{2,1,0:T(8,128)S(1)}, u32[]{:S(2)}) copy-start(f32[6,512,1024]{2,1,0:T(8,128)S(1)} %get-tuple-element.100) | copy-start | bytes 37748740
  35.0 8.9 %copy-start.50 = (f32[6,512]{1,0:T(8,128)}, f32[6,512]{1,0:T(8,128)S(1)}, u32[]{:S(2)}) copy-start(f32[6,512]{1,0:T(8,128)S(1)} %get-tuple-element.99) | copy-start | bytes 36868
  52.6 20.7 %collective-permute-start.6 = (bf16[1024,384]{1,0:T(8,128)(2,1)}, bf16[1024,384]{1,0:T(8,128)(2,1)S(1)}, u32[]{:S(2)}, u32[]{:S(2)}) collective-permute-start(bf16[1024,384]{1,0:T(8,128)(2,1)} %rest_4_.3), channel_id=1, source_target_pairs={{0,8},{8,0},{16,24},{24,16},{1,9},{9,1},{17,25},{25,17},{2,10},{10... | collective-permute-start | bytes 2359304 | tf_op jit(solution)/shard_map/ppermute | solution.py:300
  53.0 38.1 %collective-permute-start.5 = (bf16[1024,384]{1,0:T(8,128)(2,1)S(1)}, bf16[1024,384]{1,0:T(8,128)(2,1)S(1)}, u32[]{:S(2)}, u32[]{:S(2)}) collective-permute-start(bf16[1024,384]{1,0:T(8,128)(2,1)S(1)} %add_convert_fusion.2.rest_0_), channel_id=1, source_target_pairs={{0,24},{8,16},{16,8},{24,0},{1,25},{9,17},{17,9},{25,1},{2,26},{10... | collective-permute-start | bytes 2359304 | tf_op jit(solution)/shard_map/ppermute | solution.py:300
  55.7 35.5 %collective-permute-start.4 = (bf16[1024,384]{1,0:T(8,128)(2,1)S(1)}, bf16[1024,384]{1,0:T(8,128)(2,1)S(1)}, u32[]{:S(2)}, u32[]{:S(2)}) collective-permute-start(bf16[1024,384]{1,0:T(8,128)(2,1)S(1)} %add_convert_fusion.2.rest_0_), channel_id=1, source_target_pairs={{0,16},{8,24},{16,0},{24,8},{1,17},{9,25},{17,1},{25,9},{2,18},{10... | collective-permute-start | bytes 2359304 | tf_op jit(solution)/shard_map/ppermute | solution.py:300
  56.2 48.7 %collective-permute-start.3 = (bf16[1024,384]{1,0:T(8,128)(2,1)S(1)}, bf16[1024,384]{1,0:T(8,128)(2,1)}, u32[]{:S(2)}, u32[]{:S(2)}) collective-permute-start(bf16[1024,384]{1,0:T(8,128)(2,1)S(1)} %add_convert_fusion.2.rest_0_), channel_id=1, source_target_pairs={{0,8},{8,0},{16,24},{24,16},{1,9},{9,1},{17,25},{25,17},{2,10},{10... | collective-permute-start | bytes 2359304 | tf_op jit(solution)/shard_map/ppermute | solution.py:300
  73.3 31.6 %copy-start.78 = (bf16[1024,384]{1,0:T(8,128)(2,1)}, bf16[1024,384]{1,0:T(8,128)(2,1)S(1)}, u32[]{:S(2)}) copy-start(bf16[1024,384]{1,0:T(8,128)(2,1)S(1)} %collective-permute-done.6.rest_5_) | copy-start | bytes 2359300
  91.2 13.7 %copy-start.79 = (bf16[1024,384]{1,0:T(8,128)(2,1)}, bf16[1024,384]{1,0:T(8,128)(2,1)S(1)}, u32[]{:S(2)}) copy-start(bf16[1024,384]{1,0:T(8,128)(2,1)S(1)} %collective-permute-done.5.rest_3_) | copy-start | bytes 2359300
  91.2 13.7 %copy-start.80 = (bf16[1024,384]{1,0:T(8,128)(2,1)}, bf16[1024,384]{1,0:T(8,128)(2,1)S(1)}, u32[]{:S(2)}) copy-start(bf16[1024,384]{1,0:T(8,128)(2,1)S(1)} %collective-permute-done.4.rest_2_) | copy-start | bytes 2359300
  212.7 20.7 %collective-permute-start.12 = (bf16[1024,384]{1,0:T(8,128)(2,1)}, bf16[1024,384]{1,0:T(8,128)(2,1)S(1)}, u32[]{:S(2)}, u32[]{:S(2)}) collective-permute-start(bf16[1024,384]{1,0:T(8,128)(2,1)} %get-tuple-element.41), channel_id=1, source_target_pairs={{0,8},{8,0},{16,24},{24,16},{1,9},{9,1},{17,25},{25,17},{2,10},{10... | collective-permute-start | bytes 2359304 | tf_op jit(solution)/shard_map/ppermute | solution.py:300
  213.2 37.1 %collective-permute-start.13 = (bf16[1024,384]{1,0:T(8,128)(2,1)}, bf16[1024,384]{1,0:T(8,128)(2,1)}, u32[]{:S(2)}, u32[]{:S(2)}) collective-permute-start(bf16[1024,384]{1,0:T(8,128)(2,1)} %get-tuple-element.42), channel_id=1, source_target_pairs={{0,16},{8,24},{16,0},{24,8},{1,17},{9,25},{17,1},{25,9},{2,18},{10... | collective-permute-start | bytes 2359304 | tf_op jit(solution)/shard_map/ppermute | solution.py:300
  214.7 36.5 %collective-permute-start.14 = (bf16[1024,384]{1,0:T(8,128)(2,1)}, bf16[1024,384]{1,0:T(8,128)(2,1)}, u32[]{:S(2)}, u32[]{:S(2)}) collective-permute-start(bf16[1024,384]{1,0:T(8,128)(2,1)} %get-tuple-element.43), channel_id=1, source_target_pairs={{0,24},{8,16},{16,8},{24,0},{1,25},{9,17},{17,9},{25,1},{2,26},{10... | collective-permute-start | bytes 2359304 | tf_op jit(solution)/shard_map/ppermute | solution.py:300
  217.0 50.3 %collective-permute-start.9 = (bf16[1024,384]{1,0:T(8,128)(2,1)}, bf16[1024,384]{1,0:T(8,128)(2,1)}, u32[]{:S(2)}, u32[]{:S(2)}) collective-permute-start(bf16[1024,384]{1,0:T(8,128)(2,1)} %get-tuple-element.37), channel_id=1, source_target_pairs={{0,8},{8,0},{16,24},{24,16},{1,9},{9,1},{17,25},{25,17},{2,10},{10... | collective-permute-start | bytes 2359304 | tf_op jit(solution)/shard_map/ppermute | solution.py:300
  217.5 49.8 %collective-permute-start.10 = (bf16[1024,384]{1,0:T(8,128)(2,1)}, bf16[1024,384]{1,0:T(8,128)(2,1)}, u32[]{:S(2)}, u32[]{:S(2)}) collective-permute-start(bf16[1024,384]{1,0:T(8,128)(2,1)} %get-tuple-element.38), channel_id=1, source_target_pairs={{0,16},{8,24},{16,0},{24,8},{1,17},{9,25},{17,1},{25,9},{2,18},{10... | collective-permute-start | bytes 2359304 | tf_op jit(solution)/shard_map/ppermute | solution.py:300
  233.4 48.2 %collective-permute-start.11 = (bf16[1024,384]{1,0:T(8,128)(2,1)}, bf16[1024,384]{1,0:T(8,128)(2,1)}, u32[]{:S(2)}, u32[]{:S(2)}) collective-permute-start(bf16[1024,384]{1,0:T(8,128)(2,1)} %get-tuple-element.39), channel_id=1, source_target_pairs={{0,24},{8,16},{16,8},{24,0},{1,25},{9,17},{17,9},{25,1},{2,26},{10... | collective-permute-start | bytes 2359304 | tf_op jit(solution)/shard_map/ppermute | solution.py:300
  235.6 15.7 %copy-start.3 = (f32[1024,384]{1,0:T(8,128)S(1)}, f32[1024,384]{1,0:T(8,128)}, u32[]{:S(2)}) copy-start(f32[1024,384]{1,0:T(8,128)} %copy-done.2) | copy-start | bytes 4718596
  235.6 15.7 %copy-start.43 = (bf16[1024,384]{1,0:T(8,128)(2,1)S(1)}, bf16[1024,384]{1,0:T(8,128)(2,1)}, u32[]{:S(2)}) copy-start(bf16[1024,384]{1,0:T(8,128)(2,1)} %get-tuple-element.40) | copy-start | bytes 2359300
  235.6 15.7 %copy-start.49 = (f32[1024]{0:T(1024)S(1)}, f32[1024]{0:T(1024)}, u32[]{:S(2)}) copy-start(f32[1024]{0:T(1024)} %copy-done.48) | copy-start | bytes 12292
  235.6 212.1 %reduce-scatter.3.cloned.1.call-start = ((), (), s32[]{:S(2)}) async-start(), calls=%async_computation.4 | async-start | bytes 5308416 | tf_op jit(solution)/shard_map/reduce_scatter | solution.py:428
  251.3 30.4 %copy-start.9 = (f32[1024,384]{1,0:T(8,128)S(1)}, f32[1024,384]{1,0:T(8,128)}, u32[]{:S(2)}) copy-start(f32[1024,384]{1,0:T(8,128)} %copy-done.8) | copy-start | bytes 4718596
  251.3 30.4 %copy-start.42 = (bf16[1024,384]{1,0:T(8,128)(2,1)S(1)}, bf16[1024,384]{1,0:T(8,128)(2,1)}, u32[]{:S(2)}) copy-start(bf16[1024,384]{1,0:T(8,128)(2,1)} %get-tuple-element.36) | copy-start | bytes 2359300
  251.3 30.4 %copy-start.55 = (f32[1024]{0:T(1024)S(1)}, f32[1024]{0:T(1024)}, u32[]{:S(2)}) copy-start(f32[1024]{0:T(1024)} %copy-done.54) | copy-start | bytes 12292
  251.3 37.3 %slice-start = ((s8[12582912]{0:T(1024)(128)(4,1)}), s8[4194304]{0:T(1024)(128)(4,1)S(1)}, s32[]{:S(2)}) async-start(s8[12582912]{0:T(1024)(128)(4,1)} %bitcast.104), calls=%async_computation.6 | async-start | bytes 8388608
  254.3 30.6 %copy-start.6 = (f32[1024,384]{1,0:T(8,128)}, f32[1024,384]{1,0:T(8,128)S(1)}, u32[]{:S(2)}) copy-start(f32[1024,384]{1,0:T(8,128)S(1)} %get-tuple-element.70) | copy-start | bytes 4718596
  281.6 7.0 %slice-start.1 = ((s8[12582912]{0:T(1024)(128)(4,1)}), s8[4194304]{0:T(1024)(128)(4,1)S(1)}, s32[]{:S(2)}) async-start(s8[12582912]{0:T(1024)(128)(4,1)} %bitcast.104), calls=%async_computation.7 | async-start | bytes 8388608
  288.6 22.6 %slice-start.3 = ((s8[12582912]{0:T(1024)(128)(4,1)}), s8[4194304]{0:T(1024)(128)(4,1)S(1)}, s32[]{:S(2)}) async-start(s8[12582912]{0:T(1024)(128)(4,1)} %bitcast.106), calls=%async_computation.9 | async-start | bytes 8388608
  288.6 22.6 %slice-start.4 = ((s8[12582912]{0:T(1024)(128)(4,1)}), s8[4194304]{0:T(1024)(128)(4,1)S(1)}, s32[]{:S(2)}) async-start(s8[12582912]{0:T(1024)(128)(4,1)} %bitcast.106), calls=%async_computation.10 | async-start | bytes 8388608
  296.1 15.1 %slice-start.5 = ((s8[12582912]{0:T(1024)(128)(4,1)}), s8[4194304]{0:T(1024)(128)(4,1)S(1)}, s32[]{:S(2)}) async-start(s8[12582912]{0:T(1024)(128)(4,1)} %bitcast.106), calls=%async_computation.11 | async-start | bytes 8388608
  318.6 9.1 %copy-start.5 = (bf16[1024,1152]{0,1:T(8,128)(2,1)S(1)}, bf16[1024,1152]{0,1:T(8,128)(2,1)}, u32[]{:S(2)}) copy-start(bf16[1024,1152]{0,1:T(8,128)(2,1)} %copy-done.4) | copy-start | bytes 7077892
  353.1 2.6 collective-permute-start.20
  358.9 11.2 %collective-permute-start.21 = (bf16[128,1536]{1,0:T(8,128)(2,1)S(1)}, bf16[128,1536]{1,0:T(8,128)(2,1)S(1)}, u32[]{:S(2)}, u32[]{:S(2)}) collective-permute-start(bf16[128,1536]{1,0:T(8,128)(2,1)S(1)} %select_convert_fusion.1), channel_id=1, source_target_pairs={{0,8},{8,0},{16,24},{24,16},{1,9},{9,1},{17,25},{25,17},{2,10},{10... | collective-permute-start | bytes 1179656 | tf_op jit(solution)/shard_map/ppermute | solution.py:324
  360.0 13.5 %copy-start.61 = (s32[1024,4]{0,1:T(4,128)S(1)}, s32[1024,4]{0,1:T(4,128)}, u32[]{:S(2)}) copy-start(s32[1024,4]{0,1:T(4,128)} %param.23) | copy-start | bytes 49156
  372.6 6.2 %collective-permute-start.22 = (bf16[64,1536]{1,0:T(8,128)(2,1)S(1)}, bf16[64,1536]{1,0:T(8,128)(2,1)S(1)}, u32[]{:S(2)}, u32[]{:S(2)}) collective-permute-start(bf16[64,1536]{1,0:T(8,128)(2,1)S(1)} %select_convert_fusion.2), channel_id=1, source_target_pairs={{0,16},{8,24},{16,0},{24,8},{1,17},{9,25},{17,1},{25,9},{2,18},{10... | collective-permute-start | bytes 589832 | tf_op jit(solution)/shard_map/ppermute | solution.py:324
  379.9 6.8 %collective-permute-start.23 = (bf16[32,1536]{1,0:T(8,128)(2,1)S(1)}, bf16[32,1536]{1,0:T(8,128)(2,1)S(1)}, u32[]{:S(2)}, u32[]{:S(2)}) collective-permute-start(bf16[32,1536]{1,0:T(8,128)(2,1)S(1)} %select_convert_fusion.3), channel_id=1, source_target_pairs={{0,2},{1,3},{2,0},{3,1},{4,6},{5,7},{6,4},{7,5},{8,10},{9,11},{10,... | collective-permute-start | bytes 294920 | tf_op jit(solution)/shard_map/ppermute | solution.py:324
  386.8 9.7 %copy-start.7 = (f32[1024,384]{1,0:T(8,128)S(1)}, f32[1024,384]{1,0:T(8,128)}, u32[]{:S(2)}) copy-start(f32[1024,384]{1,0:T(8,128)} %copy-done.6) | copy-start | bytes 4718596
  386.8 9.7 %copy-start.63 = (s32[1024]{0:T(1024)S(1)}, s32[1024]{0:T(1024)}, u32[]{:S(2)}) copy-start(s32[1024]{0:T(1024)} %param.25) | copy-start | bytes 12292
  386.8 7.2 %collective-permute-start.24 = (bf16[16,1536]{1,0:T(8,128)(2,1)S(1)}, bf16[16,1536]{1,0:T(8,128)(2,1)S(1)}, u32[]{:S(2)}, u32[]{:S(2)}) collective-permute-start(bf16[16,1536]{1,0:T(8,128)(2,1)S(1)} %select_convert_fusion.4), channel_id=1, source_target_pairs={{0,4},{1,5},{2,6},{3,7},{4,0},{5,1},{6,2},{7,3},{8,12},{9,13},{10,... | collective-permute-start | bytes 147464 | tf_op jit(solution)/shard_map/ppermute | solution.py:324
  393.8 15.9 %copy-start.21 = (f32[1024,384]{1,0:T(8,128)}, f32[1024,384]{1,0:T(8,128)S(1)}, u32[]{:S(2)}) copy-start(f32[1024,384]{1,0:T(8,128)S(1)} %get-tuple-element.107) | copy-start | bytes 4718596
  394.1 9.7 %copy-start.67 = (f32[1024]{0:T(1024)S(1)}, f32[1024]{0:T(1024)}, u32[]{:S(2)}) copy-start(f32[1024]{0:T(1024)} %copy-done.66) | copy-start | bytes 12292
  394.1 6.8 %collective-permute-start.25 = (bf16[16,1536]{1,0:T(8,128)(2,1)S(1)}, bf16[16,1536]{1,0:T(8,128)(2,1)S(1)}, u32[]{:S(2)}, u32[]{:S(2)}) collective-permute-start(bf16[16,1536]{1,0:T(8,128)(2,1)S(1)} %add_convert_fusion.3), channel_id=1, source_target_pairs={{0,4},{1,5},{2,6},{3,7},{4,0},{5,1},{6,2},{7,3},{8,12},{9,13},{10,... | collective-permute-start | bytes 147464 | tf_op jit(solution)/shard_map/ppermute | solution.py:332
  400.9 8.2 %collective-permute-start.26 = (bf16[32,1536]{1,0:T(8,128)(2,1)S(1)}, bf16[32,1536]{1,0:T(8,128)(2,1)S(1)}, u32[]{:S(2)}, u32[]{:S(2)}) collective-permute-start(bf16[32,1536]{1,0:T(8,128)(2,1)S(1)} %pad_maximum_fusion.9), channel_id=1, source_target_pairs={{0,2},{1,3},{2,0},{3,1},{4,6},{5,7},{6,4},{7,5},{8,10},{9,11},{10,... | collective-permute-start | bytes 294920 | tf_op jit(solution)/shard_map/ppermute | solution.py:332
  409.1 5.7 %collective-permute-start.27 = (bf16[64,1536]{1,0:T(8,128)(2,1)S(1)}, bf16[64,1536]{1,0:T(8,128)(2,1)S(1)}, u32[]{:S(2)}, u32[]{:S(2)}) collective-permute-start(bf16[64,1536]{1,0:T(8,128)(2,1)S(1)} %pad_maximum_fusion.7), channel_id=1, source_target_pairs={{0,16},{8,24},{16,0},{24,8},{1,17},{9,25},{17,1},{25,9},{2,18},{10... | collective-permute-start | bytes 589832 | tf_op jit(solution)/shard_map/ppermute | solution.py:332
  414.9 18.0 %collective-permute-start.28 = (bf16[128,1536]{1,0:T(8,128)(2,1)S(1)}, bf16[128,1536]{1,0:T(8,128)(2,1)S(1)}, u32[]{:S(2)}, u32[]{:S(2)}) collective-permute-start(bf16[128,1536]{1,0:T(8,128)(2,1)S(1)} %pad_maximum_fusion.5), channel_id=1, source_target_pairs={{0,8},{8,0},{16,24},{24,16},{1,9},{9,1},{17,25},{25,17},{2,10},{10... | collective-permute-start | bytes 1179656 | tf_op jit(solution)/shard_map/ppermute | solution.py:332
  416.6 1.2 collective-permute-start.15
  417.8 5.2 %collective-permute-start.16 = (f32[8,384]{1,0:T(8,128)S(1)}, f32[8,384]{1,0:T(8,128)S(1)}, u32[]{:S(2)}, u32[]{:S(2)}) collective-permute-start(f32[8,384]{1,0:T(8,128)S(1)} %add.201), channel_id=1, source_target_pairs={{0,8},{8,0},{16,24},{24,16},{1,9},{9,1},{17,25},{25,17},{2,10},{10... | collective-permute-start | bytes 36872 | tf_op jit(solution)/shard_map/ppermute | solution.py:327
  423.0 3.7 collective-permute-start.17
  426.7 4.2 collective-permute-start.18
  431.0 5.4 %collective-permute-start.19 = (f32[8,384]{1,0:T(8,128)S(1)}, f32[8,384]{1,0:T(8,128)S(1)}, u32[]{:S(2)}, u32[]{:S(2)}) collective-permute-start(f32[8,384]{1,0:T(8,128)S(1)} %add.204), channel_id=1, source_target_pairs={{0,4},{1,5},{2,6},{3,7},{4,0},{5,1},{6,2},{7,3},{8,12},{9,13},{10,... | collective-permute-start | bytes 36872 | tf_op jit(solution)/shard_map/ppermute | solution.py:327
  433.2 4.3 collective-permute-start.29
  (59 other events, 127.3 us)
Sparse Core Ops, SparseCore 0:
  14.1 53.9 all-gather.4
  70.3 49.9 all-gather.2
  235.7 55.2 reduce-scatter.4
  373.8 61.4 reduce-scatter.2

commit v3 on v2

--- a/solution.py
+++ b/solution.py
@@ -27,81 +27,6 @@
 NORM_EPS = 1e-06
 MASKED = -1e30
 VMEM_MOST = 67043328
-
-
-def layer_norm(values):
-    center = values - jnp.mean(values, axis=-1, keepdims=True)
-    spread = jnp.mean(center * center, axis=-1, keepdims=True)
-    return center * lax.rsqrt(spread + NORM_EPS)
-
-
-def first_norm(values, gain_row, offset_row):
-    return layer_norm(values) * gain_row + offset_row
-
-
-def attend_forward(query_heads, key_heads, value_heads, seg_marks, block_rows):
-    score_scale = HEAD ** (-0.5)
-    seq_length = query_heads.shape[0]
-    outputs = []
-    log_sums = []
-    for row_start in range(0, seq_length, block_rows):
-        query_rows = query_heads[row_start : row_start + block_rows]
-        marks_rows = seg_marks[row_start : row_start + block_rows]
-        scores = (
-            jnp.einsum("qhd,khd->hqk", query_rows, key_heads, preferred_element_type=jnp.float32)
-            * score_scale
-        )
-        scores = jnp.where(marks_rows[None, :, None] == seg_marks[None, None, :], scores, MASKED)
-        row_peak = jnp.max(scores, axis=-1, keepdims=True)
-        row_exp = jnp.exp(scores - row_peak)
-        row_total = jnp.sum(row_exp, axis=-1, keepdims=True)
-        weights_low = (row_exp / row_total).astype(jnp.bfloat16)
-        mixed_rows = jnp.einsum(
-            "hqk,khd->qhd", weights_low, value_heads, preferred_element_type=jnp.float32
-        )
-        outputs.append(mixed_rows.astype(jnp.bfloat16))
-        log_sums.append(row_peak + jnp.log(row_total))
-    return (jnp.concatenate(outputs, axis=0), log_sums)
-
-
-def attend_backward(
-    query_heads, key_heads, value_heads, seg_marks, mixed_grad, log_sums, block_rows
-):
-    score_scale = HEAD ** (-0.5)
-    seq_length = query_heads.shape[0]
-    key_grad = jnp.zeros(key_heads.shape, jnp.float32)
-    value_grad = jnp.zeros(value_heads.shape, jnp.float32)
-    query_grads = []
-    for block_index in range(seq_length // block_rows):
-        row_start = block_index * block_rows
-        query_rows = query_heads[row_start : row_start + block_rows]
-        marks_rows = seg_marks[row_start : row_start + block_rows]
-        grad_rows = mixed_grad[row_start : row_start + block_rows]
-        scores = (
-            jnp.einsum("qhd,khd->hqk", query_rows, key_heads, preferred_element_type=jnp.float32)
-            * score_scale
-        )
-        scores = jnp.where(marks_rows[None, :, None] == seg_marks[None, None, :], scores, MASKED)
-        probs = jnp.exp(scores - log_sums[block_index])
-        probs_low = probs.astype(jnp.bfloat16)
-        value_grad = value_grad + jnp.einsum(
-            "hqk,qhd->khd", probs_low, grad_rows, preferred_element_type=jnp.float32
-        )
-        prob_grad = jnp.einsum(
-            "qhd,khd->hqk", grad_rows, value_heads, preferred_element_type=jnp.float32
-        )
-        row_dot = jnp.sum(prob_grad * probs, axis=-1, keepdims=True)
-        score_grad = (probs * (prob_grad - row_dot)).astype(jnp.bfloat16)
-        query_grads.append(
-            jnp.einsum("hqk,khd->qhd", score_grad, key_heads, preferred_element_type=jnp.float32)
-            * score_scale
-        )
-        key_grad = (
-            key_grad
-            + jnp.einsum("hqk,qhd->khd", score_grad, query_rows, preferred_element_type=jnp.float32)
-            * score_scale
-        )
-    return (jnp.concatenate(query_grads, axis=0), key_grad, value_grad)
 
 
 def route_kernel(first_expert, ids_ref, gates_ref, rows_ref, gate_rows_ref, cols_ref):
@@ -295,6 +220,272 @@
     )(*operands)
 
 
+def unit_rows(values):
+    center = values - jnp.mean(values, axis=1, keepdims=True)
+    rate = lax.rsqrt(jnp.mean(center * center, axis=1, keepdims=True) + NORM_EPS)
+    return center * rate, rate
+
+
+def unit_rows_back(unit, rate, grad):
+    mean_grad = jnp.mean(grad, axis=1, keepdims=True)
+    mean_dot = jnp.mean(grad * unit, axis=1, keepdims=True)
+    return rate * (grad - mean_grad - unit * mean_dot)
+
+
+def as_column(row):
+    wide = jnp.broadcast_to(row.astype(jnp.float32), (128, row.shape[1]))
+    return jnp.transpose(wide)
+
+
+def key_range(marks_ref, row_start, block, blocks):
+    first = marks_ref[row_start]
+    last = marks_ref[row_start + block - 1]
+    begin = jnp.int32(0)
+    end = jnp.int32(0)
+    for index in range(blocks):
+        begin = begin + jnp.where(marks_ref[index * block + block - 1] < first, 1, 0)
+        end = end + jnp.where(marks_ref[index * block] <= last, 1, 0)
+    return begin, end
+
+
+def head_masks(block):
+    low_half = lax.broadcasted_iota(jnp.int32, (block, 2 * HEAD), 1) < HEAD
+    return low_half, jnp.logical_not(low_half)
+
+
+def attend_kernel(
+    block, marks_ref, x_ref, norm_ref, qkv_ref, proj_ref, seg_ref, task_ref,
+    joined_ref, key_t_ref, mixed_ref, mixed_t_ref, logs_ref, hidden_ref, u_ref, value_t, column,
+):
+    tokens = x_ref.shape[0]
+    blocks = tokens // block
+    qkv_low = qkv_ref[...].astype(jnp.bfloat16)
+    proj_low = proj_ref[...].astype(jnp.bfloat16)
+    column[...] = as_column(seg_ref[...])
+
+    def project(index, carry):
+        span = pl.ds(pl.multiple_of(index * block, block), block)
+        unit, _ = unit_rows(x_ref[span, :].astype(jnp.float32))
+        attn_in = (unit * norm_ref[0:1, :] + norm_ref[1:2, :]).astype(jnp.bfloat16)
+        joined = mxu(attn_in, qkv_low)
+        joined_ref[span, :] = joined.astype(jnp.bfloat16)
+        key_t_ref[:, span] = jnp.transpose(joined[:, D : 2 * D]).astype(jnp.bfloat16)
+        value_t[:, span] = jnp.transpose(joined[:, 2 * D :]).astype(jnp.bfloat16)
+        return carry
+
+    lax.fori_loop(0, blocks, project, 0)
+
+    def rows(index, carry):
+        start = pl.multiple_of(index * block, block)
+        span = pl.ds(start, block)
+        begin, end = key_range(marks_ref, index * block, block, blocks)
+        seg_row = seg_ref[:, span].astype(jnp.float32)
+        masks = head_masks(block)
+        for pair in range(HEADS // 2):
+            lanes = slice(pair * 2 * HEAD, (pair + 1) * 2 * HEAD)
+            query = joined_ref[span, lanes] * jnp.bfloat16(HEAD ** (-0.5))
+            queries = [jnp.where(m, query, jnp.zeros_like(query)) for m in masks]
+
+            def keys(at, state):
+                key_span = pl.ds(pl.multiple_of(at * block, block), block)
+                key_pair = joined_ref[key_span, D + pair * 2 * HEAD : D + (pair + 1) * 2 * HEAD]
+                seg_col = jnp.concatenate([column[key_span, :]] * (block // 128), axis=1)
+                same = seg_col == seg_row
+                out = []
+                for side in range(2):
+                    peak, total, acc = state[side]
+                    head = 2 * pair + side
+                    scores = jnp.where(same, mxu(key_pair, queries[side], NT), MASKED)
+                    new_peak = jnp.maximum(peak, jnp.max(scores, axis=0, keepdims=True))
+                    weights = jnp.exp(scores - new_peak)
+                    fix = jnp.exp(peak - new_peak)
+                    total = total * fix + jnp.sum(weights, axis=0, keepdims=True)
+                    value = value_t[head * HEAD : (head + 1) * HEAD, key_span]
+                    acc = acc * fix + mxu(value, weights.astype(jnp.bfloat16))
+                    out.append((new_peak, total, acc))
+                return tuple(out)
+
+            zero = (
+                jnp.full((1, block), MASKED, jnp.float32),
+                jnp.zeros((1, block), jnp.float32),
+                jnp.zeros((HEAD, block), jnp.float32),
+            )
+            done = lax.fori_loop(begin, end, keys, (zero, zero))
+            for side in range(2):
+                peak, total, acc = done[side]
+                head = 2 * pair + side
+                mixed_t_ref[head * HEAD : (head + 1) * HEAD, span] = (acc / total).astype(jnp.bfloat16)
+                logs_ref[head : head + 1, span] = peak + jnp.log(total)
+        mixed = jnp.transpose(mixed_t_ref[:, span].astype(jnp.float32)).astype(jnp.bfloat16)
+        mixed_ref[span, :] = mixed
+        hidden = x_ref[span, :].astype(jnp.float32) + mxu(mixed, proj_low)
+        hidden_ref[span, :] = hidden
+        task = jnp.concatenate([as_column(task_ref[:, span])] * (D // 128), axis=1) > 0.5
+        gain = jnp.where(task, norm_ref[3:4, :], norm_ref[2:3, :])
+        bias = jnp.where(task, norm_ref[5:6, :], norm_ref[4:5, :])
+        unit, _ = unit_rows(hidden)
+        u_ref[span, :] = (unit * gain + bias).astype(jnp.bfloat16)
+        return carry
+
+    lax.fori_loop(0, blocks, rows, 0)
+
+
+def attend(marks, x, norm, qkv, proj, seg, task):
+    tokens = x.shape[0]
+    block = min(256, tokens)
+    vmem = pl.BlockSpec(memory_space=pltpu.VMEM)
+    low = jnp.bfloat16
+    return pl.pallas_call(
+        functools.partial(attend_kernel, block),
+        out_shape=(
+            jax.ShapeDtypeStruct((tokens, 3 * D), low),
+            jax.ShapeDtypeStruct((D, tokens), low),
+            jax.ShapeDtypeStruct((tokens, D), low),
+            jax.ShapeDtypeStruct((D, tokens), low),
+            jax.ShapeDtypeStruct((8, tokens), jnp.float32),
+            jax.ShapeDtypeStruct((tokens, D), jnp.float32),
+            jax.ShapeDtypeStruct((tokens, D), low),
+        ),
+        in_specs=[pl.BlockSpec(memory_space=pltpu.SMEM)] + [vmem] * 6,
+        out_specs=(vmem,) * 7,
+        scratch_shapes=[pltpu.VMEM((D, tokens), low), pltpu.VMEM((tokens, 128), jnp.float32)],
+        compiler_params=pltpu.CompilerParams(vmem_limit_bytes=48 << 20),
+        cost_estimate=pl.CostEstimate(flops=8 << 30, bytes_accessed=12 << 20, transcendentals=6 << 20),
+        name="attend",
+    )(marks, x, norm, qkv, proj, seg, task)
+
+
+def attend_back_kernel(
+    block, slots, marks_ref, x_ref, norm_ref, qkv_ref, proj_ref, seg_ref, task_ref, out_grad_ref,
+    joined_ref, key_t_ref, mixed_ref, mixed_t_ref, logs_ref, hidden_ref, *rest
+):
+    du_refs, rest = rest[:slots], rest[slots:]
+    patch_ref, weight_ref, norms_ref, grads, attn_in, key_grad, value_grad, column = rest
+    tokens = x_ref.shape[0]
+    blocks = tokens // block
+    qkv_low = qkv_ref[...].astype(jnp.bfloat16)
+    proj_low = proj_ref[...].astype(jnp.bfloat16)
+    column[...] = as_column(seg_ref[...])
+    key_grad[...] = jnp.zeros_like(key_grad)
+    value_grad[...] = jnp.zeros_like(value_grad)
+    norms_ref[...] = jnp.zeros_like(norms_ref)
+    weight_ref[...] = jnp.zeros_like(weight_ref)
+
+    def rows(index, carry):
+        start = pl.multiple_of(index * block, block)
+        span = pl.ds(start, block)
+        du = du_refs[0][span, :].astype(jnp.float32)
+        for ref in du_refs[1:]:
+            du = du + ref[span, :].astype(jnp.float32)
+        task = jnp.concatenate([as_column(task_ref[:, span])] * (D // 128), axis=1) > 0.5
+        gain = jnp.where(task, norm_ref[3:4, :], norm_ref[2:3, :])
+        unit, rate = unit_rows(hidden_ref[span, :])
+        first = jnp.where(task, 0.0, du)
+        second = jnp.where(task, du, 0.0)
+        norms_ref[2:3, :] += jnp.sum(first * unit, axis=0, keepdims=True)
+        norms_ref[3:4, :] += jnp.sum(second * unit, axis=0, keepdims=True)
+        norms_ref[4:5, :] += jnp.sum(first, axis=0, keepdims=True)
+        norms_ref[5:6, :] += jnp.sum(second, axis=0, keepdims=True)
+        hidden_grad = out_grad_ref[span, :].astype(jnp.float32) + unit_rows_back(unit, rate, du * gain)
+        patch_ref[span, :] = hidden_grad
+        grad_low = hidden_grad.astype(jnp.bfloat16)
+        weight_ref[D:, D:] += mxu(mixed_ref[span, :], grad_low, TN)
+        mixed_grad = mxu(grad_low, proj_low, NT).astype(jnp.bfloat16)
+        mixed_grad_t = mxu(proj_low, grad_low, NT).astype(jnp.bfloat16).astype(jnp.float32)
+        dots = mixed_grad_t * mixed_t_ref[:, span].astype(jnp.float32)
+        begin, end = key_range(marks_ref, index * block, block, blocks)
+        seg_row = seg_ref[:, span].astype(jnp.float32)
+        masks = head_masks(block)
+        query_grads = []
+        for pair in range(HEADS // 2):
+            lanes = slice(pair * 2 * HEAD, (pair + 1) * 2 * HEAD)
+            query = joined_ref[span, lanes] * jnp.bfloat16(HEAD ** (-0.5))
+            queries = [jnp.where(m, query, jnp.zeros_like(query)) for m in masks]
+            grad_pair = mixed_grad[:, lanes]
+            out_grads = [jnp.where(m, grad_pair, jnp.zeros_like(grad_pair)) for m in masks]
+            deltas = []
+            logs = []
+            for side in range(2):
+                head = 2 * pair + side
+                deltas.append(jnp.sum(dots[head * HEAD : (head + 1) * HEAD], axis=0, keepdims=True))
+                logs.append(logs_ref[head : head + 1, span])
+
+            def keys(at, state):
+                key_span = pl.ds(pl.multiple_of(at * block, block), block)
+                key_pair = joined_ref[key_span, D + pair * 2 * HEAD : D + (pair + 1) * 2 * HEAD]
+                value_pair = joined_ref[key_span, 2 * D + pair * 2 * HEAD : 2 * D + (pair + 1) * 2 * HEAD]
+                seg_col = jnp.concatenate([column[key_span, :]] * (block // 128), axis=1)
+                same = seg_col == seg_row
+                out = []
+                key_sum = key_grad[key_span, lanes]
+                value_sum = value_grad[key_span, lanes]
+                for side in range(2):
+                    head = 2 * pair + side
+                    scores = jnp.where(same, mxu(key_pair, queries[side], NT), MASKED)
+                    probs = jnp.exp(scores - logs[side])
+                    prob_grad = mxu(value_pair, out_grads[side], NT)
+                    score_grad = (probs * (prob_grad - deltas[side])).astype(jnp.bfloat16)
+                    value_sum = value_sum + mxu(probs.astype(jnp.bfloat16), out_grads[side])
+                    key_sum = key_sum + mxu(score_grad, queries[side])
+                    key_t = key_t_ref[head * HEAD : (head + 1) * HEAD, key_span]
+                    out.append(state[side] + mxu(key_t, score_grad))
+                key_grad[key_span, lanes] = key_sum
+                value_grad[key_span, lanes] = value_sum
+                return tuple(out)
+
+            zero = jnp.zeros((HEAD, block), jnp.float32)
+            query_grads.extend(lax.fori_loop(begin, end, keys, (zero, zero)))
+        query_grad_t = jnp.concatenate(query_grads, axis=0) * HEAD ** (-0.5)
+        grads[span, :D] = jnp.transpose(query_grad_t).astype(jnp.bfloat16)
+        return carry
+
+    lax.fori_loop(0, blocks, rows, 0)
+
+    def finish(index, carry):
+        span = pl.ds(pl.multiple_of(index * block, block), block)
+        grads[span, D : 2 * D] = key_grad[span, :].astype(jnp.bfloat16)
+        grads[span, 2 * D :] = value_grad[span, :].astype(jnp.bfloat16)
+        unit, rate = unit_rows(x_ref[span, :].astype(jnp.float32))
+        attn_in[span, :] = (unit * norm_ref[0:1, :] + norm_ref[1:2, :]).astype(jnp.bfloat16)
+        joined_grad = grads[span, :]
+        in_grad = mxu(joined_grad, qkv_low, NT)
+        norms_ref[0:1, :] += jnp.sum(in_grad * unit, axis=0, keepdims=True)
+        norms_ref[1:2, :] += jnp.sum(in_grad, axis=0, keepdims=True)
+        patch_ref[span, :] += unit_rows_back(unit, rate, in_grad * norm_ref[0:1, :])
+        return carry
+
+    lax.fori_loop(0, blocks, finish, 0)
+    weight_ref[:D, :] = mxu(attn_in[...], grads[:, : 2 * D], TN)
+    weight_ref[D:, :D] = mxu(attn_in[...], grads[:, 2 * D :], TN)
+
+
+def attend_back(marks, x, norm, qkv, proj, seg, task, out_grad, saved, du_parts):
+    tokens = x.shape[0]
+    block = min(256, tokens)
+    vmem = pl.BlockSpec(memory_space=pltpu.VMEM)
+    operands = [marks, x, norm, qkv, proj, seg, task, out_grad, *saved, *du_parts]
+    return pl.pallas_call(
+        functools.partial(attend_back_kernel, block, len(du_parts)),
+        out_shape=(
+            jax.ShapeDtypeStruct((tokens, D), jnp.float32),
+            jax.ShapeDtypeStruct((2 * D, 2 * D), jnp.float32),
+            jax.ShapeDtypeStruct((8, D), jnp.float32),
+        ),
+        in_specs=[pl.BlockSpec(memory_space=pltpu.SMEM)] + [vmem] * (len(operands) - 1),
+        out_specs=(vmem,) * 3,
+        scratch_shapes=[
+            pltpu.VMEM((tokens, 3 * D), jnp.bfloat16),
+            pltpu.VMEM((tokens, D), jnp.bfloat16),
+            pltpu.VMEM((tokens, D), jnp.float32),
+            pltpu.VMEM((tokens, D), jnp.float32),
+            pltpu.VMEM((tokens, 128), jnp.float32),
+        ],
+        compiler_params=pltpu.CompilerParams(vmem_limit_bytes=52 << 20),
+        cost_estimate=pl.CostEstimate(flops=24 << 30, bytes_accessed=24 << 20, transcendentals=6 << 20),
+        name="attend_back",
+    )(*operands)
+
+
 def to_peers(arrays, groups):
     return [arrays[0]] + [
         lax.ppermute(arrays[k], "expert", [(i, i ^ k) for i in range(groups)]) for k in range(1, groups)
@@ -370,7 +561,6 @@
     tok_count = patches.shape[0]
     tokens_all = tok_count * groups * lax.axis_size("hidden")
     local_count = EXPERTS // groups
-    block_rows = min(512, tok_count)
     own_units = expert_inner.shape[0]
     half = local_count // 2 * 2 * D
     both = jnp.stack([expert_inner, expert_outer], axis=2).astype(jnp.bfloat16)
@@ -388,31 +578,10 @@
         (expert_ids[:, :, None] == jnp.arange(EXPERTS, dtype=jnp.int32)).astype(jnp.float32), axis=(0, 1)
     )
     counts = jnp.minimum(named, float(CAP))
-    inputs = patches.astype(jnp.float32)
-    seg_marks = segments[0]
-    normed_one, first_back = jax.vjp(first_norm, inputs, norm_params[0], norm_params[1])
-    attn_in = normed_one.astype(jnp.bfloat16)
-    qkv_low = attn_qkv.astype(jnp.bfloat16)
-    proj_low = attn_proj.astype(jnp.bfloat16)
-    joined = jnp.dot(attn_in, qkv_low, preferred_element_type=jnp.float32).astype(jnp.bfloat16)
-    joined = joined.reshape(tok_count, 3, HEADS, HEAD)
-    query_heads = joined[:, 0]
-    key_heads = joined[:, 1]
-    value_heads = joined[:, 2]
-    mixed, log_sums = attend_forward(query_heads, key_heads, value_heads, seg_marks, block_rows)
-    mixed = mixed.reshape(tok_count, D)
-    hidden_one = inputs + jnp.dot(mixed, proj_low, preferred_element_type=jnp.float32)
-    task_hot = (task_ids[:, None] == jnp.arange(TASKS, dtype=jnp.int32)[None, :]).astype(
-        jnp.float32
-    )
-
-    def second_norm(values, table):
-        gain_rows = jnp.dot(task_hot, table[:TASKS], precision=lax.Precision.HIGHEST)
-        bias_rows = jnp.dot(task_hot, table[TASKS:], precision=lax.Precision.HIGHEST)
-        return layer_norm(values) * gain_rows + bias_rows
-
-    normed_two, second_back = jax.vjp(second_norm, hidden_one, norm_params[2:])
-    moe_in = normed_two.astype(jnp.bfloat16)
+    marks = segments[0]
+    task_row = task_ids[None]
+    *saved, moe_in = attend(marks, patches, norm_params, attn_qkv, attn_proj, segments, task_row)
+    hidden_one = saved[-1]
     u_all = to_peers([moe_in] * groups, groups)
     sums, grads_first = moe(rows, gate_rows, cols, u_all, g_all, weights[0], 0, None, False)
     *parts, grads_second = moe(
@@ -420,10 +589,8 @@
     )
     du_parts = to_peers(parts[:groups], groups)
     y_parts = to_peers(parts[groups:], groups)
-    moe_grad = sum(p.astype(jnp.float32) for p in du_parts)
     moe_sum = sum(p.astype(jnp.float32) for p in y_parts)
     block_out = (hidden_one + moe_sum).astype(jnp.bfloat16)
-    out_grad = cotangent.astype(jnp.float32)
     owned = [
         lax.psum_scatter(g, "hidden", scatter_dimension=0, tiled=True)
         for g in (grads_first, grads_second)
@@ -431,34 +598,14 @@
     owned = jnp.concatenate(owned, axis=1).astype(jnp.float32)
     owned = owned.reshape(own_units, local_count, 2, D)
     inner_grad, outer_grad = owned[:, :, 0], owned[:, :, 1]
-    hidden_grad, table_grad = second_back(moe_grad)
-    hidden_grad = hidden_grad + out_grad
-    attn_grad_low = hidden_grad.astype(jnp.bfloat16)
-    proj_grad = jnp.einsum("td,te->de", mixed, attn_grad_low, preferred_element_type=jnp.float32)
-    mixed_grad = jnp.einsum(
-        "te,de->td", attn_grad_low, proj_low, preferred_element_type=jnp.float32
-    )
-    mixed_grad = mixed_grad.astype(jnp.bfloat16).reshape(tok_count, HEADS, HEAD)
-    query_grad, key_grad, value_grad = attend_backward(
-        query_heads, key_heads, value_heads, seg_marks, mixed_grad, log_sums, block_rows
-    )
-    joined_grad = (
-        jnp.stack([query_grad, key_grad, value_grad], axis=1)
-        .reshape(tok_count, 3 * D)
-        .astype(jnp.bfloat16)
-    )
-    qkv_grad = jnp.einsum("td,te->de", attn_in, joined_grad, preferred_element_type=jnp.float32)
-    attn_in_grad = jnp.einsum("te,de->td", joined_grad, qkv_low, preferred_element_type=jnp.float32)
-    input_first, gain_grad, offset_grad = first_back(attn_in_grad)
-    patch_grad = hidden_grad + input_first
-    norm_grad = jnp.concatenate([gain_grad[None], offset_grad[None], table_grad], axis=0)
-    big = jnp.concatenate([qkv_grad, proj_grad], axis=1)
-    pad_rows = -big.shape[0] % 512
-    big = jnp.concatenate([big, jnp.zeros((pad_rows, big.shape[1]), jnp.float32)], axis=0)
-    big_sum = butterfly_sum(big, jnp.bfloat16)[:D]
-    qkv_sum, proj_sum = big_sum[:, : 3 * D], big_sum[:, 3 * D :]
+    patch_grad, big, norm_grad = attend_back(
+        marks, patches, norm_params, attn_qkv, attn_proj, segments, task_row, cotangent, saved, du_parts
+    )
+    big_sum = butterfly_sum(big, jnp.bfloat16)
+    qkv_sum = jnp.concatenate([big_sum[:D], big_sum[D:, :D]], axis=1)
+    proj_sum = big_sum[D:, D:]
     count_row = jnp.pad(counts, (0, D - EXPERTS))[None]
-    small = jnp.concatenate([norm_grad, count_row, jnp.zeros((1, D), jnp.float32)], axis=0)
+    small = jnp.concatenate([norm_grad[:6], count_row, jnp.zeros((1, D), jnp.float32)], axis=0)
     small_sum = butterfly_sum(small, jnp.float32)
     norm_sum, count_sum = small_sum[:6], small_sum[6, :EXPERTS]
     expert_load = count_sum * (EXPERTS / (tokens_all * TOP))

time: 469 us -> 443 us (0.945)
  Pallas kernels: 110 us -> 182 us
  matrix products: 63.3 us -> 0 us
  other arithmetic: 61.9 us -> 21 us
  waiting for transfers between devices: 149 us -> 166 us
  local copies, waits for them, and re-layouts: 25.4 us -> 18.6 us
    pallas_call x0 -> x2, Pallas kernels: none -> 72.6 us  [the longest x1 38.3 us: attend_back(): pl.pallas_call(functools.partial(attend_back_kernel, block, len(du_parts)...]
    dot_general x22 -> x0, matrix products: 63.3 us -> none  [the longest x2 14.8 us: attend_backward(): jnp.einsum('qhd,khd->hqk', grad_rows, value_heads, preferred_element_type...]
    convert_element_type x3 -> x1, other arithmetic: 20.6 us -> 1.34 us  [body(): block_out = (hidden_one + moe_sum).astype(jnp.bfloat16)]
    ppermute x5, waiting for transfers between devices: 10.8 us -> 25 us  [butterfly_sum(): lax.ppermute(value.astype(wire), axis, [(i, i ^ bit) for i in range(size)])]
    reduce_sum x8 -> x0, other arithmetic: 13.7 us -> none  [the longest x2 5.62 us: attend_forward(): row_total = jnp.sum(row_exp, axis=-1, keepdims=True)]
    ppermute x5, waiting for transfers between devices: 12.7 us -> 22.3 us  [butterfly_sum(): got = lax.ppermute(value, axis, [(i, i ^ bit) for i in range(size)])]
    ppermute x15, waiting for transfers between devices: 103 us -> 93.7 us  [to_peers(): lax.ppermute(arrays[k], 'expert', [(i, i ^ k) for i in range(groups)])]
    unnamed x178 -> x84, local copies, waits for them, and re-layouts: 12.1 us -> 7.83 us
  transfers between devices with their start and end apart: 34 -> 34, of which waited for: 20 -> 21; matrix products, arithmetic and copies ran while one was open for 27% -> 3% of each run, Pallas kernels for 12% -> 29%
where the time goes in v3:
time: 443 us; the launch traced here: 437 us
  Pallas kernels  182 us (41%)
  waiting for transfers between devices  166 us (37%)
  starting transfers between devices  34.5 us (8%)
  other arithmetic  21 us (5%)
  local copies, waits for them, and re-layouts  18.6 us (4%)
  between operations  14.6 us (3%)
    pallas_call x2, Pallas kernels, moe(): pl.pallas_call(functools.partial(moe_kernel, offset, count, start is not...  107 us
    ppermute x15, waiting for transfers between devices, to_peers(): lax.ppermute(arrays[k], 'expert', [(i, i ^ k) for i in range(groups)])  93.7 us
    pallas_call x1, Pallas kernels, attend_back(): pl.pallas_call(functools.partial(attend_back_kernel, block, len(du_parts)...  38.3 us
    pallas_call x1, Pallas kernels, attend(): pl.pallas_call(functools.partial(attend_kernel, block), out_shape=(jax.Sh...  34.3 us
    ppermute x5, waiting for transfers between devices, butterfly_sum(): lax.ppermute(value.astype(wire), axis, [(i, i ^ bit) for i in range(size)])  25 us
    ppermute x5, waiting for transfers between devices, butterfly_sum(): got = lax.ppermute(send, axis, [(i, i ^ bit) for i in range(size)])  23.8 us
    ppermute x5, waiting for transfers between devices, butterfly_sum(): got = lax.ppermute(value, axis, [(i, i ^ bit) for i in range(size)])  22.3 us
    ppermute x15, starting transfers between devices, to_peers(): lax.ppermute(arrays[k], 'expert', [(i, i ^ k) for i in range(groups)])  17.3 us
  transfers between devices with their start and end apart: 34, of which 21 were waited for; matrix products, arithmetic and copies ran while one was open for 3% of the time, Pallas kernels for 29%

profile of v3, /device:TPU:0, one launch (start us, length us, event | category | flops | bytes accessed | tf_op | source)
XLA Modules:
  0.0 436.5 jit_solution(13147685712374032066)
XLA Ops:
  7.2 2.0 convert_bitcast_fusion
  9.3 0.8 pad_maximum_fusion.1
  10.1 1.8 copy.43
  11.9 0.9 convert_element_type.69
  12.9 1.1 fusion.5
  15.1 34.3 %attend.1 = (bf16[1024,1152]{1,0:T(8,128)(2,1)}, bf16[384,1024]{1,0:T(8,128)(2,1)S(1)}, bf16[1024,384]{1,0:T(8,128)(2,1)S(1)}, bf16[384,1024]{1,0:T(8,128)(2,1)S...) custom-call(s32[1024]{0:T(1024)S(1)} %bitcast.37, ...), custom_call_target="tpu_custom_call" | custom-call | flops 8589934592 | bytes 12582912 | tf_op jit(solution)/shard_map/attend/pallas_call | solution.py:338
  49.4 1.1 copy-done
  50.5 0.9 copy-done.13
  51.4 0.9 copy-done.14
  52.3 0.9 copy-done.15
  53.3 2.1 collective-permute-start
  55.3 3.0 collective-permute-start.1
  58.3 1.5 collective-permute-start.4
  59.9 14.3 %collective-permute-done = f32[8,1024]{1,0:T(8,128)S(1)} collective-permute-done((f32[8,1024]{1,0:T(8,128)S(1)}, f32[8,1024]{1,0:T(8,128)S(1)}, u32[]{:S(2)}, u32[]{:S(2)}) %collective-permute-start) | collective-permute-done | bytes 32800 | tf_op jit(solution)/shard_map/ppermute | solution.py:491
  74.4 3.3 collective-permute-start.7
  78.6 2.2 route.1
  80.8 12.1 %collective-permute-done.4.rest_2_ = bf16[1024,384]{1,0:T(8,128)(2,1)} collective-permute-done((bf16[1024,384]{1,0:T(8,128)(2,1)S(1)}, bf16[1024,384]{1,0:T(8,128)(2,1)}, u32[]{:S(2)}, u32[]{:S(2)}) %collective-permute-start.4) | collective-permute-done | bytes 786464 | tf_op jit(solution)/shard_map/ppermute | solution.py:491
  92.9 2.7 collective-permute-done.5.rest_3_
  95.7 14.0 %collective-permute-done.6.rest_5_ = bf16[1024,384]{1,0:T(8,128)(2,1)} collective-permute-done((bf16[1024,384]{1,0:T(8,128)(2,1)S(1)}, bf16[1024,384]{1,0:T(8,128)(2,1)}, u32[]{:S(2)}, u32[]{:S(2)}) %collective-permute-start.6) | collective-permute-done | bytes 786464 | tf_op jit(solution)/shard_map/ppermute | solution.py:491
  109.7 15.9 %collective-permute-done.7.rest_6_ = bf16[1024,384]{1,0:T(8,128)(2,1)} collective-permute-done((bf16[1024,384]{1,0:T(8,128)(2,1)S(1)}, bf16[1024,384]{1,0:T(8,128)(2,1)}, u32[]{:S(2)}, u32[]{:S(2)}) %collective-permute-start.7) | collective-permute-done | bytes 786464 | tf_op jit(solution)/shard_map/ppermute | solution.py:491
  125.6 2.2 collective-permute-done.8.rest_7_
  127.8 52.7 %moe.2 = (f32[4,1024,768]{2,1,0:T(8,128)}, bf16[1536,1536]{1,0:T(8,128)(2,1)}) custom-call(s32[4,4,1024]{2,1,0:T(4,128)} %get-tuple-element.43.rows_ref, f32[4,4,1024]{2,1,0:T(4,128)} %get-tuple-element.44.gate_rows_ref, s32[1024,128]{1,0:T(8,128)} %get-tuple-element.45.cols_ref, bf16[1024,384]{1,0:T(8,128)(2,1)} %copy-done.8, bf16[1024,384]{1,0:T(8,128)(2,1)} %copy-done.39, ...), custom_call_target="tpu_custom_call" | custom-call | flops 26172456960 | bytes 41943040 | tf_op jit(solution)/shard_map/moe/pallas_call | solution.py:204
  180.6 54.7 %moe.3 = (bf16[1024,384]{1,0:T(8,128)(2,1)}, bf16[1024,384]{1,0:T(8,128)(2,1)}, bf16[1024,384]{1,0:T(8,128)(2,1)}, bf16[1024,384]{1,0:T(8,128)(2,1)}, bf16[1024,...) custom-call(s32[4,4,1024]{2,1,0:T(4,128)} %get-tuple-element.43.rows, ...), custom_call_target="tpu_custom_call" | custom-call | flops 26172456960 | bytes 41943040 | tf_op jit(solution)/shard_map/moe/pallas_call | solution.py:204
  235.4 1.1 collective-permute-start.12
  236.5 0.8 collective-permute-start.13
  237.3 1.7 collective-permute-start.14
  239.0 17.2 %collective-permute-done.12.rest_1_ = bf16[1024,384]{1,0:T(8,128)(2,1)} collective-permute-done((bf16[1024,384]{1,0:T(8,128)(2,1)}, bf16[1024,384]{1,0:T(8,128)(2,1)}, u32[]{:S(2)}, u32[]{:S(2)}) %collective-permute-start.12) | collective-permute-done | bytes 786464 | tf_op jit(solution)/shard_map/ppermute | solution.py:491
  256.2 15.2 %collective-permute-done.13.rest_2_ = bf16[1024,384]{1,0:T(8,128)(2,1)} collective-permute-done((bf16[1024,384]{1,0:T(8,128)(2,1)S(1)}, bf16[1024,384]{1,0:T(8,128)(2,1)}, u32[]{:S(2)}, u32[]{:S(2)}) %collective-permute-start.13) | collective-permute-done | bytes 786464 | tf_op jit(solution)/shard_map/ppermute | solution.py:491
  271.4 38.3 %attend_back.1 = (f32[1024,384]{1,0:T(8,128)}, f32[768,768]{1,0:T(8,128)}, f32[8,384]{1,0:T(8,128)S(1)}) custom-call(s32[1024]{0:T(1024)S(1)} %bitcast.38, bf16[1024,384]{1,0:T(8,128)(2,1)S(1)} %copy-done.7, f32[6,384]{1,0:T(8,128)S(1)} %copy-done.5, f32[384,1152]{1,0:T(8,128)} %qkv_ref.3, f32[384,384]{1,0:T(8,128)S(1)} %copy-done.3, ...), custom_call_target="tpu_custom_call" | custom-call | flops 25769803776 | bytes 25165824 | tf_op jit(solution)/shard_map/attend_back/pallas_call | solution.py:467
  309.7 1.7 select_convert_fusion
  311.6 2.0 collective-permute-done.20
  313.6 1.9 convert_add_fusion
  315.6 9.0 %collective-permute-done.21 = bf16[192,768]{1,0:T(8,128)(2,1)S(1)} collective-permute-done((bf16[192,768]{1,0:T(8,128)(2,1)S(1)}, bf16[192,768]{1,0:T(8,128)(2,1)S(1)}, u32[]{:S(2)}, u32[]{:S(2)}) %collective-permute-start.21) | collective-permute-done | bytes 294944 | tf_op jit(solution)/shard_map/ppermute | solution.py:515
  324.8 0.9 collective-permute-start.22
  325.7 4.3 collective-permute-done.22
  330.1 1.6 collective-permute-start.23
  331.6 5.2 %collective-permute-done.23 = bf16[48,768]{1,0:T(8,128)(2,1)S(1)} collective-permute-done((bf16[48,768]{1,0:T(8,128)(2,1)S(1)}, bf16[48,768]{1,0:T(8,128)(2,1)S(1)}, u32[]{:S(2)}, u32[]{:S(2)}) %collective-permute-start.23) | collective-permute-done | bytes 73760 | tf_op jit(solution)/shard_map/ppermute | solution.py:515
  336.8 3.3 collective-permute-start.24
  340.2 3.3 collective-permute-done.24
  343.5 2.5 collective-permute-start.25
  346.0 2.9 collective-permute-done.25
  349.0 1.8 collective-permute-start.26
  350.9 2.5 collective-permute-done.26
  353.4 1.5 collective-permute-start.27
  355.6 2.1 collective-permute-start.11
  357.7 0.9 collective-permute-start.9
  358.6 17.0 %collective-permute-done.27 = bf16[96,768]{1,0:T(8,128)(2,1)S(1)} collective-permute-done((bf16[96,768]{1,0:T(8,128)(2,1)S(1)}, bf16[96,768]{1,0:T(8,128)(2,1)S(1)}, u32[]{:S(2)}, u32[]{:S(2)}) %collective-permute-start.27) | collective-permute-done | bytes 147488 | tf_op jit(solution)/shard_map/ppermute | solution.py:523
  376.4 1.2 collective-permute-done.15
  377.6 1.4 collective-permute-start.16
  379.0 16.6 %collective-permute-done.16 = f32[8,384]{1,0:T(8,128)S(1)} collective-permute-done((f32[8,384]{1,0:T(8,128)S(1)}, f32[8,384]{1,0:T(8,128)S(1)}, u32[]{:S(2)}, u32[]{:S(2)}) %collective-permute-start.16) | collective-permute-done | bytes 12320 | tf_op jit(solution)/shard_map/ppermute | solution.py:518
  395.6 1.4 collective-permute-start.17
  397.0 2.3 collective-permute-done.17
  399.9 3.1 collective-permute-done.18
  403.0 1.2 collective-permute-start.19
  404.6 1.3 add_convert_fusion
  406.0 1.8 collective-permute-done.19
  409.5 1.3 copy-done.18
  411.5 1.4 multiply_add_fusion.6
  412.8 0.9 slice-done
  414.3 2.8 multiply_add_fusion
  417.2 1.9 concatenate.41
  419.6 2.3 concatenate.40
  422.4 1.1 maximum_convert_fusion.1
  424.4 5.4 %multiply_add_fusion.2 = (f32[192,4,384]{2,1,0:T(4,128)}, f32[192,4,384]{2,1,0:T(4,128)}, f32[192,4,384]{2,1,0:T(4,128)}, f32[192,4,384]{2,1,0:T(4,128)}, f32[192,4,384]{2,1,0:T(4,128)}, /*index=5*/f32[192,4,384]{2,1,0:T(4,128)}) fusion(f32[192,4,384]{2,1,0:T(4,128)S(1)} %copy-done.24, f32[192,4,384]{2,1,0:T(4,128)S(1)} %copy-done.19, ...), kind=kLoop, calls=%fused_computation.10 | loop fusion | flops 5308416 | bytes 16515072 | tf_op jit(solution)/shard_map/add | solution.py:533
  (151 shorter events, 10.3 us)
Async XLA Ops:
  7.2 120.6 %all-gather.5.cloned.1.call-start = ((), (), s32[]{:S(2)}) async-start(), calls=%async_computation.3 | async-start | bytes 5308416 | tf_op jit(solution)/shard_map/all_gather | solution.py:569
  12.8 1.9 copy-start.6
  14.0 166.6 %all-gather.3.cloned.1.call-start = ((), (), s32[]{:S(2)}) async-start(), calls=%async_computation.2 | async-start | bytes 5308416 | tf_op jit(solution)/shard_map/all_gather | solution.py:570
  14.7 402.4 %reduce-scatter.5.cloned.1.call-start = ((), (), s32[]{:S(2)}) async-start(), calls=%async_computation.5 | async-start | bytes 5308416 | tf_op jit(solution)/shard_map/reduce_scatter | solution.py:595
  15.1 38.1 %copy-start.30 = (s32[1024,4]{0,1:T(4,128)S(1)}, s32[1024,4]{0,1:T(4,128)}, u32[]{:S(2)}) copy-start(s32[1024,4]{0,1:T(4,128)} %param.23) | copy-start | bytes 49156
  15.1 38.2 %copy-start.32 = (f32[1024,4]{0,1:T(4,128)S(1)}, f32[1024,4]{0,1:T(4,128)}, u32[]{:S(2)}) copy-start(f32[1024,4]{0,1:T(4,128)} %param.24) | copy-start | bytes 49156
  15.1 59.1 %copy-start.35 = (bf16[1024,384]{1,0:T(8,128)(2,1)S(1)}, bf16[1024,384]{1,0:T(8,128)(2,1)}, u32[]{:S(2)}) copy-start(bf16[1024,384]{1,0:T(8,128)(2,1)} %out_grad_ref.1) | copy-start | bytes 2359300
  53.2 21.0 %copy-start.8 = (bf16[1024,384]{1,0:T(8,128)(2,1)}, bf16[1024,384]{1,0:T(8,128)(2,1)S(1)}, u32[]{:S(2)}) copy-start(bf16[1024,384]{1,0:T(8,128)(2,1)S(1)} %get-tuple-element.46.rest_0_) | copy-start | bytes 2359300
  53.2 24.5 %copy-start.16 = (f32[8,1024]{1,0:T(8,128)}, f32[8,1024]{1,0:T(8,128)S(1)}, u32[]{:S(2)}) copy-start(f32[8,1024]{1,0:T(8,128)S(1)} %get-tuple-element.56.logs_ref) | copy-start | bytes 98308
  53.2 24.5 %collective-permute-start.3 = (bf16[1024,384]{1,0:T(8,128)(2,1)S(1)}, bf16[1024,384]{1,0:T(8,128)(2,1)S(1)}, u32[]{:S(2)}, u32[]{:S(2)}) collective-permute-start(bf16[1024,384]{1,0:T(8,128)(2,1)S(1)} %get-tuple-element.46.rest_0_), channel_id=1, source_target_pairs={{0,8},{8,0},{16,24},{24,16},{1,9},{9,1},{17,25},{25,17},{2,10},{10... | collective-permute-start | bytes 2359304 | tf_op jit(solution)/shard_map/ppermute | solution.py:491
  53.3 21.0 %collective-permute-start = (f32[8,1024]{1,0:T(8,128)S(1)}, f32[8,1024]{1,0:T(8,128)S(1)}, u32[]{:S(2)}, u32[]{:S(2)}) collective-permute-start(f32[8,1024]{1,0:T(8,128)S(1)} %get-tuple-element.101), channel_id=1, source_target_pairs={{0,8},{8,0},{16,24},{24,16},{1,9},{9,1},{17,25},{25,17},{2,10},{10... | collective-permute-start | bytes 98312 | tf_op jit(solution)/shard_map/ppermute | solution.py:491
  55.3 18.9 %collective-permute-start.1 = (f32[8,1024]{1,0:T(8,128)S(1)}, f32[8,1024]{1,0:T(8,128)S(1)}, u32[]{:S(2)}, u32[]{:S(2)}) collective-permute-start(f32[8,1024]{1,0:T(8,128)S(1)} %get-tuple-element.101), channel_id=1, source_target_pairs={{0,16},{8,24},{16,0},{24,8},{1,17},{9,25},{17,1},{25,9},{2,18},{10... | collective-permute-start | bytes 98312 | tf_op jit(solution)/shard_map/ppermute | solution.py:491
  58.3 16.1 %collective-permute-start.2 = (f32[8,1024]{1,0:T(8,128)S(1)}, f32[8,1024]{1,0:T(8,128)S(1)}, u32[]{:S(2)}, u32[]{:S(2)}) collective-permute-start(f32[8,1024]{1,0:T(8,128)S(1)} %get-tuple-element.101), channel_id=1, source_target_pairs={{0,24},{8,16},{16,8},{24,0},{1,25},{9,17},{17,9},{25,1},{2,26},{10... | collective-permute-start | bytes 98312 | tf_op jit(solution)/shard_map/ppermute | solution.py:491
  58.3 34.6 %collective-permute-start.4 = (bf16[1024,384]{1,0:T(8,128)(2,1)S(1)}, bf16[1024,384]{1,0:T(8,128)(2,1)}, u32[]{:S(2)}, u32[]{:S(2)}) collective-permute-start(bf16[1024,384]{1,0:T(8,128)(2,1)S(1)} %get-tuple-element.46.rest_0_), channel_id=1, source_target_pairs={{0,16},{8,24},{16,0},{24,8},{1,17},{9,25},{17,1},{25,9},{2,18},{10... | collective-permute-start | bytes 2359304 | tf_op jit(solution)/shard_map/ppermute | solution.py:491
  74.2 21.5 %collective-permute-start.5 = (bf16[1024,384]{1,0:T(8,128)(2,1)S(1)}, bf16[1024,384]{1,0:T(8,128)(2,1)}, u32[]{:S(2)}, u32[]{:S(2)}) collective-permute-start(bf16[1024,384]{1,0:T(8,128)(2,1)S(1)} %get-tuple-element.46.rest_0_), channel_id=1, source_target_pairs={{0,24},{8,16},{16,8},{24,0},{1,25},{9,17},{17,9},{25,1},{2,26},{10... | collective-permute-start | bytes 2359304 | tf_op jit(solution)/shard_map/ppermute | solution.py:491
  74.2 35.4 %collective-permute-start.6 = (bf16[1024,384]{1,0:T(8,128)(2,1)S(1)}, bf16[1024,384]{1,0:T(8,128)(2,1)}, u32[]{:S(2)}, u32[]{:S(2)}) collective-permute-start(bf16[1024,384]{1,0:T(8,128)(2,1)S(1)} %copy-done.35), channel_id=1, source_target_pairs={{0,8},{8,0},{16,24},{24,16},{1,9},{9,1},{17,25},{25,17},{2,10},{10... | collective-permute-start | bytes 2359304 | tf_op jit(solution)/shard_map/ppermute | solution.py:491
  74.4 51.2 %collective-permute-start.7 = (bf16[1024,384]{1,0:T(8,128)(2,1)S(1)}, bf16[1024,384]{1,0:T(8,128)(2,1)}, u32[]{:S(2)}, u32[]{:S(2)}) collective-permute-start(bf16[1024,384]{1,0:T(8,128)(2,1)S(1)} %copy-done.35), channel_id=1, source_target_pairs={{0,16},{8,24},{16,0},{24,8},{1,17},{9,25},{17,1},{25,9},{2,18},{10... | collective-permute-start | bytes 2359304 | tf_op jit(solution)/shard_map/ppermute | solution.py:491
  77.7 50.1 %copy-start.39 = (bf16[1024,384]{1,0:T(8,128)(2,1)}, bf16[1024,384]{1,0:T(8,128)(2,1)S(1)}, u32[]{:S(2)}) copy-start(bf16[1024,384]{1,0:T(8,128)(2,1)S(1)} %collective-permute-done.3.rest_1_) | copy-start | bytes 2359300
  77.7 50.1 %collective-permute-start.8 = (bf16[1024,384]{1,0:T(8,128)(2,1)S(1)}, bf16[1024,384]{1,0:T(8,128)(2,1)}, u32[]{:S(2)}, u32[]{:S(2)}) collective-permute-start(bf16[1024,384]{1,0:T(8,128)(2,1)S(1)} %copy-done.35), channel_id=1, source_target_pairs={{0,24},{8,16},{16,8},{24,0},{1,25},{9,17},{17,9},{25,1},{2,26},{10... | collective-permute-start | bytes 2359304 | tf_op jit(solution)/shard_map/ppermute | solution.py:491
  235.3 2.0 copy-start.40
  235.3 184.2 %reduce-scatter.3.cloned.1.call-start = ((), (), s32[]{:S(2)}) async-start(), calls=%async_computation.4 | async-start | bytes 5308416 | tf_op jit(solution)/shard_map/reduce_scatter | solution.py:595
  235.4 20.8 %collective-permute-start.12 = (bf16[1024,384]{1,0:T(8,128)(2,1)}, bf16[1024,384]{1,0:T(8,128)(2,1)}, u32[]{:S(2)}, u32[]{:S(2)}) collective-permute-start(bf16[1024,384]{1,0:T(8,128)(2,1)} %get-tuple-element.58), channel_id=1, source_target_pairs={{0,8},{8,0},{16,24},{24,16},{1,9},{9,1},{17,25},{25,17},{2,10},{10... | collective-permute-start | bytes 2359304 | tf_op jit(solution)/shard_map/ppermute | solution.py:491
  236.5 34.9 %collective-permute-start.13 = (bf16[1024,384]{1,0:T(8,128)(2,1)S(1)}, bf16[1024,384]{1,0:T(8,128)(2,1)}, u32[]{:S(2)}, u32[]{:S(2)}) collective-permute-start(bf16[1024,384]{1,0:T(8,128)(2,1)S(1)} %copy-done.41), channel_id=1, source_target_pairs={{0,16},{8,24},{16,0},{24,8},{1,17},{9,25},{17,1},{25,9},{2,18},{10... | collective-permute-start | bytes 2359304 | tf_op jit(solution)/shard_map/ppermute | solution.py:491
  237.3 34.1 %collective-permute-start.14 = (bf16[1024,384]{1,0:T(8,128)(2,1)S(1)}, bf16[1024,384]{1,0:T(8,128)(2,1)}, u32[]{:S(2)}, u32[]{:S(2)}) collective-permute-start(bf16[1024,384]{1,0:T(8,128)(2,1)S(1)} %copy-done.40), channel_id=1, source_target_pairs={{0,24},{8,16},{16,8},{24,0},{1,25},{9,17},{17,9},{25,1},{2,26},{10... | collective-permute-start | bytes 2359304 | tf_op jit(solution)/shard_map/ppermute | solution.py:491
  239.0 32.4 %copy-start.3 = (f32[384,384]{1,0:T(8,128)S(1)}, f32[384,384]{1,0:T(8,128)}, u32[]{:S(2)}) copy-start(f32[384,384]{1,0:T(8,128)} %proj_ref.3) | copy-start | bytes 1769476
  239.0 32.4 %copy-start.5 = (f32[6,384]{1,0:T(8,128)S(1)}, f32[6,384]{1,0:T(8,128)}, u32[]{:S(2)}) copy-start(f32[6,384]{1,0:T(8,128)} %norm_ref.3) | copy-start | bytes 27652
  239.0 32.4 %copy-start.7 = (bf16[1024,384]{1,0:T(8,128)(2,1)S(1)}, bf16[1024,384]{1,0:T(8,128)(2,1)}, u32[]{:S(2)}) copy-start(bf16[1024,384]{1,0:T(8,128)(2,1)} %x_ref.3) | copy-start | bytes 2359300
  239.0 32.4 %copy-start.10 = (s32[1,1024]{1,0:T(1,128)S(1)}, s32[1,1024]{1,0:T(1,128)}, u32[]{:S(2)}) copy-start(s32[1,1024]{1,0:T(1,128)} %seg_ref.3) | copy-start | bytes 12292
  239.0 32.4 %copy-start.12 = (s32[1024]{0:T(1024)S(1)}, s32[1024]{0:T(1024)}, u32[]{:S(2)}) copy-start(s32[1024]{0:T(1024)} %param.25) | copy-start | bytes 12292
  239.0 32.4 %copy-start.17 = (f32[8,1024]{1,0:T(8,128)S(1)}, f32[8,1024]{1,0:T(8,128)}, u32[]{:S(2)}) copy-start(f32[8,1024]{1,0:T(8,128)} %copy-done.16) | copy-start | bytes 98308
  311.5 2.1 collective-permute-start.20
  315.5 9.1 %collective-permute-start.21 = (bf16[192,768]{1,0:T(8,128)(2,1)S(1)}, bf16[192,768]{1,0:T(8,128)(2,1)S(1)}, u32[]{:S(2)}, u32[]{:S(2)}) collective-permute-start(bf16[192,768]{1,0:T(8,128)(2,1)S(1)} %select_convert_fusion.1), channel_id=1, source_target_pairs={{0,8},{8,0},{16,24},{24,16},{1,9},{9,1},{17,25},{25,17},{2,10},{10... | collective-permute-start | bytes 884744 | tf_op jit(solution)/shard_map/ppermute | solution.py:515
  324.8 5.2 %collective-permute-start.22 = (bf16[96,768]{1,0:T(8,128)(2,1)S(1)}, bf16[96,768]{1,0:T(8,128)(2,1)S(1)}, u32[]{:S(2)}, u32[]{:S(2)}) collective-permute-start(bf16[96,768]{1,0:T(8,128)(2,1)S(1)} %select_convert_fusion.2), channel_id=1, source_target_pairs={{0,16},{8,24},{16,0},{24,8},{1,17},{9,25},{17,1},{25,9},{2,18},{10... | collective-permute-start | bytes 442376 | tf_op jit(solution)/shard_map/ppermute | solution.py:515
  325.7 25.1 %copy-start.31 = (s32[1024,4]{0,1:T(4,128)S(1)}, s32[1024,4]{0,1:T(4,128)}, u32[]{:S(2)}) copy-start(s32[1024,4]{0,1:T(4,128)} %param.23) | copy-start | bytes 49156
  330.0 25.1 %copy-start.38 = (bf16[1024,384]{1,0:T(8,128)(2,1)S(1)}, bf16[1024,384]{1,0:T(8,128)(2,1)}, u32[]{:S(2)}) copy-start(bf16[1024,384]{1,0:T(8,128)(2,1)} %get-tuple-element.50) | copy-start | bytes 2359300
  330.0 25.6 %copy-start.37 = (bf16[1024,384]{1,0:T(8,128)(2,1)S(1)}, bf16[1024,384]{1,0:T(8,128)(2,1)}, u32[]{:S(2)}) copy-start(bf16[1024,384]{1,0:T(8,128)(2,1)} %get-tuple-element.51) | copy-start | bytes 2359300
  330.0 27.7 %copy-start.36 = (bf16[1024,384]{1,0:T(8,128)(2,1)S(1)}, bf16[1024,384]{1,0:T(8,128)(2,1)}, u32[]{:S(2)}) copy-start(bf16[1024,384]{1,0:T(8,128)(2,1)} %get-tuple-element.49) | copy-start | bytes 2359300
  330.1 6.7 %collective-permute-start.23 = (bf16[48,768]{1,0:T(8,128)(2,1)S(1)}, bf16[48,768]{1,0:T(8,128)(2,1)S(1)}, u32[]{:S(2)}, u32[]{:S(2)}) collective-permute-start(bf16[48,768]{1,0:T(8,128)(2,1)S(1)} %select_convert_fusion.3), channel_id=1, source_target_pairs={{0,2},{1,3},{2,0},{3,1},{4,6},{5,7},{6,4},{7,5},{8,10},{9,11},{10,... | collective-permute-start | bytes 221192 | tf_op jit(solution)/shard_map/ppermute | solution.py:515
  336.8 6.7 %collective-permute-start.24 = (bf16[24,768]{1,0:T(8,128)(2,1)S(1)}, bf16[24,768]{1,0:T(8,128)(2,1)S(1)}, u32[]{:S(2)}, u32[]{:S(2)}) collective-permute-start(bf16[24,768]{1,0:T(8,128)(2,1)S(1)} %select_convert_fusion.4), channel_id=1, source_target_pairs={{0,4},{1,5},{2,6},{3,7},{4,0},{5,1},{6,2},{7,3},{8,12},{9,13},{10,... | collective-permute-start | bytes 110600 | tf_op jit(solution)/shard_map/ppermute | solution.py:515
  343.5 5.4 %collective-permute-start.25 = (bf16[24,768]{1,0:T(8,128)(2,1)S(1)}, bf16[24,768]{1,0:T(8,128)(2,1)S(1)}, u32[]{:S(2)}, u32[]{:S(2)}) collective-permute-start(bf16[24,768]{1,0:T(8,128)(2,1)S(1)} %add_convert_fusion.1), channel_id=1, source_target_pairs={{0,4},{1,5},{2,6},{3,7},{4,0},{5,1},{6,2},{7,3},{8,12},{9,13},{10,... | collective-permute-start | bytes 110600 | tf_op jit(solution)/shard_map/ppermute | solution.py:523
  349.0 4.4 %collective-permute-start.26 = (bf16[48,768]{1,0:T(8,128)(2,1)S(1)}, bf16[48,768]{1,0:T(8,128)(2,1)S(1)}, u32[]{:S(2)}, u32[]{:S(2)}) collective-permute-start(bf16[48,768]{1,0:T(8,128)(2,1)S(1)} %pad_maximum_fusion.7), channel_id=1, source_target_pairs={{0,2},{1,3},{2,0},{3,1},{4,6},{5,7},{6,4},{7,5},{8,10},{9,11},{10,... | collective-permute-start | bytes 221192 | tf_op jit(solution)/shard_map/ppermute | solution.py:523
  353.4 22.1 %collective-permute-start.27 = (bf16[96,768]{1,0:T(8,128)(2,1)S(1)}, bf16[96,768]{1,0:T(8,128)(2,1)S(1)}, u32[]{:S(2)}, u32[]{:S(2)}) collective-permute-start(bf16[96,768]{1,0:T(8,128)(2,1)S(1)} %pad_maximum_fusion.5), channel_id=1, source_target_pairs={{0,16},{8,24},{16,0},{24,8},{1,17},{9,25},{17,1},{25,9},{2,18},{10... | collective-permute-start | bytes 442376 | tf_op jit(solution)/shard_map/ppermute | solution.py:523
  355.1 49.3 %collective-permute-start.10 = (bf16[1024,384]{1,0:T(8,128)(2,1)S(1)}, bf16[1024,384]{1,0:T(8,128)(2,1)S(1)}, u32[]{:S(2)}, u32[]{:S(2)}) collective-permute-start(bf16[1024,384]{1,0:T(8,128)(2,1)S(1)} %copy-done.38), channel_id=1, source_target_pairs={{0,16},{8,24},{16,0},{24,8},{1,17},{9,25},{17,1},{25,9},{2,18},{10... | collective-permute-start | bytes 2359304 | tf_op jit(solution)/shard_map/ppermute | solution.py:491
  355.6 48.8 %collective-permute-start.11 = (bf16[1024,384]{1,0:T(8,128)(2,1)S(1)}, bf16[1024,384]{1,0:T(8,128)(2,1)S(1)}, u32[]{:S(2)}, u32[]{:S(2)}) collective-permute-start(bf16[1024,384]{1,0:T(8,128)(2,1)S(1)} %copy-done.37), channel_id=1, source_target_pairs={{0,24},{8,16},{16,8},{24,0},{1,25},{9,17},{17,9},{25,1},{2,26},{10... | collective-permute-start | bytes 2359304 | tf_op jit(solution)/shard_map/ppermute | solution.py:491
  357.7 46.7 %collective-permute-start.9 = (bf16[1024,384]{1,0:T(8,128)(2,1)S(1)}, bf16[1024,384]{1,0:T(8,128)(2,1)S(1)}, u32[]{:S(2)}, u32[]{:S(2)}) collective-permute-start(bf16[1024,384]{1,0:T(8,128)(2,1)S(1)} %copy-done.36), channel_id=1, source_target_pairs={{0,8},{8,0},{16,24},{24,16},{1,9},{9,1},{17,25},{25,17},{2,10},{10... | collective-permute-start | bytes 2359304 | tf_op jit(solution)/shard_map/ppermute | solution.py:491
  375.6 28.6 %collective-permute-start.28 = (bf16[192,768]{1,0:T(8,128)(2,1)S(1)}, bf16[192,768]{1,0:T(8,128)(2,1)S(1)}, u32[]{:S(2)}, u32[]{:S(2)}) collective-permute-start(bf16[192,768]{1,0:T(8,128)(2,1)S(1)} %pad_maximum_fusion.4), channel_id=1, source_target_pairs={{0,8},{8,0},{16,24},{24,16},{1,9},{9,1},{17,25},{25,17},{2,10},{10... | collective-permute-start | bytes 884744 | tf_op jit(solution)/shard_map/ppermute | solution.py:523
  376.4 1.2 collective-permute-start.15
  377.6 18.0 %collective-permute-start.16 = (f32[8,384]{1,0:T(8,128)S(1)}, f32[8,384]{1,0:T(8,128)S(1)}, u32[]{:S(2)}, u32[]{:S(2)}) collective-permute-start(f32[8,384]{1,0:T(8,128)S(1)} %fusion.7), channel_id=1, source_target_pairs={{0,8},{8,0},{16,24},{24,16},{1,9},{9,1},{17,25},{25,17},{2,10},{10... | collective-permute-start | bytes 36872 | tf_op jit(solution)/shard_map/ppermute | solution.py:518
  395.6 3.7 collective-permute-start.17
  399.3 3.7 collective-permute-start.18
  403.0 1.6 copy-start.27
  403.0 4.8 %collective-permute-start.19 = (f32[8,384]{1,0:T(8,128)S(1)}, f32[8,384]{1,0:T(8,128)S(1)}, u32[]{:S(2)}, u32[]{:S(2)}) collective-permute-start(f32[8,384]{1,0:T(8,128)S(1)} %add.100), channel_id=1, source_target_pairs={{0,4},{1,5},{2,6},{3,7},{4,0},{5,1},{6,2},{7,3},{8,12},{9,13},{10,... | collective-permute-start | bytes 36872 | tf_op jit(solution)/shard_map/ppermute | solution.py:518
  404.3 4.6 %collective-permute-start.29 = (bf16[384,768]{1,0:T(8,128)(2,1)S(1)}, bf16[384,768]{1,0:T(8,128)(2,1)S(1)}, u32[]{:S(2)}, u32[]{:S(2)}) collective-permute-start(bf16[384,768]{1,0:T(8,128)(2,1)S(1)} %pad_maximum_fusion.2), channel_id=1, source_target_pairs={{0,1},{1,0},{2,3},{3,2},{4,5},{5,4},{6,7},{7,6},{8,9},{9,8},{10,11... | collective-permute-start | bytes 1769480 | tf_op jit(solution)/shard_map/ppermute | solution.py:523
  404.6 3.7 copy-start.33
  404.6 3.7 copy-start.34
  409.4 2.1 copy-start.29
  409.4 3.4 copy-start.23
  409.4 3.4 copy-start.22
  411.5 2.3 slice-start
  411.5 2.9 copy-start.21
  419.6 3.9 copy-start.25
  419.6 3.9 copy-start.26
  422.4 1.6 copy-start.20
  422.4 2.0 copy-start.24
  (13 other events, 15.1 us)
Sparse Core Ops, SparseCore 0:
  14.1 53.9 all-gather.4
  70.3 49.9 all-gather.2
  235.5 56.6 reduce-scatter.4
  294.3 56.1 reduce-scatter.2

commit v4 on v3

--- a/solution.py
+++ b/solution.py
@@ -13,7 +13,6 @@
 HEAD = 64
 EXPERTS = 16
 TOP = 4
-TASKS = 2
 CAP = 320
 
 
@@ -27,6 +26,7 @@
 NORM_EPS = 1e-06
 MASKED = -1e30
 VMEM_MOST = 67043328
+DIGITS = 9
 
 
 def route_kernel(first_expert, ids_ref, gates_ref, rows_ref, gate_rows_ref, cols_ref):
@@ -359,8 +359,8 @@
     block, slots, marks_ref, x_ref, norm_ref, qkv_ref, proj_ref, seg_ref, task_ref, out_grad_ref,
     joined_ref, key_t_ref, mixed_ref, mixed_t_ref, logs_ref, hidden_ref, *rest
 ):
-    du_refs, rest = rest[:slots], rest[slots:]
-    patch_ref, weight_ref, norms_ref, grads, attn_in, key_grad, value_grad, column = rest
+    du_refs, digits_ref, rest = rest[:slots], rest[slots], rest[slots + 1 :]
+    patch_ref, weight_ref, grads, attn_in, norms_ref, key_grad, value_grad, column = rest
     tokens = x_ref.shape[0]
     blocks = tokens // block
     qkv_low = qkv_ref[...].astype(jnp.bfloat16)
@@ -389,7 +389,7 @@
         hidden_grad = out_grad_ref[span, :].astype(jnp.float32) + unit_rows_back(unit, rate, du * gain)
         patch_ref[span, :] = hidden_grad
         grad_low = hidden_grad.astype(jnp.bfloat16)
-        weight_ref[D:, D:] += mxu(mixed_ref[span, :], grad_low, TN)
+        weight_ref[D:, D : 2 * D] += mxu(mixed_ref[span, :], grad_low, TN)
         mixed_grad = mxu(grad_low, proj_low, NT).astype(jnp.bfloat16)
         mixed_grad_t = mxu(proj_low, grad_low, NT).astype(jnp.bfloat16).astype(jnp.float32)
         dots = mixed_grad_t * mixed_t_ref[:, span].astype(jnp.float32)
@@ -455,27 +455,30 @@
         return carry
 
     lax.fori_loop(0, blocks, finish, 0)
-    weight_ref[:D, :] = mxu(attn_in[...], grads[:, : 2 * D], TN)
+    weight_ref[:D, : 2 * D] = mxu(attn_in[...], grads[:, : 2 * D], TN)
     weight_ref[D:, :D] = mxu(attn_in[...], grads[:, 2 * D :], TN)
-
-
-def attend_back(marks, x, norm, qkv, proj, seg, task, out_grad, saved, du_parts):
+    for part in range(D // 128):
+        weight_ref[part * 8 : part * 8 + 8, 2 * D :] = norms_ref[:, part * 128 : (part + 1) * 128]
+    weight_ref[24 : 24 + digits_ref.shape[0], 2 * D :] = digits_ref[...]
+
+
+def attend_back(marks, x, norm, qkv, proj, seg, task, out_grad, saved, du_parts, digits):
     tokens = x.shape[0]
     block = min(256, tokens)
     vmem = pl.BlockSpec(memory_space=pltpu.VMEM)
-    operands = [marks, x, norm, qkv, proj, seg, task, out_grad, *saved, *du_parts]
+    operands = [marks, x, norm, qkv, proj, seg, task, out_grad, *saved, *du_parts, digits]
     return pl.pallas_call(
         functools.partial(attend_back_kernel, block, len(du_parts)),
         out_shape=(
             jax.ShapeDtypeStruct((tokens, D), jnp.float32),
-            jax.ShapeDtypeStruct((2 * D, 2 * D), jnp.float32),
-            jax.ShapeDtypeStruct((8, D), jnp.float32),
+            jax.ShapeDtypeStruct((2 * D, 2 * D + 128), jnp.float32),
         ),
         in_specs=[pl.BlockSpec(memory_space=pltpu.SMEM)] + [vmem] * (len(operands) - 1),
-        out_specs=(vmem,) * 3,
+        out_specs=(vmem,) * 2,
         scratch_shapes=[
             pltpu.VMEM((tokens, 3 * D), jnp.bfloat16),
             pltpu.VMEM((tokens, D), jnp.bfloat16),
+            pltpu.VMEM((8, D), jnp.float32),
             pltpu.VMEM((tokens, D), jnp.float32),
             pltpu.VMEM((tokens, D), jnp.float32),
             pltpu.VMEM((tokens, 128), jnp.float32),
@@ -570,14 +573,17 @@
         lax.all_gather(both[:, half:], "hidden", axis=0, tiled=True),
     ]
     table = jnp.concatenate([expert_ids.astype(jnp.float32).T, gates.T], axis=0)
-    tables = jnp.stack(to_peers([table] * groups, groups))
+    tables = to_peers([table] * groups, groups)
     g_all = to_peers([cotangent] * groups, groups)
     first_expert = (lax.axis_index("expert") * local_count).astype(jnp.int32).reshape(1)
+    tables = jnp.stack(tables)
     rows, gate_rows, cols = route(first_expert, tables[:, :TOP], tables[:, TOP:], local_count)
     named = jnp.sum(
-        (expert_ids[:, :, None] == jnp.arange(EXPERTS, dtype=jnp.int32)).astype(jnp.float32), axis=(0, 1)
-    )
-    counts = jnp.minimum(named, float(CAP))
+        (expert_ids[:, :, None] == jnp.arange(EXPERTS, dtype=jnp.int32)).astype(jnp.int32), axis=(0, 1)
+    )
+    counts = jnp.minimum(named, CAP)
+    digits = (counts[None, :] >> jnp.arange(16, dtype=jnp.int32)[:, None]) & 1
+    digits = jnp.pad(digits.astype(jnp.float32), ((0, 0), (0, 128 - EXPERTS)))
     marks = segments[0]
     task_row = task_ids[None]
     *saved, moe_in = attend(marks, patches, norm_params, attn_qkv, attn_proj, segments, task_row)
@@ -591,23 +597,23 @@
     y_parts = to_peers(parts[groups:], groups)
     moe_sum = sum(p.astype(jnp.float32) for p in y_parts)
     block_out = (hidden_one + moe_sum).astype(jnp.bfloat16)
-    owned = [
-        lax.psum_scatter(g, "hidden", scatter_dimension=0, tiled=True)
-        for g in (grads_first, grads_second)
-    ]
+    owned = []
+    for grads in (grads_first, grads_second):
+        owned.append(lax.psum_scatter(grads, "hidden", scatter_dimension=0, tiled=True))
     owned = jnp.concatenate(owned, axis=1).astype(jnp.float32)
     owned = owned.reshape(own_units, local_count, 2, D)
     inner_grad, outer_grad = owned[:, :, 0], owned[:, :, 1]
-    patch_grad, big, norm_grad = attend_back(
-        marks, patches, norm_params, attn_qkv, attn_proj, segments, task_row, cotangent, saved, du_parts
+    patch_grad, big = attend_back(
+        marks, patches, norm_params, attn_qkv, attn_proj, segments, task_row, cotangent, saved,
+        du_parts, digits,
     )
     big_sum = butterfly_sum(big, jnp.bfloat16)
-    qkv_sum = jnp.concatenate([big_sum[:D], big_sum[D:, :D]], axis=1)
-    proj_sum = big_sum[D:, D:]
-    count_row = jnp.pad(counts, (0, D - EXPERTS))[None]
-    small = jnp.concatenate([norm_grad[:6], count_row, jnp.zeros((1, D), jnp.float32)], axis=0)
-    small_sum = butterfly_sum(small, jnp.float32)
-    norm_sum, count_sum = small_sum[:6], small_sum[6, :EXPERTS]
+    qkv_sum = jnp.concatenate([big_sum[:D, : 2 * D], big_sum[D:, :D]], axis=1)
+    proj_sum = big_sum[D:, D : 2 * D]
+    extra = big_sum[:, 2 * D :]
+    norm_sum = jnp.concatenate([extra[8 * p : 8 * p + 6] for p in range(D // 128)], axis=1)
+    powers = 2.0 ** jnp.arange(DIGITS, dtype=jnp.float32)
+    count_sum = jnp.sum(extra[24 : 24 + DIGITS, :EXPERTS] * powers[:, None], axis=0)
     expert_load = count_sum * (EXPERTS / (tokens_all * TOP))
     root_tokens = math.sqrt(tokens_all)
     norm_new = nesterov(norm_params, norm_moment, norm_average, norm_sum, RATE_NORM / root_tokens)

time: 443 us -> 436 us (0.984)
  waiting for transfers between devices: 166 us -> 157 us
    ppermute x5 -> x0, waiting for transfers between devices: 25 us -> none  [butterfly_sum(): lax.ppermute(value.astype(wire), axis, [(i, i ^ bit) for i in range(size)])]
    ppermute x15, waiting for transfers between devices: 93.7 us -> 117 us  [to_peers(): lax.ppermute(arrays[k], 'expert', [(i, i ^ k) for i in range(groups)])]
    ppermute x5, waiting for transfers between devices: 22.3 us -> 15 us  [butterfly_sum(): got = lax.ppermute(value, axis, [(i, i ^ bit) for i in range(size)])]
    ppermute x15, starting transfers between devices: 17.3 us -> 21.8 us  [to_peers(): lax.ppermute(arrays[k], 'expert', [(i, i ^ k) for i in range(groups)])]
    ppermute x5 -> x0, starting transfers between devices: 4.55 us -> none  [butterfly_sum(): lax.ppermute(value.astype(wire), axis, [(i, i ^ bit) for i in range(size)])]
  transfers between devices with their start and end apart: 34 -> 29, of which waited for: 21 -> 18; matrix products, arithmetic and copies ran while one was open for 3% -> 4% of each run, Pallas kernels for 29% -> 30%
where the time goes in v4:
time: 436 us; the launch traced here: 429 us
  Pallas kernels  183 us (42%)
  waiting for transfers between devices  157 us (36%)
  starting transfers between devices  37.6 us (9%)
  other arithmetic  21.4 us (5%)
  local copies, waits for them, and re-layouts  16.2 us (4%)
  between operations  14.7 us (3%)
    ppermute x15, waiting for transfers between devices, to_peers(): lax.ppermute(arrays[k], 'expert', [(i, i ^ k) for i in range(groups)])  117 us
    pallas_call x2, Pallas kernels, moe(): pl.pallas_call(functools.partial(moe_kernel, offset, count, start is not...  108 us
    pallas_call x1, Pallas kernels, attend_back(): pl.pallas_call(functools.partial(attend_back_kernel, block, len(du_parts)...  38.7 us
    pallas_call x1, Pallas kernels, attend(): pl.pallas_call(functools.partial(attend_kernel, block), out_shape=(jax.Sh...  34.2 us
    ppermute x5, waiting for transfers between devices, butterfly_sum(): got = lax.ppermute(send, axis, [(i, i ^ bit) for i in range(size)])  23.8 us
    ppermute x15, starting transfers between devices, to_peers(): lax.ppermute(arrays[k], 'expert', [(i, i ^ k) for i in range(groups)])  21.8 us
    ppermute x5, waiting for transfers between devices, butterfly_sum(): got = lax.ppermute(value, axis, [(i, i ^ bit) for i in range(size)])  15 us
    add x4, other arithmetic, nesterov(): average_new = AVERAGE_DECAY * average + (1.0 - AVERAGE_DECAY) * weight_new  10.2 us
  transfers between devices with their start and end apart: 29, of which 18 were waited for; matrix products, arithmetic and copies ran while one was open for 4% of the time, Pallas kernels for 30%

profile of v4, /device:TPU:0, one launch (start us, length us, event | category | flops | bytes accessed | tf_op | source)
XLA Modules:
  0.0 429.3 jit_solution(11173234526181441075)
XLA Ops:
  7.2 2.0 convert_bitcast_fusion
  9.3 0.8 pad_maximum_fusion.1
  10.1 1.8 copy.43
  11.9 0.9 convert_element_type.72
  12.9 1.1 fusion.5
  14.1 0.7 all-gather.3.cloned.1.call-update
  14.9 34.2 %attend.1 = (bf16[1024,1152]{1,0:T(8,128)(2,1)}, bf16[384,1024]{1,0:T(8,128)(2,1)S(1)}, bf16[1024,384]{1,0:T(8,128)(2,1)S(1)}, bf16[384,1024]{1,0:T(8,128)(2,1)S...) custom-call(s32[1024]{0:T(1024)S(1)} %bitcast.31, ...), custom_call_target="tpu_custom_call" | custom-call | flops 8589934592 | bytes 12582912 | tf_op jit(solution)/shard_map/attend/pallas_call | solution.py:338
  49.1 1.1 copy-done
  50.3 0.9 copy-done.13
  51.2 0.9 copy-done.14
  52.1 0.9 copy-done.15
  53.0 3.0 collective-permute-start.3
  56.1 2.0 collective-permute-start.1
  58.1 1.4 collective-permute-start.2
  59.5 1.5 collective-permute-start.4
  61.1 12.9 %collective-permute-done = f32[8,1024]{1,0:T(8,128)S(1)} collective-permute-done((f32[8,1024]{1,0:T(8,128)S(1)}, f32[8,1024]{1,0:T(8,128)S(1)}, u32[]{:S(2)}, u32[]{:S(2)}) %collective-permute-start) | collective-permute-done | bytes 32800 | tf_op jit(solution)/shard_map/ppermute | solution.py:494
  74.0 3.3 collective-permute-start.5
  77.9 2.9 collective-permute-start.8
  80.8 0.7 fusion.6
  81.5 2.2 route.1
  83.6 12.7 %collective-permute-done.4.rest_2_ = bf16[1024,384]{1,0:T(8,128)(2,1)} collective-permute-done((bf16[1024,384]{1,0:T(8,128)(2,1)S(1)}, bf16[1024,384]{1,0:T(8,128)(2,1)}, u32[]{:S(2)}, u32[]{:S(2)}) %collective-permute-start.4) | collective-permute-done | bytes 786464 | tf_op jit(solution)/shard_map/ppermute | solution.py:494
  96.4 16.7 %collective-permute-done.6.rest_5_ = bf16[1024,384]{1,0:T(8,128)(2,1)} collective-permute-done((bf16[1024,384]{1,0:T(8,128)(2,1)S(1)}, bf16[1024,384]{1,0:T(8,128)(2,1)}, u32[]{:S(2)}, u32[]{:S(2)}) %collective-permute-start.6) | collective-permute-done | bytes 786464 | tf_op jit(solution)/shard_map/ppermute | solution.py:494
  113.1 15.7 %collective-permute-done.7.rest_6_ = bf16[1024,384]{1,0:T(8,128)(2,1)} collective-permute-done((bf16[1024,384]{1,0:T(8,128)(2,1)S(1)}, bf16[1024,384]{1,0:T(8,128)(2,1)}, u32[]{:S(2)}, u32[]{:S(2)}) %collective-permute-start.7) | collective-permute-done | bytes 786464 | tf_op jit(solution)/shard_map/ppermute | solution.py:494
  128.8 52.9 %moe.2 = (f32[4,1024,768]{2,1,0:T(8,128)}, bf16[1536,1536]{1,0:T(8,128)(2,1)}) custom-call(s32[4,4,1024]{2,1,0:T(4,128)} %get-tuple-element.42.rows_ref, f32[4,4,1024]{2,1,0:T(4,128)} %get-tuple-element.43.gate_rows_ref, s32[1024,128]{1,0:T(8,128)} %get-tuple-element.44.cols_ref, bf16[1024,384]{1,0:T(8,128)(2,1)} %copy-done.8, bf16[1024,384]{1,0:T(8,128)(2,1)} %copy-done.38, ...), custom_call_target="tpu_custom_call" | custom-call | flops 26172456960 | bytes 41943040 | tf_op jit(solution)/shard_map/moe/pallas_call | solution.py:204
  181.8 54.8 %moe.3 = (bf16[1024,384]{1,0:T(8,128)(2,1)}, bf16[1024,384]{1,0:T(8,128)(2,1)}, bf16[1024,384]{1,0:T(8,128)(2,1)}, bf16[1024,384]{1,0:T(8,128)(2,1)}, bf16[1024,...) custom-call(s32[4,4,1024]{2,1,0:T(4,128)} %get-tuple-element.42.rows, ...), custom_call_target="tpu_custom_call" | custom-call | flops 26172456960 | bytes 41943040 | tf_op jit(solution)/shard_map/moe/pallas_call | solution.py:204
  236.7 1.0 collective-permute-start.12
  237.7 1.7 collective-permute-start.13
  239.4 0.8 collective-permute-start.14
  240.5 17.0 %collective-permute-done.12.rest_1_ = bf16[1024,384]{1,0:T(8,128)(2,1)} collective-permute-done((bf16[1024,384]{1,0:T(8,128)(2,1)}, bf16[1024,384]{1,0:T(8,128)(2,1)}, u32[]{:S(2)}, u32[]{:S(2)}) %collective-permute-start.12) | collective-permute-done | bytes 786464 | tf_op jit(solution)/shard_map/ppermute | solution.py:494
  257.5 12.6 %collective-permute-done.13.rest_2_ = bf16[1024,384]{1,0:T(8,128)(2,1)} collective-permute-done((bf16[1024,384]{1,0:T(8,128)(2,1)S(1)}, bf16[1024,384]{1,0:T(8,128)(2,1)}, u32[]{:S(2)}, u32[]{:S(2)}) %collective-permute-start.13) | collective-permute-done | bytes 786464 | tf_op jit(solution)/shard_map/ppermute | solution.py:494
  270.1 1.0 collective-permute-done.14.rest_3_
  271.2 38.7 %attend_back.1 = (f32[1024,384]{1,0:T(8,128)}, f32[768,896]{1,0:T(8,128)}) custom-call(s32[1024]{0:T(1024)S(1)} %bitcast.32, bf16[1024,384]{1,0:T(8,128)(2,1)S(1)} %copy-done.7, f32[6,384]{1,0:T(8,128)S(1)} %copy-done.5, f32[384,1152]{1,0:T(8,128)} %qkv_ref.3, f32[384,384]{1,0:T(8,128)S(1)} %copy-done.3, s32[1,1024]{1,0:T(1,128)S(1)} %copy-done.10, ...), custom_call_target="tpu_custom_call" | custom-call | flops 25769803776 | bytes 25165824 | tf_op jit(solution)/shard_map/attend_back/pallas_call | solution.py:470
  309.8 1.9 select_convert_fusion
  311.8 2.1 collective-permute-done.15
  314.0 2.0 convert_add_fusion
  316.1 1.5 collective-permute-start.16
  317.6 8.6 %collective-permute-done.16 = bf16[192,896]{1,0:T(8,128)(2,1)S(1)} collective-permute-done((bf16[192,896]{1,0:T(8,128)(2,1)S(1)}, bf16[192,896]{1,0:T(8,128)(2,1)S(1)}, u32[]{:S(2)}, u32[]{:S(2)}) %collective-permute-start.16) | collective-permute-done | bytes 344096 | tf_op jit(solution)/shard_map/ppermute | solution.py:518
  326.4 1.6 collective-permute-start.17
  328.0 4.1 collective-permute-done.17
  332.1 1.8 collective-permute-start.18
  333.9 5.2 %collective-permute-done.18 = bf16[48,896]{1,0:T(8,128)(2,1)S(1)} collective-permute-done((bf16[48,896]{1,0:T(8,128)(2,1)S(1)}, bf16[48,896]{1,0:T(8,128)(2,1)S(1)}, u32[]{:S(2)}, u32[]{:S(2)}) %collective-permute-start.18) | collective-permute-done | bytes 86048 | tf_op jit(solution)/shard_map/ppermute | solution.py:518
  339.2 2.8 collective-permute-start.19
  341.9 3.8 collective-permute-done.19
  345.8 2.2 collective-permute-start.20
  348.0 2.7 collective-permute-done.20
  350.8 1.6 collective-permute-start.21
  352.4 3.0 collective-permute-done.21
  355.4 1.6 collective-permute-start.22
  357.0 3.8 collective-permute-done.22
  361.0 2.3 collective-permute-start.23
  363.3 0.9 collective-permute-start.10
  364.2 0.6 collective-permute-start.11
  364.9 1.9 collective-permute-start.9
  366.8 5.4 %collective-permute-done.23 = bf16[192,896]{1,0:T(8,128)(2,1)S(1)} collective-permute-done((bf16[192,896]{1,0:T(8,128)(2,1)S(1)}, bf16[192,896]{1,0:T(8,128)(2,1)S(1)}, u32[]{:S(2)}, u32[]{:S(2)}) %collective-permute-start.23) | collective-permute-done | bytes 344096 | tf_op jit(solution)/shard_map/ppermute | solution.py:526
  372.5 22.2 %collective-permute-done.10 = bf16[1024,384]{1,0:T(8,128)(2,1)S(1)} collective-permute-done((bf16[1024,384]{1,0:T(8,128)(2,1)S(1)}, bf16[1024,384]{1,0:T(8,128)(2,1)S(1)}, u32[]{:S(2)}, u32[]{:S(2)}) %collective-permute-start.10) | collective-permute-done | bytes 786464 | tf_op jit(solution)/shard_map/ppermute | solution.py:494
  394.7 6.1 %collective-permute-done.9 = bf16[1024,384]{1,0:T(8,128)(2,1)S(1)} collective-permute-done((bf16[1024,384]{1,0:T(8,128)(2,1)S(1)}, bf16[1024,384]{1,0:T(8,128)(2,1)S(1)}, u32[]{:S(2)}, u32[]{:S(2)}) %collective-permute-start.9) | collective-permute-done | bytes 786464 | tf_op jit(solution)/shard_map/ppermute | solution.py:494
  400.9 1.3 add_convert_fusion
  404.3 1.4 multiply_add_fusion.6
  405.7 0.8 copy-done.20
  407.0 2.8 multiply_add_fusion
  409.9 1.9 concatenate.41
  412.3 2.3 concatenate.40
  415.2 1.1 maximum_convert_fusion.1
  417.1 5.4 %multiply_add_fusion.2 = (f32[192,4,384]{2,1,0:T(4,128)}, f32[192,4,384]{2,1,0:T(4,128)}, f32[192,4,384]{2,1,0:T(4,128)}, f32[192,4,384]{2,1,0:T(4,128)}, f32[192,4,384]{2,1,0:T(4,128)}, /*index=5*/f32[192,4,384]{2,1,0:T(4,128)}) fusion(f32[192,4,384]{2,1,0:T(4,128)S(1)} %copy-done.23, f32[192,4,384]{2,1,0:T(4,128)S(1)} %copy-done.18, ...), kind=kLoop, calls=%fused_computation.12 | loop fusion | flops 5308416 | bytes 16515072 | tf_op jit(solution)/shard_map/add | solution.py:536
  (134 shorter events, 6.6 us)
Async XLA Ops:
  7.2 121.7 %all-gather.5.cloned.1.call-start = ((), (), s32[]{:S(2)}) async-start(), calls=%async_computation.3 | async-start | bytes 5308416 | tf_op jit(solution)/shard_map/all_gather | solution.py:572
  12.8 2.0 copy-start.2
  12.9 2.0 copy-start.4
  12.9 2.0 copy-start.6
  12.9 2.0 copy-start.9
  12.9 2.0 copy-start.11
  14.0 167.8 %all-gather.3.cloned.1.call-start = ((), (), s32[]{:S(2)}) async-start(), calls=%async_computation.2 | async-start | bytes 5308416 | tf_op jit(solution)/shard_map/all_gather | solution.py:573
  14.8 395.1 %reduce-scatter.5.cloned.1.call-start = ((), (), s32[]{:S(2)}) async-start(), calls=%async_computation.5 | async-start | bytes 5308416 | tf_op jit(solution)/shard_map/reduce_scatter | solution.py:602
  14.9 41.1 %copy-start.29 = (s32[1024,4]{0,1:T(4,128)S(1)}, s32[1024,4]{0,1:T(4,128)}, u32[]{:S(2)}) copy-start(s32[1024,4]{0,1:T(4,128)} %param.23) | copy-start | bytes 49156
  14.9 41.1 %copy-start.31 = (f32[1024,4]{0,1:T(4,128)S(1)}, f32[1024,4]{0,1:T(4,128)}, u32[]{:S(2)}) copy-start(f32[1024,4]{0,1:T(4,128)} %param.24) | copy-start | bytes 49156
  14.9 62.4 %copy-start.34 = (bf16[1024,384]{1,0:T(8,128)(2,1)S(1)}, bf16[1024,384]{1,0:T(8,128)(2,1)}, u32[]{:S(2)}) copy-start(bf16[1024,384]{1,0:T(8,128)(2,1)} %out_grad_ref.1) | copy-start | bytes 2359300
  49.1 1.1 copy-start
  53.0 21.0 %copy-start.8 = (bf16[1024,384]{1,0:T(8,128)(2,1)}, bf16[1024,384]{1,0:T(8,128)(2,1)S(1)}, u32[]{:S(2)}) copy-start(bf16[1024,384]{1,0:T(8,128)(2,1)S(1)} %get-tuple-element.45.rest_0_) | copy-start | bytes 2359300
  53.0 24.9 %copy-start.16 = (f32[8,1024]{1,0:T(8,128)}, f32[8,1024]{1,0:T(8,128)S(1)}, u32[]{:S(2)}) copy-start(f32[8,1024]{1,0:T(8,128)S(1)} %get-tuple-element.55.logs_ref) | copy-start | bytes 98308
  53.0 24.9 %collective-permute-start.3 = (bf16[1024,384]{1,0:T(8,128)(2,1)S(1)}, bf16[1024,384]{1,0:T(8,128)(2,1)S(1)}, u32[]{:S(2)}, u32[]{:S(2)}) collective-permute-start(bf16[1024,384]{1,0:T(8,128)(2,1)S(1)} %get-tuple-element.45.rest_0_), channel_id=1, source_target_pairs={{0,8},{8,0},{16,24},{24,16},{1,9},{9,1},{17,25},{25,17},{2,10},{10... | collective-permute-start | bytes 2359304 | tf_op jit(solution)/shard_map/ppermute | solution.py:494
  56.0 18.0 %collective-permute-start = (f32[8,1024]{1,0:T(8,128)S(1)}, f32[8,1024]{1,0:T(8,128)S(1)}, u32[]{:S(2)}, u32[]{:S(2)}) collective-permute-start(f32[8,1024]{1,0:T(8,128)S(1)} %get-tuple-element.102), channel_id=1, source_target_pairs={{0,8},{8,0},{16,24},{24,16},{1,9},{9,1},{17,25},{25,17},{2,10},{10... | collective-permute-start | bytes 98312 | tf_op jit(solution)/shard_map/ppermute | solution.py:494
  56.1 21.2 %collective-permute-start.1 = (f32[8,1024]{1,0:T(8,128)S(1)}, f32[8,1024]{1,0:T(8,128)S(1)}, u32[]{:S(2)}, u32[]{:S(2)}) collective-permute-start(f32[8,1024]{1,0:T(8,128)S(1)} %get-tuple-element.102), channel_id=1, source_target_pairs={{0,16},{8,24},{16,0},{24,8},{1,17},{9,25},{17,1},{25,9},{2,18},{10... | collective-permute-start | bytes 98312 | tf_op jit(solution)/shard_map/ppermute | solution.py:494
  58.1 19.7 %collective-permute-start.2 = (f32[8,1024]{1,0:T(8,128)S(1)}, f32[8,1024]{1,0:T(8,128)S(1)}, u32[]{:S(2)}, u32[]{:S(2)}) collective-permute-start(f32[8,1024]{1,0:T(8,128)S(1)} %get-tuple-element.102), channel_id=1, source_target_pairs={{0,24},{8,16},{16,8},{24,0},{1,25},{9,17},{17,9},{25,1},{2,26},{10... | collective-permute-start | bytes 98312 | tf_op jit(solution)/shard_map/ppermute | solution.py:494
  59.5 36.9 %collective-permute-start.4 = (bf16[1024,384]{1,0:T(8,128)(2,1)S(1)}, bf16[1024,384]{1,0:T(8,128)(2,1)}, u32[]{:S(2)}, u32[]{:S(2)}) collective-permute-start(bf16[1024,384]{1,0:T(8,128)(2,1)S(1)} %get-tuple-element.45.rest_0_), channel_id=1, source_target_pairs={{0,16},{8,24},{16,0},{24,8},{1,17},{9,25},{17,1},{25,9},{2,18},{10... | collective-permute-start | bytes 2359304 | tf_op jit(solution)/shard_map/ppermute | solution.py:494
  74.0 22.4 %collective-permute-start.5 = (bf16[1024,384]{1,0:T(8,128)(2,1)S(1)}, bf16[1024,384]{1,0:T(8,128)(2,1)}, u32[]{:S(2)}, u32[]{:S(2)}) collective-permute-start(bf16[1024,384]{1,0:T(8,128)(2,1)S(1)} %get-tuple-element.45.rest_0_), channel_id=1, source_target_pairs={{0,24},{8,16},{16,8},{24,0},{1,25},{9,17},{17,9},{25,1},{2,26},{10... | collective-permute-start | bytes 2359304 | tf_op jit(solution)/shard_map/ppermute | solution.py:494
  77.2 35.9 %collective-permute-start.6 = (bf16[1024,384]{1,0:T(8,128)(2,1)S(1)}, bf16[1024,384]{1,0:T(8,128)(2,1)}, u32[]{:S(2)}, u32[]{:S(2)}) collective-permute-start(bf16[1024,384]{1,0:T(8,128)(2,1)S(1)} %copy-done.34), channel_id=1, source_target_pairs={{0,8},{8,0},{16,24},{24,16},{1,9},{9,1},{17,25},{25,17},{2,10},{10... | collective-permute-start | bytes 2359304 | tf_op jit(solution)/shard_map/ppermute | solution.py:494
  77.8 51.1 %collective-permute-start.7 = (bf16[1024,384]{1,0:T(8,128)(2,1)S(1)}, bf16[1024,384]{1,0:T(8,128)(2,1)}, u32[]{:S(2)}, u32[]{:S(2)}) collective-permute-start(bf16[1024,384]{1,0:T(8,128)(2,1)S(1)} %copy-done.34), channel_id=1, source_target_pairs={{0,16},{8,24},{16,0},{24,8},{1,17},{9,25},{17,1},{25,9},{2,18},{10... | collective-permute-start | bytes 2359304 | tf_op jit(solution)/shard_map/ppermute | solution.py:494
  77.9 50.9 %copy-start.38 = (bf16[1024,384]{1,0:T(8,128)(2,1)}, bf16[1024,384]{1,0:T(8,128)(2,1)S(1)}, u32[]{:S(2)}) copy-start(bf16[1024,384]{1,0:T(8,128)(2,1)S(1)} %collective-permute-done.3.rest_1_) | copy-start | bytes 2359300
  77.9 50.9 %collective-permute-start.8 = (bf16[1024,384]{1,0:T(8,128)(2,1)S(1)}, bf16[1024,384]{1,0:T(8,128)(2,1)}, u32[]{:S(2)}, u32[]{:S(2)}) collective-permute-start(bf16[1024,384]{1,0:T(8,128)(2,1)S(1)} %copy-done.34), channel_id=1, source_target_pairs={{0,24},{8,16},{16,8},{24,0},{1,25},{9,17},{17,9},{25,1},{2,26},{10... | collective-permute-start | bytes 2359304 | tf_op jit(solution)/shard_map/ppermute | solution.py:494
  236.6 2.9 copy-start.39
  236.6 3.6 copy-start.30
  236.6 175.7 %reduce-scatter.3.cloned.1.call-start = ((), (), s32[]{:S(2)}) async-start(), calls=%async_computation.4 | async-start | bytes 5308416 | tf_op jit(solution)/shard_map/reduce_scatter | solution.py:602
  236.7 20.8 %collective-permute-start.12 = (bf16[1024,384]{1,0:T(8,128)(2,1)}, bf16[1024,384]{1,0:T(8,128)(2,1)}, u32[]{:S(2)}, u32[]{:S(2)}) collective-permute-start(bf16[1024,384]{1,0:T(8,128)(2,1)} %get-tuple-element.57), channel_id=1, source_target_pairs={{0,8},{8,0},{16,24},{24,16},{1,9},{9,1},{17,25},{25,17},{2,10},{10... | collective-permute-start | bytes 2359304 | tf_op jit(solution)/shard_map/ppermute | solution.py:494
  237.7 32.4 %collective-permute-start.13 = (bf16[1024,384]{1,0:T(8,128)(2,1)S(1)}, bf16[1024,384]{1,0:T(8,128)(2,1)}, u32[]{:S(2)}, u32[]{:S(2)}) collective-permute-start(bf16[1024,384]{1,0:T(8,128)(2,1)S(1)} %copy-done.40), channel_id=1, source_target_pairs={{0,16},{8,24},{16,0},{24,8},{1,17},{9,25},{17,1},{25,9},{2,18},{10... | collective-permute-start | bytes 2359304 | tf_op jit(solution)/shard_map/ppermute | solution.py:494
  239.4 31.7 %collective-permute-start.14 = (bf16[1024,384]{1,0:T(8,128)(2,1)S(1)}, bf16[1024,384]{1,0:T(8,128)(2,1)}, u32[]{:S(2)}, u32[]{:S(2)}) collective-permute-start(bf16[1024,384]{1,0:T(8,128)(2,1)S(1)} %copy-done.39), channel_id=1, source_target_pairs={{0,24},{8,16},{16,8},{24,0},{1,25},{9,17},{17,9},{25,1},{2,26},{10... | collective-permute-start | bytes 2359304 | tf_op jit(solution)/shard_map/ppermute | solution.py:494
  240.4 30.7 %copy-start.3 = (f32[384,384]{1,0:T(8,128)S(1)}, f32[384,384]{1,0:T(8,128)}, u32[]{:S(2)}) copy-start(f32[384,384]{1,0:T(8,128)} %proj_ref.3) | copy-start | bytes 1769476
  240.4 30.7 %copy-start.5 = (f32[6,384]{1,0:T(8,128)S(1)}, f32[6,384]{1,0:T(8,128)}, u32[]{:S(2)}) copy-start(f32[6,384]{1,0:T(8,128)} %norm_ref.3) | copy-start | bytes 27652
  240.4 30.7 %copy-start.7 = (bf16[1024,384]{1,0:T(8,128)(2,1)S(1)}, bf16[1024,384]{1,0:T(8,128)(2,1)}, u32[]{:S(2)}) copy-start(bf16[1024,384]{1,0:T(8,128)(2,1)} %x_ref.3) | copy-start | bytes 2359300
  240.5 30.7 %copy-start.10 = (s32[1,1024]{1,0:T(1,128)S(1)}, s32[1,1024]{1,0:T(1,128)}, u32[]{:S(2)}) copy-start(s32[1,1024]{1,0:T(1,128)} %seg_ref.3) | copy-start | bytes 12292
  240.5 30.7 %copy-start.12 = (s32[1024]{0:T(1024)S(1)}, s32[1024]{0:T(1024)}, u32[]{:S(2)}) copy-start(s32[1024]{0:T(1024)} %param.25) | copy-start | bytes 12292
  240.5 30.7 %copy-start.17 = (f32[8,1024]{1,0:T(8,128)S(1)}, f32[8,1024]{1,0:T(8,128)}, u32[]{:S(2)}) copy-start(f32[8,1024]{1,0:T(8,128)} %copy-done.16) | copy-start | bytes 98308
  311.8 2.2 collective-permute-start.15
  316.1 10.1 %collective-permute-start.16 = (bf16[192,896]{1,0:T(8,128)(2,1)S(1)}, bf16[192,896]{1,0:T(8,128)(2,1)S(1)}, u32[]{:S(2)}, u32[]{:S(2)}) collective-permute-start(bf16[192,896]{1,0:T(8,128)(2,1)S(1)} %select_convert_fusion.1), channel_id=1, source_target_pairs={{0,8},{8,0},{16,24},{24,16},{1,9},{9,1},{17,25},{25,17},{2,10},{10... | collective-permute-start | bytes 1032200 | tf_op jit(solution)/shard_map/ppermute | solution.py:518
  326.4 5.7 %collective-permute-start.17 = (bf16[96,896]{1,0:T(8,128)(2,1)S(1)}, bf16[96,896]{1,0:T(8,128)(2,1)S(1)}, u32[]{:S(2)}, u32[]{:S(2)}) collective-permute-start(bf16[96,896]{1,0:T(8,128)(2,1)S(1)} %select_convert_fusion.2), channel_id=1, source_target_pairs={{0,16},{8,24},{16,0},{24,8},{1,17},{9,25},{17,1},{25,9},{2,18},{10... | collective-permute-start | bytes 516104 | tf_op jit(solution)/shard_map/ppermute | solution.py:518
  332.1 6.9 %collective-permute-start.18 = (bf16[48,896]{1,0:T(8,128)(2,1)S(1)}, bf16[48,896]{1,0:T(8,128)(2,1)S(1)}, u32[]{:S(2)}, u32[]{:S(2)}) collective-permute-start(bf16[48,896]{1,0:T(8,128)(2,1)S(1)} %select_convert_fusion.3), channel_id=1, source_target_pairs={{0,2},{1,3},{2,0},{3,1},{4,6},{5,7},{6,4},{7,5},{8,10},{9,11},{10,... | collective-permute-start | bytes 258056 | tf_op jit(solution)/shard_map/ppermute | solution.py:518
  339.1 24.2 %copy-start.37 = (bf16[1024,384]{1,0:T(8,128)(2,1)S(1)}, bf16[1024,384]{1,0:T(8,128)(2,1)}, u32[]{:S(2)}) copy-start(bf16[1024,384]{1,0:T(8,128)(2,1)} %get-tuple-element.49) | copy-start | bytes 2359300
  339.1 25.1 %copy-start.36 = (bf16[1024,384]{1,0:T(8,128)(2,1)S(1)}, bf16[1024,384]{1,0:T(8,128)(2,1)}, u32[]{:S(2)}) copy-start(bf16[1024,384]{1,0:T(8,128)(2,1)} %get-tuple-element.50) | copy-start | bytes 2359300
  339.1 25.7 %copy-start.35 = (bf16[1024,384]{1,0:T(8,128)(2,1)S(1)}, bf16[1024,384]{1,0:T(8,128)(2,1)}, u32[]{:S(2)}) copy-start(bf16[1024,384]{1,0:T(8,128)(2,1)} %get-tuple-element.48) | copy-start | bytes 2359300
  339.2 6.6 %collective-permute-start.19 = (bf16[24,896]{1,0:T(8,128)(2,1)S(1)}, bf16[24,896]{1,0:T(8,128)(2,1)S(1)}, u32[]{:S(2)}, u32[]{:S(2)}) collective-permute-start(bf16[24,896]{1,0:T(8,128)(2,1)S(1)} %select_convert_fusion.4), channel_id=1, source_target_pairs={{0,4},{1,5},{2,6},{3,7},{4,0},{5,1},{6,2},{7,3},{8,12},{9,13},{10,... | collective-permute-start | bytes 129032 | tf_op jit(solution)/shard_map/ppermute | solution.py:518
  345.8 5.0 %collective-permute-start.20 = (bf16[24,896]{1,0:T(8,128)(2,1)S(1)}, bf16[24,896]{1,0:T(8,128)(2,1)S(1)}, u32[]{:S(2)}, u32[]{:S(2)}) collective-permute-start(bf16[24,896]{1,0:T(8,128)(2,1)S(1)} %add_convert_fusion.1), channel_id=1, source_target_pairs={{0,4},{1,5},{2,6},{3,7},{4,0},{5,1},{6,2},{7,3},{8,12},{9,13},{10,... | collective-permute-start | bytes 129032 | tf_op jit(solution)/shard_map/ppermute | solution.py:526
  350.8 4.6 %collective-permute-start.21 = (bf16[48,896]{1,0:T(8,128)(2,1)S(1)}, bf16[48,896]{1,0:T(8,128)(2,1)S(1)}, u32[]{:S(2)}, u32[]{:S(2)}) collective-permute-start(bf16[48,896]{1,0:T(8,128)(2,1)S(1)} %pad_maximum_fusion.7), channel_id=1, source_target_pairs={{0,2},{1,3},{2,0},{3,1},{4,6},{5,7},{6,4},{7,5},{8,10},{9,11},{10,... | collective-permute-start | bytes 258056 | tf_op jit(solution)/shard_map/ppermute | solution.py:526
  355.4 5.5 %collective-permute-start.22 = (bf16[96,896]{1,0:T(8,128)(2,1)S(1)}, bf16[96,896]{1,0:T(8,128)(2,1)S(1)}, u32[]{:S(2)}, u32[]{:S(2)}) collective-permute-start(bf16[96,896]{1,0:T(8,128)(2,1)S(1)} %pad_maximum_fusion.5), channel_id=1, source_target_pairs={{0,16},{8,24},{16,0},{24,8},{1,17},{9,25},{17,1},{25,9},{2,18},{10... | collective-permute-start | bytes 516104 | tf_op jit(solution)/shard_map/ppermute | solution.py:526
  361.0 11.3 %collective-permute-start.23 = (bf16[192,896]{1,0:T(8,128)(2,1)S(1)}, bf16[192,896]{1,0:T(8,128)(2,1)S(1)}, u32[]{:S(2)}, u32[]{:S(2)}) collective-permute-start(bf16[192,896]{1,0:T(8,128)(2,1)S(1)} %pad_maximum_fusion.3), channel_id=1, source_target_pairs={{0,8},{8,0},{16,24},{24,16},{1,9},{9,1},{17,25},{25,17},{2,10},{10... | collective-permute-start | bytes 1032200 | tf_op jit(solution)/shard_map/ppermute | solution.py:526
  363.3 31.4 %collective-permute-start.10 = (bf16[1024,384]{1,0:T(8,128)(2,1)S(1)}, bf16[1024,384]{1,0:T(8,128)(2,1)S(1)}, u32[]{:S(2)}, u32[]{:S(2)}) collective-permute-start(bf16[1024,384]{1,0:T(8,128)(2,1)S(1)} %copy-done.37), channel_id=1, source_target_pairs={{0,16},{8,24},{16,0},{24,8},{1,17},{9,25},{17,1},{25,9},{2,18},{10... | collective-permute-start | bytes 2359304 | tf_op jit(solution)/shard_map/ppermute | solution.py:494
  364.2 30.5 %collective-permute-start.11 = (bf16[1024,384]{1,0:T(8,128)(2,1)S(1)}, bf16[1024,384]{1,0:T(8,128)(2,1)S(1)}, u32[]{:S(2)}, u32[]{:S(2)}) collective-permute-start(bf16[1024,384]{1,0:T(8,128)(2,1)S(1)} %copy-done.36), channel_id=1, source_target_pairs={{0,24},{8,16},{16,8},{24,0},{1,25},{9,17},{17,9},{25,1},{2,26},{10... | collective-permute-start | bytes 2359304 | tf_op jit(solution)/shard_map/ppermute | solution.py:494
  364.9 36.0 %copy-start.1 = (f32[1024,384]{1,0:T(8,128)S(1)}, f32[1024,384]{1,0:T(8,128)}, u32[]{:S(2)}) copy-start(f32[1024,384]{1,0:T(8,128)} %copy-done) | copy-start | bytes 4718596
  364.9 36.0 %copy-start.26 = (bf16[1024,384]{1,0:T(8,128)(2,1)S(1)}, bf16[1024,384]{1,0:T(8,128)(2,1)}, u32[]{:S(2)}) copy-start(bf16[1024,384]{1,0:T(8,128)(2,1)} %get-tuple-element.47) | copy-start | bytes 2359300
  364.9 36.0 %collective-permute-start.9 = (bf16[1024,384]{1,0:T(8,128)(2,1)S(1)}, bf16[1024,384]{1,0:T(8,128)(2,1)S(1)}, u32[]{:S(2)}, u32[]{:S(2)}) collective-permute-start(bf16[1024,384]{1,0:T(8,128)(2,1)S(1)} %copy-done.35), channel_id=1, source_target_pairs={{0,8},{8,0},{16,24},{24,16},{1,9},{9,1},{17,25},{25,17},{2,10},{10... | collective-permute-start | bytes 2359304 | tf_op jit(solution)/shard_map/ppermute | solution.py:494
  372.4 29.8 %collective-permute-start.24 = (bf16[384,896]{1,0:T(8,128)(2,1)S(1)}, bf16[384,896]{1,0:T(8,128)(2,1)S(1)}, u32[]{:S(2)}, u32[]{:S(2)}) collective-permute-start(bf16[384,896]{1,0:T(8,128)(2,1)S(1)} %pad_maximum_fusion.2), channel_id=1, source_target_pairs={{0,1},{1,0},{2,3},{3,2},{4,5},{5,4},{6,7},{7,6},{8,9},{9,8},{10,11... | collective-permute-start | bytes 2064392 | tf_op jit(solution)/shard_map/ppermute | solution.py:526
  402.8 1.5 copy-start.27
  402.8 1.5 copy-start.28
  402.9 2.8 copy-start.22
  404.3 2.2 copy-start.20
  404.3 2.7 copy-start.21
  412.3 3.9 copy-start.24
  412.3 3.9 copy-start.25
  415.1 1.3 copy-start.18
  415.1 1.6 copy-start.19
  415.1 2.0 copy-start.23
  (6 other events, 5.4 us)
Sparse Core Ops, SparseCore 0:
  14.1 54.0 all-gather.4
  70.4 49.8 all-gather.2
  236.8 55.7 reduce-scatter.4
  294.7 56.5 reduce-scatter.2

commit v5 on v4

--- a/solution.py
+++ b/solution.py
@@ -83,141 +83,220 @@
     return lax.dot_general(left, right, dims, preferred_element_type=jnp.float32)
 
 
-def moe_kernel(
-    offset, count, has_start, last, chunk, rows_ref, gate_rows_ref, cols_ref, *rest
-):
+def dispatch(rows_ref, gate_rows_ref, u_refs, g_refs, lane, x_out, dy_out, gate_out):
     slots, _, tokens = rows_ref.shape
-    rest = list(rest)
-    u_refs, g_refs, rest = rest[:slots], rest[slots : 2 * slots], rest[2 * slots :]
-    inner_ref, outer_ref, rest = rest[0], rest[1], rest[2:]
-    if has_start:
-        start_ref, rest = rest[0], rest[1:]
-    out_count = 2 * slots if last else 1
-    sums_refs, grads_ref, rest = rest[:out_count], rest[out_count], rest[out_count + 1 :]
-    x_buf, dy_buf, act_buf, dpre_buf, gate_buf, sum_buf = rest[:6]
-    step = pl.program_id(0)
-    width = u_refs[0].shape[1]
-    units = inner_ref.shape[0]
     for slot in range(slots):
-        place = rows_ref[slot, pl.ds(offset + step, 1), :]
+        place = rows_ref[slot, pl.ds(lane, 1), :]
         same = lax.broadcasted_iota(jnp.int32, (CAP, tokens), 0) == place
         pick = jnp.where(same, 1.0, 0.0).astype(jnp.bfloat16)
-        gate = jnp.sum(
-            jnp.where(same, gate_rows_ref[slot, pl.ds(offset + step, 1), :], 0.0), axis=1, keepdims=True
-        )
+        gate = jnp.sum(jnp.where(same, gate_rows_ref[slot, pl.ds(lane, 1), :], 0.0), axis=1, keepdims=True)
         span = pl.ds(slot * CAP, CAP)
-        x_buf[span, :] = mxu(pick, u_refs[slot][...]).astype(jnp.bfloat16)
-        dy_buf[span, :] = (gate * mxu(pick, g_refs[slot][...])).astype(jnp.bfloat16)
-        gate_buf[span, :] = jnp.broadcast_to(gate, (CAP, 128))
+        x_out[span, :] = mxu(pick, u_refs[slot][...]).astype(jnp.bfloat16)
+        dy_out[span, :] = (gate * mxu(pick, g_refs[slot][...])).astype(jnp.bfloat16)
+        gate_out[span, :] = jnp.broadcast_to(gate, (CAP, 128))
+
+
+def combine(cols_ref, lanes, step, buf, sum_buf, fresh):
+    tokens = cols_ref.shape[0]
+    for slot, lane in enumerate(lanes):
+        wide = lax.broadcasted_iota(jnp.int32, (tokens, 128), 1) == lane
+        column = jnp.sum(jnp.where(wide, cols_ref[...], 0), axis=1, keepdims=True)
+        same = lax.broadcasted_iota(jnp.int32, (tokens, CAP), 1) == column
+        spread = jnp.where(same, 1.0, 0.0).astype(jnp.bfloat16)
+        add = mxu(spread, buf[pl.ds(slot * CAP, CAP), :])
+        old = sum_buf[slot]
+        if fresh:
+            old = jnp.where(step > 0, old, 0.0)
+        sum_buf[slot] = old + add
+
+
+def gelu_pair(pre, act_grad):
+    phi = 0.5 + 0.5 * lax.erf(pre * math.sqrt(0.5))
+    bell = jnp.exp(pre * pre * -0.5) * (1.0 / math.sqrt(2.0 * math.pi))
+    return (pre * phi).astype(jnp.bfloat16), (act_grad * (phi + pre * bell)).astype(jnp.bfloat16)
+
+
+def times_gate(gate, result):
+    gate_wide = jnp.concatenate([gate] * (result.shape[1] // 128), axis=1)
+    return (gate_wide * result).astype(jnp.bfloat16)
+
+
+def slot_lanes(slots, count, offset, step):
+    return [slot * count + offset + step for slot in range(slots)]
+
+
+def moe_full_kernel(offset, chunk, slots, rows_ref, gate_rows_ref, cols_ref, *rest):
+    u_refs, g_refs, rest = rest[:slots], rest[slots : 2 * slots], rest[2 * slots :]
+    inner_ref, outer_ref, y_ref, du_ref, grads_ref = rest[:5]
+    x_buf, dy_buf, act_buf, dpre_buf, gate_buf, y_buf, du_buf = rest[5:]
+    step = pl.program_id(0)
+    width = inner_ref.shape[1]
+    dispatch(rows_ref, gate_rows_ref, u_refs, g_refs, offset + step, x_buf, dy_buf, gate_buf)
 
     def part(index, carry):
-        at = pl.multiple_of(index * chunk, chunk)
-        span = pl.ds(at, chunk)
+        span = pl.ds(pl.multiple_of(index * chunk, chunk), chunk)
         rows_in = x_buf[...]
         rows_grad = dy_buf[...]
-        pre = mxu(rows_in, inner_ref[span, :], NT)
-        act_grad = mxu(rows_grad, outer_ref[span, :], NT)
-        phi = 0.5 + 0.5 * lax.erf(pre * math.sqrt(0.5))
-        bell = jnp.exp(pre * pre * -0.5) * (1.0 / math.sqrt(2.0 * math.pi))
-        act = (pre * phi).astype(jnp.bfloat16)
-        dpre = (act_grad * (phi + pre * bell)).astype(jnp.bfloat16)
+        act, dpre = gelu_pair(mxu(rows_in, inner_ref[span, :], NT), mxu(rows_grad, outer_ref[span, :], NT))
         act_buf[:, span] = act
         dpre_buf[:, span] = dpre
         grads_ref[span, :width] = mxu(dpre, rows_in, TN).astype(jnp.bfloat16)
         grads_ref[span, width:] = mxu(act, rows_grad, TN).astype(jnp.bfloat16)
         return carry
 
-    lax.fori_loop(0, units // chunk, part, 0)
-    result = mxu(act_buf[...], outer_ref[...])
-    gate_wide = jnp.concatenate([gate_buf[...]] * (width // 128), axis=1)
-    x_buf[...] = (gate_wide * result).astype(jnp.bfloat16)
+    lax.fori_loop(0, inner_ref.shape[0] // chunk, part, 0)
+    x_buf[...] = times_gate(gate_buf[...], mxu(act_buf[...], outer_ref[...]))
     dy_buf[...] = mxu(dpre_buf[...], inner_ref[...]).astype(jnp.bfloat16)
-
-    if has_start:
-        @pl.when(step == 0)
-        def _():
-            copy = pltpu.make_async_copy(start_ref, sum_buf, rest[6])
-            copy.start()
-            copy.wait()
-
-    for slot in range(slots):
-        lane = slot * count + offset + step
-        wide = lax.broadcasted_iota(jnp.int32, (tokens, 128), 1) == lane
-        column = jnp.sum(jnp.where(wide, cols_ref[...], 0), axis=1, keepdims=True)
-        same = lax.broadcasted_iota(jnp.int32, (tokens, CAP), 1) == column
-        spread = jnp.where(same, 1.0, 0.0).astype(jnp.bfloat16)
-        span = pl.ds(slot * CAP, CAP)
-        for side, buf in enumerate((x_buf, dy_buf)):
-            add = mxu(spread, buf[span, :])
-            lanes = slice(side * width, (side + 1) * width)
-            if has_start:
-                sum_buf[slot, :, lanes] = sum_buf[slot, :, lanes] + add
-            else:
-                first = jnp.where(step == 0, 0.0, 1.0)
-                old = sum_buf[slot, :, lanes]
-                sum_buf[slot, :, lanes] = jnp.where(first > 0.5, old, 0.0) + add
+    lanes = slot_lanes(slots, rows_ref.shape[1], offset, step)
+    combine(cols_ref, lanes, step, x_buf, y_buf, True)
+    combine(cols_ref, lanes, step, dy_buf, du_buf, True)
 
     @pl.when(step == pl.num_programs(0) - 1)
     def _():
-        if last:
-            for slot in range(slots):
-                sums_refs[slot][...] = sum_buf[slot, :, width:].astype(jnp.bfloat16)
-                sums_refs[slots + slot][...] = sum_buf[slot, :, :width].astype(jnp.bfloat16)
-        else:
-            sums_refs[0][...] = sum_buf[...]
-
-
-def moe(rows, gate_rows, cols, u_all, g_all, weights, offset, start, last):
-    slots, count, tokens = rows.shape
-    width = u_all[0].shape[1]
-    units = weights.shape[0]
-    steps = weights.shape[1] // (2 * width)
-    pairs = slots * CAP
-    once = pl.Buffered(1)
-
-    def whole(array):
-        return pl.BlockSpec(array.shape, lambda e: (0,) * array.ndim, pipeline_mode=once)
-
-    sums_shape = (slots, tokens, 2 * width)
-    scratch = [
-        pltpu.VMEM((pairs, width), jnp.bfloat16),
-        pltpu.VMEM((pairs, width), jnp.bfloat16),
-        pltpu.VMEM((pairs, units), jnp.bfloat16),
-        pltpu.VMEM((pairs, units), jnp.bfloat16),
-        pltpu.VMEM((pairs, 128), jnp.float32),
-        pltpu.VMEM(sums_shape, jnp.float32),
-    ]
-    operands = [rows, gate_rows, cols, *u_all, *g_all, weights, weights]
-    in_specs = [whole(a) for a in operands[:-2]] + [
-        pl.BlockSpec((units, width), lambda e: (0, 2 * e)),
-        pl.BlockSpec((units, width), lambda e: (0, 2 * e + 1)),
-    ]
-    if start is not None:
-        operands.append(start)
-        in_specs.append(pl.BlockSpec(memory_space=pl.ANY))
-        scratch.append(pltpu.SemaphoreType.DMA)
-    if last:
-        sums_out = (jax.ShapeDtypeStruct((tokens, width), jnp.bfloat16),) * (2 * slots)
-    else:
-        sums_out = (jax.ShapeDtypeStruct(sums_shape, jnp.float32),)
-    flops = steps * pairs * width * (12 * units + 8 * tokens)
+        y_ref[...] = y_buf[...]
+        du_ref[...] = du_buf[...]
+
+
+def fetch(start_ref, sum_buf, sem):
+    @pl.when(pl.program_id(0) == 0)
+    def _():
+        copy = pltpu.make_async_copy(start_ref, sum_buf, sem)
+        copy.start()
+        copy.wait()
+
+
+def finish_sums(out_refs, sum_buf):
+    @pl.when(pl.program_id(0) == pl.num_programs(0) - 1)
+    def _():
+        for slot, ref in enumerate(out_refs):
+            ref[...] = sum_buf[slot].astype(jnp.bfloat16)
+
+
+def moe_front_kernel(offset, chunk, slots, rows_ref, gate_rows_ref, cols_ref, *rest):
+    u_refs, g_refs, rest = rest[:slots], rest[slots : 2 * slots], rest[2 * slots :]
+    inner_ref, outer_ref, start_ref, rest = rest[0], rest[1], rest[2], rest[3:]
+    du_refs, rest = rest[:slots], rest[slots:]
+    x_ref, dy_ref, gate_ref, act_ref, dpre_ref, buf, sum_buf, sem = rest
+    step = pl.program_id(0)
+    fetch(start_ref, sum_buf, sem)
+    dispatch(rows_ref, gate_rows_ref, u_refs, g_refs, offset + step, x_ref, dy_ref, gate_ref)
+
+    def part(index, carry):
+        span = pl.ds(pl.multiple_of(index * chunk, chunk), chunk)
+        act, dpre = gelu_pair(mxu(x_ref[...], inner_ref[span, :], NT), mxu(dy_ref[...], outer_ref[span, :], NT))
+        act_ref[:, span] = act
+        dpre_ref[:, span] = dpre
+        return carry
+
+    lax.fori_loop(0, inner_ref.shape[0] // chunk, part, 0)
+    buf[...] = mxu(dpre_ref[...], inner_ref[...]).astype(jnp.bfloat16)
+    combine(cols_ref, slot_lanes(slots, rows_ref.shape[1], offset, step), step, buf, sum_buf, False)
+    finish_sums(du_refs, sum_buf)
+
+
+def moe_rest_kernel(offset, chunk, slots, count, cols_ref, x_ref, dy_ref, gate_ref, act_ref, dpre_ref, *rest):
+    outer_ref, start_ref, rest = rest[0], rest[1], rest[2:]
+    y_refs, rest = rest[:slots], rest[slots:]
+    grads_ref, buf, sum_buf, sem = rest
+    step = pl.program_id(0)
+    width = x_ref.shape[1]
+    fetch(start_ref, sum_buf, sem)
+
+    def part(index, carry):
+        span = pl.ds(pl.multiple_of(index * chunk, chunk), chunk)
+        grads_ref[span, :width] = mxu(dpre_ref[:, span], x_ref[...], TN).astype(jnp.bfloat16)
+        grads_ref[span, width:] = mxu(act_ref[:, span], dy_ref[...], TN).astype(jnp.bfloat16)
+        return carry
+
+    lax.fori_loop(0, outer_ref.shape[0] // chunk, part, 0)
+    buf[...] = times_gate(gate_ref[...], mxu(act_ref[...], outer_ref[...]))
+    combine(cols_ref, slot_lanes(slots, count, offset, step), step, buf, sum_buf, False)
+    finish_sums(y_refs, sum_buf)
+
+
+def once(array):
+    return pl.BlockSpec(array.shape, lambda e: (0,) * len(array.shape), pipeline_mode=pl.Buffered(1))
+
+
+def moe_call(kernel, steps, operands, in_specs, outs, out_specs, scratch, flops):
     return pl.pallas_call(
-        functools.partial(moe_kernel, offset, count, start is not None, last, units // 3),
-        out_shape=sums_out + (jax.ShapeDtypeStruct((units, steps * 2 * width), jnp.bfloat16),),
+        kernel,
+        out_shape=tuple(outs),
         grid_spec=pltpu.PrefetchScalarGridSpec(
-            num_scalar_prefetch=0,
-            grid=(steps,),
-            in_specs=in_specs,
-            out_specs=tuple(whole(s) for s in sums_out)
-            + (pl.BlockSpec((units, 2 * width), lambda e: (0, e)),),
+            num_scalar_prefetch=0, grid=(steps,), in_specs=in_specs, out_specs=tuple(out_specs),
             scratch_shapes=scratch,
         ),
         compiler_params=pltpu.CompilerParams(
             dimension_semantics=("arbitrary",), vmem_limit_bytes=VMEM_MOST
         ),
         cost_estimate=pl.CostEstimate(flops=flops, bytes_accessed=40 << 20, transcendentals=0),
-        name="moe",
     )(*operands)
+
+
+def moe_sizes(slots, tokens, weights, width):
+    units = weights.shape[0]
+    steps = weights.shape[1] // (2 * width)
+    pairs = slots * CAP
+    low, full = jnp.bfloat16, jnp.float32
+    sums = jax.ShapeDtypeStruct((slots, tokens, width), full)
+    part = jax.ShapeDtypeStruct((tokens, width), low)
+    inner = pl.BlockSpec((units, width), lambda e: (0, 2 * e))
+    outer = pl.BlockSpec((units, width), lambda e: (0, 2 * e + 1))
+    grads = jax.ShapeDtypeStruct((units, steps * 2 * width), low)
+    grads_spec = pl.BlockSpec((units, 2 * width), lambda e: (0, e))
+    return units, steps, pairs, sums, part, inner, outer, grads, grads_spec
+
+
+def moe_full(rows, gate_rows, cols, u_all, g_all, weights, offset):
+    slots, _, tokens = rows.shape
+    width = u_all[0].shape[1]
+    units, steps, pairs, sums, _, inner, outer, grads, grads_spec = moe_sizes(slots, tokens, weights, width)
+    operands = [rows, gate_rows, cols, *u_all, *g_all, weights, weights]
+    low, full = jnp.bfloat16, jnp.float32
+    scratch = [pltpu.VMEM((pairs, width), low)] * 2 + [pltpu.VMEM((pairs, units), low)] * 2
+    scratch += [pltpu.VMEM((pairs, 128), full)] + [pltpu.VMEM(sums.shape, full)] * 2
+    return moe_call(
+        functools.partial(moe_full_kernel, offset, units // 3, slots), steps, operands,
+        [once(a) for a in operands[:-2]] + [inner, outer],
+        [sums, sums, grads], [once(sums), once(sums), grads_spec], scratch,
+        steps * pairs * width * (12 * units + 8 * tokens),
+    )
+
+
+def moe_front(rows, gate_rows, cols, u_all, g_all, weights, offset, start):
+    slots, _, tokens = rows.shape
+    width = u_all[0].shape[1]
+    units, steps, pairs, sums, part, inner, outer, _, _ = moe_sizes(slots, tokens, weights, width)
+    operands = [rows, gate_rows, cols, *u_all, *g_all, weights, weights, start]
+    low, full = jnp.bfloat16, jnp.float32
+    kept = [((pairs, width), low), ((pairs, width), low), ((pairs, 128), full)]
+    kept += [((pairs, units), low), ((pairs, units), low)]
+    outs = [part] * slots + [jax.ShapeDtypeStruct((steps,) + shape, kind) for shape, kind in kept]
+    specs = [once(part)] * slots
+    specs += [pl.BlockSpec((pl.Squeezed(),) + shape, lambda e: (e, 0, 0)) for shape, _ in kept]
+    return moe_call(
+        functools.partial(moe_front_kernel, offset, units // 3, slots), steps, operands,
+        [once(a) for a in operands[:-3]] + [inner, outer, pl.BlockSpec(memory_space=pl.ANY)],
+        outs, specs,
+        [pltpu.VMEM((pairs, width), low), pltpu.VMEM(sums.shape, full), pltpu.SemaphoreType.DMA],
+        steps * pairs * width * (6 * units + 6 * tokens),
+    )
+
+
+def moe_rest(cols, kept, weights, offset, count, start):
+    slots, tokens, width = start.shape
+    units, steps, pairs, sums, part, _, outer, grads, grads_spec = moe_sizes(slots, tokens, weights, width)
+    operands = [cols, *kept, weights, start]
+    low, full = jnp.bfloat16, jnp.float32
+    in_specs = [once(cols)]
+    in_specs += [pl.BlockSpec((pl.Squeezed(),) + a.shape[1:], lambda e: (e, 0, 0)) for a in kept]
+    return moe_call(
+        functools.partial(moe_rest_kernel, offset, units // 3, slots, count), steps, operands,
+        in_specs + [outer, pl.BlockSpec(memory_space=pl.ANY)],
+        [part] * slots + [grads], [once(part)] * slots + [grads_spec],
+        [pltpu.VMEM((pairs, width), low), pltpu.VMEM(sums.shape, full), pltpu.SemaphoreType.DMA],
+        steps * pairs * width * (6 * units + 2 * tokens),
+    )
 
 
 def unit_rows(values):
@@ -589,12 +668,12 @@
     *saved, moe_in = attend(marks, patches, norm_params, attn_qkv, attn_proj, segments, task_row)
     hidden_one = saved[-1]
     u_all = to_peers([moe_in] * groups, groups)
-    sums, grads_first = moe(rows, gate_rows, cols, u_all, g_all, weights[0], 0, None, False)
-    *parts, grads_second = moe(
-        rows, gate_rows, cols, u_all, g_all, weights[1], local_count // 2, sums, True
-    )
-    du_parts = to_peers(parts[:groups], groups)
-    y_parts = to_peers(parts[groups:], groups)
+    second = local_count // 2
+    y_sums, du_sums, grads_first = moe_full(rows, gate_rows, cols, u_all, g_all, weights[0], 0)
+    outs = moe_front(rows, gate_rows, cols, u_all, g_all, weights[1], second, du_sums)
+    du_parts = to_peers(outs[:groups], groups)
+    *y_own, grads_second = moe_rest(cols, outs[groups:], weights[1], second, local_count, y_sums)
+    y_parts = to_peers(y_own, groups)
     moe_sum = sum(p.astype(jnp.float32) for p in y_parts)
     block_out = (hidden_one + moe_sum).astype(jnp.bfloat16)
     owned = []

time: 436 us -> 401 us (0.920)
  waiting for transfers between devices: 157 us -> 109 us
  Pallas kernels: 183 us -> 198 us
  starting transfers between devices: 37.6 us -> 32.2 us
    ppermute x15, waiting for transfers between devices: 117 us -> 68.3 us  [to_peers(): lax.ppermute(arrays[k], 'expert', [(i, i ^ k) for i in range(groups)])]
    pallas_call x2 -> x3, Pallas kernels: 108 us -> 122 us  [moe_call(): pl.pallas_call(kernel, out_shape=tuple(outs), grid_spec=pltpu.PrefetchSca...]
  transfers between devices with their start and end apart: 29 -> 29, of which waited for: 18 -> 14; matrix products, arithmetic and copies ran while one was open for 4% -> 4% of each run, Pallas kernels for 30% -> 50%
where the time goes in v5:
time: 401 us; the launch traced here: 394 us
  Pallas kernels  198 us (49%)
  waiting for transfers between devices  109 us (27%)
  starting transfers between devices  32.2 us (8%)
  other arithmetic  21.4 us (5%)
  local copies, waits for them, and re-layouts  19.6 us (5%)
  between operations  14.6 us (4%)
    pallas_call x3, Pallas kernels, moe_call(): pl.pallas_call(kernel, out_shape=tuple(outs), grid_spec=pltpu.PrefetchSca...  122 us
    ppermute x15, waiting for transfers between devices, to_peers(): lax.ppermute(arrays[k], 'expert', [(i, i ^ k) for i in range(groups)])  68.3 us
    pallas_call x1, Pallas kernels, attend_back(): pl.pallas_call(functools.partial(attend_back_kernel, block, len(du_parts)...  38.7 us
    pallas_call x1, Pallas kernels, attend(): pl.pallas_call(functools.partial(attend_kernel, block), out_shape=(jax.Sh...  34.2 us
    ppermute x5, waiting for transfers between devices, butterfly_sum(): got = lax.ppermute(send, axis, [(i, i ^ bit) for i in range(size)])  22 us
    ppermute x15, starting transfers between devices, to_peers(): lax.ppermute(arrays[k], 'expert', [(i, i ^ k) for i in range(groups)])  18.7 us
    ppermute x5, waiting for transfers between devices, butterfly_sum(): got = lax.ppermute(value, axis, [(i, i ^ bit) for i in range(size)])  17.5 us
    add x4, other arithmetic, nesterov(): average_new = AVERAGE_DECAY * average + (1.0 - AVERAGE_DECAY) * weight_new  10.2 us
  transfers between devices with their start and end apart: 29, of which 14 were waited for; matrix products, arithmetic and copies ran while one was open for 4% of the time, Pallas kernels for 50%

profile of v5, /device:TPU:0, one launch (start us, length us, event | category | flops | bytes accessed | tf_op | source)
XLA Modules:
  0.0 394.0 jit_solution(7351860517025208617)
XLA Ops:
  7.2 2.0 convert_bitcast_fusion
  9.3 0.8 pad_maximum_fusion.1
  10.1 1.8 copy.43
  11.9 0.9 convert_element_type.72
  12.9 1.1 fusion.5
  14.1 0.7 all-gather.3.cloned.1.call-update
  14.9 3.1 collective-permute-start.1
  17.9 1.5 collective-permute-start
  19.5 2.9 collective-permute-start.8
  22.4 0.5 collective-permute-start.7
  22.9 34.2 %attend.1 = (bf16[1024,1152]{1,0:T(8,128)(2,1)}, bf16[384,1024]{1,0:T(8,128)(2,1)S(1)}, bf16[1024,384]{1,0:T(8,128)(2,1)S(1)}, bf16[384,1024]{1,0:T(8,128)(2,1)S...) custom-call(s32[1024]{0:T(1024)S(1)} %bitcast.31, ...), custom_call_target="tpu_custom_call" | custom-call | flops 8589934592 | bytes 12582912 | tf_op jit(solution)/shard_map/attend/pallas_call | solution.py:417
  57.2 1.1 copy-done
  58.3 0.9 copy-done.14
  59.2 0.9 copy-done.15
  60.1 0.9 copy-done.16
  61.0 0.6 copy-done.17
  61.7 3.0 collective-permute-start.5
  65.3 0.7 copy-done.39
  66.0 0.7 fusion.6
  66.7 2.2 route.1
  68.9 13.2 %collective-permute-done.6.rest_5_ = bf16[1024,384]{1,0:T(8,128)(2,1)S(1)} collective-permute-done((bf16[1024,384]{1,0:T(8,128)(2,1)S(1)}, bf16[1024,384]{1,0:T(8,128)(2,1)S(1)}, u32[]{:S(2)}, u32[]{:S(2)}) %collective-permute-start.6) | collective-permute-done | bytes 786464 | tf_op jit(solution)/shard_map/ppermute | solution.py:573
  82.0 18.0 %collective-permute-done.5.rest_3_ = bf16[1024,384]{1,0:T(8,128)(2,1)} collective-permute-done((bf16[1024,384]{1,0:T(8,128)(2,1)S(1)}, bf16[1024,384]{1,0:T(8,128)(2,1)}, u32[]{:S(2)}, u32[]{:S(2)}) %collective-permute-start.5) | collective-permute-done | bytes 786464 | tf_op jit(solution)/shard_map/ppermute | solution.py:573
  100.0 13.3 %collective-permute-done.3.rest_1_ = bf16[1024,384]{1,0:T(8,128)(2,1)} collective-permute-done((bf16[1024,384]{1,0:T(8,128)(2,1)S(1)}, bf16[1024,384]{1,0:T(8,128)(2,1)}, u32[]{:S(2)}, u32[]{:S(2)}) %collective-permute-start.3) | collective-permute-done | bytes 786464 | tf_op jit(solution)/shard_map/ppermute | solution.py:573
  113.3 52.9 %shard_map.340 = (f32[4,1024,384]{2,1,0:T(8,128)}, f32[4,1024,384]{2,1,0:T(8,128)}, bf16[1536,1536]{1,0:T(8,128)(2,1)}) custom-call(s32[4,4,1024]{2,1,0:T(4,128)} %get-tuple-element.49.rows_ref, f32[4,4,1024]{2,1,0:T(4,128)} %get-tuple-element.50.gate_rows_ref, s32[1024,128]{1,0:T(8,128)} %get-tuple-element.48.cols_ref, bf16[1024,384]{1,0:T(8,128)(2,1)} %copy-done.9, ...), custom_call_target="tpu_custom_call" | custom-call | flops 26172456960 | bytes 41943040 | tf_op jit(solution)/shard_map/pallas_call | solution.py:222
  166.3 0.6 copy-done.31
  167.1 0.6 pad.4.rest_4_
  167.7 38.0 %shard_map.341 = (bf16[1024,384]{1,0:T(8,128)(2,1)}, bf16[1024,384]{1,0:T(8,128)(2,1)}, bf16[1024,384]{1,0:T(8,128)(2,1)}, bf16[1024,384]{1,0:T(8,128)(2,1)}, bf...) custom-call(s32[4,4,1024]{2,1,0:T(4,128)} %get-tuple-element.49.rows, ...), custom_call_target="tpu_custom_call" | custom-call | flops 15099494400 | bytes 41943040 | tf_op jit(solution)/shard_map/pallas_call | solution.py:222
  205.8 1.9 collective-permute-start.13
  207.8 1.5 collective-permute-start.14
  209.3 31.5 %shard_map.342 = (bf16[1024,384]{1,0:T(8,128)(2,1)}, bf16[1024,384]{1,0:T(8,128)(2,1)}, bf16[1024,384]{1,0:T(8,128)(2,1)}, bf16[1024,384]{1,0:T(8,128)(2,1)}, bf16[1536,1536]{1,0:T(8,128)(2,1)}) custom-call(s32[1024,128]{1,0:T(8,128)} %get-tuple-element.48.cols_ref, bf16[2,1280,384]{2,1,0:T(8,128)(2,1)} %get-tuple-element.53.x_ref, ...), custom_call_target="tpu_custom_call" | custom-call | flops 11072962560 | bytes 41943040 | tf_op jit(solution)/shard_map/pallas_call | solution.py:222
  240.9 0.9 copy-done.3
  242.2 38.7 %attend_back.1 = (f32[1024,384]{1,0:T(8,128)}, f32[768,896]{1,0:T(8,128)}) custom-call(s32[1024]{0:T(1024)S(1)} %bitcast.32, bf16[1024,384]{1,0:T(8,128)(2,1)S(1)} %copy-done.8, f32[6,384]{1,0:T(8,128)S(1)} %copy-done.5, f32[384,1152]{1,0:T(8,128)} %qkv_ref.3, f32[384,384]{1,0:T(8,128)S(1)} %copy-done.3, s32[1,1024]{1,0:T(1,128)S(1)} %copy-done.11, ...), custom_call_target="tpu_custom_call" | custom-call | flops 25769803776 | bytes 25165824 | tf_op jit(solution)/shard_map/attend_back/pallas_call | solution.py:549
  280.9 1.9 select_convert_fusion
  282.9 2.2 collective-permute-done.15
  285.1 2.0 convert_add_fusion
  287.3 10.0 %collective-permute-done.16 = bf16[192,896]{1,0:T(8,128)(2,1)S(1)} collective-permute-done((bf16[192,896]{1,0:T(8,128)(2,1)S(1)}, bf16[192,896]{1,0:T(8,128)(2,1)S(1)}, u32[]{:S(2)}, u32[]{:S(2)}) %collective-permute-start.16) | collective-permute-done | bytes 344096 | tf_op jit(solution)/shard_map/ppermute | solution.py:597
  297.5 1.6 collective-permute-start.17
  299.1 4.1 %collective-permute-done.17 = bf16[96,896]{1,0:T(8,128)(2,1)S(1)} collective-permute-done((bf16[96,896]{1,0:T(8,128)(2,1)S(1)}, bf16[96,896]{1,0:T(8,128)(2,1)S(1)}, u32[]{:S(2)}, u32[]{:S(2)}) %collective-permute-start.17) | collective-permute-done | bytes 172064 | tf_op jit(solution)/shard_map/ppermute | solution.py:597
  303.2 1.5 collective-permute-start.18
  304.8 3.0 collective-permute-done.18
  307.9 2.6 collective-permute-start.19
  310.4 2.7 collective-permute-done.19
  313.1 2.7 collective-permute-start.20
  315.9 2.3 collective-permute-done.20
  318.2 2.6 collective-permute-start.21
  320.7 2.5 collective-permute-done.21
  323.3 1.6 collective-permute-start.22
  324.8 5.7 %collective-permute-done.22 = bf16[96,896]{1,0:T(8,128)(2,1)S(1)} collective-permute-done((bf16[96,896]{1,0:T(8,128)(2,1)S(1)}, bf16[96,896]{1,0:T(8,128)(2,1)S(1)}, u32[]{:S(2)}, u32[]{:S(2)}) %collective-permute-start.22) | collective-permute-done | bytes 172064 | tf_op jit(solution)/shard_map/ppermute | solution.py:605
  331.1 1.7 collective-permute-start.9
  332.8 1.5 collective-permute-start.10
  334.6 7.1 %collective-permute-done.23 = bf16[192,896]{1,0:T(8,128)(2,1)S(1)} collective-permute-done((bf16[192,896]{1,0:T(8,128)(2,1)S(1)}, bf16[192,896]{1,0:T(8,128)(2,1)S(1)}, u32[]{:S(2)}, u32[]{:S(2)}) %collective-permute-start.23) | collective-permute-done | bytes 344096 | tf_op jit(solution)/shard_map/ppermute | solution.py:605
  342.0 14.5 %collective-permute-done.9 = bf16[1024,384]{1,0:T(8,128)(2,1)S(1)} collective-permute-done((bf16[1024,384]{1,0:T(8,128)(2,1)S(1)}, bf16[1024,384]{1,0:T(8,128)(2,1)S(1)}, u32[]{:S(2)}, u32[]{:S(2)}) %collective-permute-start.9) | collective-permute-done | bytes 786464 | tf_op jit(solution)/shard_map/ppermute | solution.py:573
  356.5 9.4 %collective-permute-done.11 = bf16[1024,384]{1,0:T(8,128)(2,1)S(1)} collective-permute-done((bf16[1024,384]{1,0:T(8,128)(2,1)S(1)}, bf16[1024,384]{1,0:T(8,128)(2,1)S(1)}, u32[]{:S(2)}, u32[]{:S(2)}) %collective-permute-start.11) | collective-permute-done | bytes 786464 | tf_op jit(solution)/shard_map/ppermute | solution.py:573
  365.9 1.3 add_convert_fusion
  368.0 0.5 broadcast_multiply_fusion
  368.7 0.6 multiply_add_fusion.7
  369.3 1.4 multiply_add_fusion.6
  370.7 0.8 copy-done.21
  371.5 0.5 copy-done.22
  372.0 2.8 multiply_add_fusion
  374.9 1.9 concatenate.40
  377.3 2.1 concatenate.41
  379.9 1.1 maximum_convert_fusion.1
  381.9 5.4 %multiply_add_fusion.2 = (f32[192,4,384]{2,1,0:T(4,128)}, f32[192,4,384]{2,1,0:T(4,128)}, f32[192,4,384]{2,1,0:T(4,128)}, f32[192,4,384]{2,1,0:T(4,128)}, f32[192,4,384]{2,1,0:T(4,128)}, /*index=5*/f32[192,4,384]{2,1,0:T(4,128)}) fusion(f32[192,4,384]{2,1,0:T(4,128)S(1)} %copy-done.24, f32[192,4,384]{2,1,0:T(4,128)S(1)} %copy-done.19, ...), kind=kLoop, calls=%fused_computation.12 | loop fusion | flops 5308416 | bytes 16515072 | tf_op jit(solution)/shard_map/add | solution.py:615
  (135 shorter events, 6.2 us)
Async XLA Ops:
  7.2 106.1 %all-gather.5.cloned.1.call-start = ((), (), s32[]{:S(2)}) async-start(), calls=%async_computation.3 | async-start | bytes 5308416 | tf_op jit(solution)/shard_map/all_gather | solution.py:651
  12.8 2.0 copy-start.30
  12.9 2.0 copy-start.32
  12.9 10.0 %copy-start.2 = (f32[384,384]{1,0:T(8,128)S(1)}, f32[384,384]{1,0:T(8,128)}, u32[]{:S(2)}) copy-start(f32[384,384]{1,0:T(8,128)} %proj_ref.3) | copy-start | bytes 1769476
  12.9 10.0 %copy-start.4 = (f32[6,384]{1,0:T(8,128)S(1)}, f32[6,384]{1,0:T(8,128)}, u32[]{:S(2)}) copy-start(f32[6,384]{1,0:T(8,128)} %norm_ref.3) | copy-start | bytes 27652
  12.9 10.0 %copy-start.7 = (bf16[1024,384]{1,0:T(8,128)(2,1)S(1)}, bf16[1024,384]{1,0:T(8,128)(2,1)}, u32[]{:S(2)}) copy-start(bf16[1024,384]{1,0:T(8,128)(2,1)} %x_ref.3) | copy-start | bytes 2359300
  12.9 10.0 %copy-start.10 = (s32[1,1024]{1,0:T(1,128)S(1)}, s32[1,1024]{1,0:T(1,128)}, u32[]{:S(2)}) copy-start(s32[1,1024]{1,0:T(1,128)} %seg_ref.3) | copy-start | bytes 12292
  12.9 10.0 %copy-start.12 = (s32[1024]{0:T(1024)S(1)}, s32[1024]{0:T(1024)}, u32[]{:S(2)}) copy-start(s32[1024]{0:T(1024)} %param.25) | copy-start | bytes 12292
  14.0 153.7 %all-gather.3.cloned.1.call-start = ((), (), s32[]{:S(2)}) async-start(), calls=%async_computation.2 | async-start | bytes 5308416 | tf_op jit(solution)/shard_map/all_gather | solution.py:652
  14.8 360.1 %reduce-scatter.3.cloned.1.call-start = ((), (), s32[]{:S(2)}) async-start(), calls=%async_computation.4 | async-start | bytes 5308416 | tf_op jit(solution)/shard_map/reduce_scatter | solution.py:681
  14.9 46.7 %collective-permute-start.1 = (f32[8,1024]{1,0:T(8,128)S(1)}, f32[8,1024]{1,0:T(8,128)S(1)}, u32[]{:S(2)}, u32[]{:S(2)}) collective-permute-start(f32[8,1024]{1,0:T(8,128)S(1)} %get-tuple-element.114), channel_id=1, source_target_pairs={{0,16},{8,24},{16,0},{24,8},{1,17},{9,25},{17,1},{25,9},{2,18},{10... | collective-permute-start | bytes 98312 | tf_op jit(solution)/shard_map/ppermute | solution.py:573
  17.9 43.7 %collective-permute-start = (f32[8,1024]{1,0:T(8,128)S(1)}, f32[8,1024]{1,0:T(8,128)S(1)}, u32[]{:S(2)}, u32[]{:S(2)}) collective-permute-start(f32[8,1024]{1,0:T(8,128)S(1)} %get-tuple-element.114), channel_id=1, source_target_pairs={{0,8},{8,0},{16,24},{24,16},{1,9},{9,1},{17,25},{25,17},{2,10},{10... | collective-permute-start | bytes 98312 | tf_op jit(solution)/shard_map/ppermute | solution.py:573
  19.4 45.2 %collective-permute-start.2 = (f32[8,1024]{1,0:T(8,128)S(1)}, f32[8,1024]{1,0:T(8,128)S(1)}, u32[]{:S(2)}, u32[]{:S(2)}) collective-permute-start(f32[8,1024]{1,0:T(8,128)S(1)} %get-tuple-element.114), channel_id=1, source_target_pairs={{0,24},{8,16},{16,8},{24,0},{1,25},{9,17},{17,9},{25,1},{2,26},{10... | collective-permute-start | bytes 98312 | tf_op jit(solution)/shard_map/ppermute | solution.py:573
  19.5 45.6 %collective-permute-start.8 = (bf16[1024,384]{1,0:T(8,128)(2,1)}, bf16[1024,384]{1,0:T(8,128)(2,1)S(1)}, u32[]{:S(2)}, u32[]{:S(2)}) collective-permute-start(bf16[1024,384]{1,0:T(8,128)(2,1)} %out_grad_ref.1), channel_id=1, source_target_pairs={{0,24},{8,16},{16,8},{24,0},{1,25},{9,17},{17,9},{25,1},{2,26},{10... | collective-permute-start | bytes 2359304 | tf_op jit(solution)/shard_map/ppermute | solution.py:573
  22.4 46.5 %collective-permute-start.7 = (bf16[1024,384]{1,0:T(8,128)(2,1)}, bf16[1024,384]{1,0:T(8,128)(2,1)}, u32[]{:S(2)}, u32[]{:S(2)}) collective-permute-start(bf16[1024,384]{1,0:T(8,128)(2,1)} %out_grad_ref.1), channel_id=1, source_target_pairs={{0,16},{8,24},{16,0},{24,8},{1,17},{9,25},{17,1},{25,9},{2,18},{10... | collective-permute-start | bytes 2359304 | tf_op jit(solution)/shard_map/ppermute | solution.py:573
  22.9 38.7 %copy-start.35 = (bf16[1024,384]{1,0:T(8,128)(2,1)S(1)}, bf16[1024,384]{1,0:T(8,128)(2,1)}, u32[]{:S(2)}) copy-start(bf16[1024,384]{1,0:T(8,128)(2,1)} %out_grad_ref.1) | copy-start | bytes 2359300
  57.2 1.1 copy-start
  59.2 0.9 copy-start.15
  60.1 0.9 copy-start.16
  61.6 3.6 copy-start.9
  61.6 20.5 %collective-permute-start.6 = (bf16[1024,384]{1,0:T(8,128)(2,1)S(1)}, bf16[1024,384]{1,0:T(8,128)(2,1)S(1)}, u32[]{:S(2)}, u32[]{:S(2)}) collective-permute-start(bf16[1024,384]{1,0:T(8,128)(2,1)S(1)} %copy-done.35), channel_id=1, source_target_pairs={{0,8},{8,0},{16,24},{24,16},{1,9},{9,1},{17,25},{25,17},{2,10},{10... | collective-permute-start | bytes 2359304 | tf_op jit(solution)/shard_map/ppermute | solution.py:573
  61.7 38.4 %collective-permute-start.5 = (bf16[1024,384]{1,0:T(8,128)(2,1)S(1)}, bf16[1024,384]{1,0:T(8,128)(2,1)}, u32[]{:S(2)}, u32[]{:S(2)}) collective-permute-start(bf16[1024,384]{1,0:T(8,128)(2,1)S(1)} %get-tuple-element.51.rest_0_), channel_id=1, source_target_pairs={{0,24},{8,16},{16,8},{24,0},{1,25},{9,17},{17,9},{25,1},{2,26},{10... | collective-permute-start | bytes 2359304 | tf_op jit(solution)/shard_map/ppermute | solution.py:573
  64.6 35.4 %collective-permute-start.4 = (bf16[1024,384]{1,0:T(8,128)(2,1)S(1)}, bf16[1024,384]{1,0:T(8,128)(2,1)}, u32[]{:S(2)}, u32[]{:S(2)}) collective-permute-start(bf16[1024,384]{1,0:T(8,128)(2,1)S(1)} %get-tuple-element.51.rest_0_), channel_id=1, source_target_pairs={{0,16},{8,24},{16,0},{24,8},{1,17},{9,25},{17,1},{25,9},{2,18},{10... | collective-permute-start | bytes 2359304 | tf_op jit(solution)/shard_map/ppermute | solution.py:573
  65.1 48.1 %collective-permute-start.3 = (bf16[1024,384]{1,0:T(8,128)(2,1)S(1)}, bf16[1024,384]{1,0:T(8,128)(2,1)}, u32[]{:S(2)}, u32[]{:S(2)}) collective-permute-start(bf16[1024,384]{1,0:T(8,128)(2,1)S(1)} %get-tuple-element.51.rest_0_), channel_id=1, source_target_pairs={{0,8},{8,0},{16,24},{24,16},{1,9},{9,1},{17,25},{25,17},{2,10},{10... | collective-permute-start | bytes 2359304 | tf_op jit(solution)/shard_map/ppermute | solution.py:573
  82.0 31.2 %copy-start.40 = (bf16[1024,384]{1,0:T(8,128)(2,1)}, bf16[1024,384]{1,0:T(8,128)(2,1)S(1)}, u32[]{:S(2)}) copy-start(bf16[1024,384]{1,0:T(8,128)(2,1)S(1)} %collective-permute-done.6.rest_5_) | copy-start | bytes 2359300
  166.3 211.0 %reduce-scatter.5.cloned.1.call-start = ((), (), s32[]{:S(2)}) async-start(), calls=%async_computation.5 | async-start | bytes 5308416 | tf_op jit(solution)/shard_map/reduce_scatter | solution.py:681
  205.7 35.2 %collective-permute-start.12 = (bf16[1024,384]{1,0:T(8,128)(2,1)}, bf16[1024,384]{1,0:T(8,128)(2,1)}, u32[]{:S(2)}, u32[]{:S(2)}) collective-permute-start(bf16[1024,384]{1,0:T(8,128)(2,1)} %get-tuple-element.69), channel_id=1, source_target_pairs={{0,8},{8,0},{16,24},{24,16},{1,9},{9,1},{17,25},{25,17},{2,10},{10... | collective-permute-start | bytes 2359304 | tf_op jit(solution)/shard_map/ppermute | solution.py:573
  205.8 35.1 %collective-permute-start.13 = (bf16[1024,384]{1,0:T(8,128)(2,1)}, bf16[1024,384]{1,0:T(8,128)(2,1)}, u32[]{:S(2)}, u32[]{:S(2)}) collective-permute-start(bf16[1024,384]{1,0:T(8,128)(2,1)} %get-tuple-element.70), channel_id=1, source_target_pairs={{0,16},{8,24},{16,0},{24,8},{1,17},{9,25},{17,1},{25,9},{2,18},{10... | collective-permute-start | bytes 2359304 | tf_op jit(solution)/shard_map/ppermute | solution.py:573
  207.8 33.2 %collective-permute-start.14 = (bf16[1024,384]{1,0:T(8,128)(2,1)}, bf16[1024,384]{1,0:T(8,128)(2,1)}, u32[]{:S(2)}, u32[]{:S(2)}) collective-permute-start(bf16[1024,384]{1,0:T(8,128)(2,1)} %get-tuple-element.71), channel_id=1, source_target_pairs={{0,24},{8,16},{16,8},{24,0},{1,25},{9,17},{17,9},{25,1},{2,26},{10... | collective-permute-start | bytes 2359304 | tf_op jit(solution)/shard_map/ppermute | solution.py:573
  240.8 1.1 copy-start.3
  240.8 1.1 copy-start.5
  240.8 1.0 copy-start.6
  240.8 1.3 copy-start.8
  240.9 1.3 copy-start.11
  240.9 1.3 copy-start.13
  240.9 1.3 copy-start.18
  282.8 2.3 collective-permute-start.15
  287.2 10.2 %collective-permute-start.16 = (bf16[192,896]{1,0:T(8,128)(2,1)S(1)}, bf16[192,896]{1,0:T(8,128)(2,1)S(1)}, u32[]{:S(2)}, u32[]{:S(2)}) collective-permute-start(bf16[192,896]{1,0:T(8,128)(2,1)S(1)} %select_convert_fusion.1), channel_id=1, source_target_pairs={{0,8},{8,0},{16,24},{24,16},{1,9},{9,1},{17,25},{25,17},{2,10},{10... | collective-permute-start | bytes 1032200 | tf_op jit(solution)/shard_map/ppermute | solution.py:597
  297.5 5.6 %collective-permute-start.17 = (bf16[96,896]{1,0:T(8,128)(2,1)S(1)}, bf16[96,896]{1,0:T(8,128)(2,1)S(1)}, u32[]{:S(2)}, u32[]{:S(2)}) collective-permute-start(bf16[96,896]{1,0:T(8,128)(2,1)S(1)} %select_convert_fusion.2), channel_id=1, source_target_pairs={{0,16},{8,24},{16,0},{24,8},{1,17},{9,25},{17,1},{25,9},{2,18},{10... | collective-permute-start | bytes 516104 | tf_op jit(solution)/shard_map/ppermute | solution.py:597
  303.2 4.6 %collective-permute-start.18 = (bf16[48,896]{1,0:T(8,128)(2,1)S(1)}, bf16[48,896]{1,0:T(8,128)(2,1)S(1)}, u32[]{:S(2)}, u32[]{:S(2)}) collective-permute-start(bf16[48,896]{1,0:T(8,128)(2,1)S(1)} %select_convert_fusion.3), channel_id=1, source_target_pairs={{0,2},{1,3},{2,0},{3,1},{4,6},{5,7},{6,4},{7,5},{8,10},{9,11},{10,... | collective-permute-start | bytes 258056 | tf_op jit(solution)/shard_map/ppermute | solution.py:597
  307.8 23.3 %copy-start.38 = (bf16[1024,384]{1,0:T(8,128)(2,1)S(1)}, bf16[1024,384]{1,0:T(8,128)(2,1)}, u32[]{:S(2)}) copy-start(bf16[1024,384]{1,0:T(8,128)(2,1)} %get-tuple-element.60) | copy-start | bytes 2359300
  307.8 25.0 %copy-start.37 = (bf16[1024,384]{1,0:T(8,128)(2,1)S(1)}, bf16[1024,384]{1,0:T(8,128)(2,1)}, u32[]{:S(2)}) copy-start(bf16[1024,384]{1,0:T(8,128)(2,1)} %get-tuple-element.61) | copy-start | bytes 2359300
  307.8 26.5 %copy-start.36 = (bf16[1024,384]{1,0:T(8,128)(2,1)S(1)}, bf16[1024,384]{1,0:T(8,128)(2,1)}, u32[]{:S(2)}) copy-start(bf16[1024,384]{1,0:T(8,128)(2,1)} %get-tuple-element.62) | copy-start | bytes 2359300
  307.9 5.3 %collective-permute-start.19 = (bf16[24,896]{1,0:T(8,128)(2,1)S(1)}, bf16[24,896]{1,0:T(8,128)(2,1)S(1)}, u32[]{:S(2)}, u32[]{:S(2)}) collective-permute-start(bf16[24,896]{1,0:T(8,128)(2,1)S(1)} %select_convert_fusion.4), channel_id=1, source_target_pairs={{0,4},{1,5},{2,6},{3,7},{4,0},{5,1},{6,2},{7,3},{8,12},{9,13},{10,... | collective-permute-start | bytes 129032 | tf_op jit(solution)/shard_map/ppermute | solution.py:597
  313.1 5.0 %collective-permute-start.20 = (bf16[24,896]{1,0:T(8,128)(2,1)S(1)}, bf16[24,896]{1,0:T(8,128)(2,1)S(1)}, u32[]{:S(2)}, u32[]{:S(2)}) collective-permute-start(bf16[24,896]{1,0:T(8,128)(2,1)S(1)} %add_convert_fusion.1), channel_id=1, source_target_pairs={{0,4},{1,5},{2,6},{3,7},{4,0},{5,1},{6,2},{7,3},{8,12},{9,13},{10,... | collective-permute-start | bytes 129032 | tf_op jit(solution)/shard_map/ppermute | solution.py:605
  318.2 5.0 %collective-permute-start.21 = (bf16[48,896]{1,0:T(8,128)(2,1)S(1)}, bf16[48,896]{1,0:T(8,128)(2,1)S(1)}, u32[]{:S(2)}, u32[]{:S(2)}) collective-permute-start(bf16[48,896]{1,0:T(8,128)(2,1)S(1)} %pad_maximum_fusion.7), channel_id=1, source_target_pairs={{0,2},{1,3},{2,0},{3,1},{4,6},{5,7},{6,4},{7,5},{8,10},{9,11},{10,... | collective-permute-start | bytes 258056 | tf_op jit(solution)/shard_map/ppermute | solution.py:605
  323.3 7.3 %collective-permute-start.22 = (bf16[96,896]{1,0:T(8,128)(2,1)S(1)}, bf16[96,896]{1,0:T(8,128)(2,1)S(1)}, u32[]{:S(2)}, u32[]{:S(2)}) collective-permute-start(bf16[96,896]{1,0:T(8,128)(2,1)S(1)} %pad_maximum_fusion.5), channel_id=1, source_target_pairs={{0,16},{8,24},{16,0},{24,8},{1,17},{9,25},{17,1},{25,9},{2,18},{10... | collective-permute-start | bytes 516104 | tf_op jit(solution)/shard_map/ppermute | solution.py:605
  330.7 11.0 %collective-permute-start.23 = (bf16[192,896]{1,0:T(8,128)(2,1)S(1)}, bf16[192,896]{1,0:T(8,128)(2,1)S(1)}, u32[]{:S(2)}, u32[]{:S(2)}) collective-permute-start(bf16[192,896]{1,0:T(8,128)(2,1)S(1)} %pad_maximum_fusion.3), channel_id=1, source_target_pairs={{0,8},{8,0},{16,24},{24,16},{1,9},{9,1},{17,25},{25,17},{2,10},{10... | collective-permute-start | bytes 1032200 | tf_op jit(solution)/shard_map/ppermute | solution.py:605
  331.1 25.4 %collective-permute-start.9 = (bf16[1024,384]{1,0:T(8,128)(2,1)S(1)}, bf16[1024,384]{1,0:T(8,128)(2,1)S(1)}, u32[]{:S(2)}, u32[]{:S(2)}) collective-permute-start(bf16[1024,384]{1,0:T(8,128)(2,1)S(1)} %copy-done.38), channel_id=1, source_target_pairs={{0,8},{8,0},{16,24},{24,16},{1,9},{9,1},{17,25},{25,17},{2,10},{10... | collective-permute-start | bytes 2359304 | tf_op jit(solution)/shard_map/ppermute | solution.py:573
  332.8 23.7 %collective-permute-start.10 = (bf16[1024,384]{1,0:T(8,128)(2,1)S(1)}, bf16[1024,384]{1,0:T(8,128)(2,1)S(1)}, u32[]{:S(2)}, u32[]{:S(2)}) collective-permute-start(bf16[1024,384]{1,0:T(8,128)(2,1)S(1)} %copy-done.37), channel_id=1, source_target_pairs={{0,16},{8,24},{16,0},{24,8},{1,17},{9,25},{17,1},{25,9},{2,18},{10... | collective-permute-start | bytes 2359304 | tf_op jit(solution)/shard_map/ppermute | solution.py:573
  334.3 31.6 %copy-start.1 = (f32[1024,384]{1,0:T(8,128)S(1)}, f32[1024,384]{1,0:T(8,128)}, u32[]{:S(2)}) copy-start(f32[1024,384]{1,0:T(8,128)} %copy-done) | copy-start | bytes 4718596
  334.3 31.6 %copy-start.27 = (bf16[1024,384]{1,0:T(8,128)(2,1)S(1)}, bf16[1024,384]{1,0:T(8,128)(2,1)}, u32[]{:S(2)}) copy-start(bf16[1024,384]{1,0:T(8,128)(2,1)} %get-tuple-element.59) | copy-start | bytes 2359300
  334.3 31.6 %collective-permute-start.11 = (bf16[1024,384]{1,0:T(8,128)(2,1)S(1)}, bf16[1024,384]{1,0:T(8,128)(2,1)S(1)}, u32[]{:S(2)}, u32[]{:S(2)}) collective-permute-start(bf16[1024,384]{1,0:T(8,128)(2,1)S(1)} %copy-done.36), channel_id=1, source_target_pairs={{0,24},{8,16},{16,8},{24,0},{1,25},{9,17},{17,9},{25,1},{2,26},{10... | collective-permute-start | bytes 2359304 | tf_op jit(solution)/shard_map/ppermute | solution.py:573
  341.9 25.3 %collective-permute-start.24 = (bf16[384,896]{1,0:T(8,128)(2,1)S(1)}, bf16[384,896]{1,0:T(8,128)(2,1)S(1)}, u32[]{:S(2)}, u32[]{:S(2)}) collective-permute-start(bf16[384,896]{1,0:T(8,128)(2,1)S(1)} %pad_maximum_fusion.2), channel_id=1, source_target_pairs={{0,1},{1,0},{2,3},{3,2},{4,5},{5,4},{6,7},{7,6},{8,9},{9,8},{10,11... | collective-permute-start | bytes 2064392 | tf_op jit(solution)/shard_map/ppermute | solution.py:605
  367.7 1.5 copy-start.28
  367.8 1.5 copy-start.29
  367.9 2.8 copy-start.23
  369.3 2.2 copy-start.21
  369.3 2.7 copy-start.22
  377.3 3.7 copy-start.25
  377.3 3.7 copy-start.26
  379.9 1.3 copy-start.19
  379.9 1.6 copy-start.20
  379.9 2.0 copy-start.24
  (6 other events, 4.7 us)
Sparse Core Ops, SparseCore 0:
  14.2 53.9 all-gather.4
  70.3 49.9 all-gather.2
  166.4 55.2 reduce-scatter.2
  241.0 55.2 reduce-scatter.4

commit v6 on v5

--- a/solution.py
+++ b/solution.py
@@ -83,17 +83,40 @@
     return lax.dot_general(left, right, dims, preferred_element_type=jnp.float32)
 
 
-def dispatch(rows_ref, gate_rows_ref, u_refs, g_refs, lane, x_out, dy_out, gate_out):
-    slots, _, tokens = rows_ref.shape
+def moe_early_kernel(slots, rows_ref, gate_rows_ref, *rest):
+    g_refs, dy_ref, gate_ref = rest[:slots], rest[slots], rest[slots + 1]
+    tokens = rows_ref.shape[2]
+    lane = pl.program_id(0)
     for slot in range(slots):
-        place = rows_ref[slot, pl.ds(lane, 1), :]
-        same = lax.broadcasted_iota(jnp.int32, (CAP, tokens), 0) == place
+        same = lax.broadcasted_iota(jnp.int32, (CAP, tokens), 0) == rows_ref[slot, pl.ds(lane, 1), :]
         pick = jnp.where(same, 1.0, 0.0).astype(jnp.bfloat16)
         gate = jnp.sum(jnp.where(same, gate_rows_ref[slot, pl.ds(lane, 1), :], 0.0), axis=1, keepdims=True)
         span = pl.ds(slot * CAP, CAP)
-        x_out[span, :] = mxu(pick, u_refs[slot][...]).astype(jnp.bfloat16)
-        dy_out[span, :] = (gate * mxu(pick, g_refs[slot][...])).astype(jnp.bfloat16)
-        gate_out[span, :] = jnp.broadcast_to(gate, (CAP, 128))
+        dy_ref[span, :] = (gate * mxu(pick, g_refs[slot][...])).astype(jnp.bfloat16)
+        gate_ref[span, :] = jnp.broadcast_to(gate, (CAP, 128))
+
+
+def moe_early(rows, gate_rows, g_all):
+    slots, count, tokens = rows.shape
+    width = g_all[0].shape[1]
+    pairs = slots * CAP
+    operands = [rows, gate_rows, *g_all]
+    shapes = [((pairs, width), jnp.bfloat16), ((pairs, 128), jnp.float32)]
+    return moe_call(
+        functools.partial(moe_early_kernel, slots), count, operands,
+        [once(a) for a in operands],
+        [jax.ShapeDtypeStruct((count,) + shape, kind) for shape, kind in shapes],
+        [pl.BlockSpec((pl.Squeezed(),) + shape, lambda e: (e, 0, 0)) for shape, _ in shapes],
+        [], count * pairs * width * 2 * tokens,
+    )
+
+
+def dispatch(rows_ref, u_refs, lane, x_out):
+    slots, _, tokens = rows_ref.shape
+    for slot in range(slots):
+        same = lax.broadcasted_iota(jnp.int32, (CAP, tokens), 0) == rows_ref[slot, pl.ds(lane, 1), :]
+        pick = jnp.where(same, 1.0, 0.0).astype(jnp.bfloat16)
+        x_out[pl.ds(slot * CAP, CAP), :] = mxu(pick, u_refs[slot][...]).astype(jnp.bfloat16)
 
 
 def combine(cols_ref, lanes, step, buf, sum_buf, fresh):
@@ -125,18 +148,18 @@
     return [slot * count + offset + step for slot in range(slots)]
 
 
-def moe_full_kernel(offset, chunk, slots, rows_ref, gate_rows_ref, cols_ref, *rest):
-    u_refs, g_refs, rest = rest[:slots], rest[slots : 2 * slots], rest[2 * slots :]
+def moe_full_kernel(offset, chunk, slots, rows_ref, cols_ref, dy_ref, gate_ref, *rest):
+    u_refs, rest = rest[:slots], rest[slots:]
     inner_ref, outer_ref, y_ref, du_ref, grads_ref = rest[:5]
-    x_buf, dy_buf, act_buf, dpre_buf, gate_buf, y_buf, du_buf = rest[5:]
+    x_buf, dy_buf, act_buf, dpre_buf, y_buf, du_buf = rest[5:]
     step = pl.program_id(0)
     width = inner_ref.shape[1]
-    dispatch(rows_ref, gate_rows_ref, u_refs, g_refs, offset + step, x_buf, dy_buf, gate_buf)
+    dispatch(rows_ref, u_refs, offset + step, x_buf)
 
     def part(index, carry):
         span = pl.ds(pl.multiple_of(index * chunk, chunk), chunk)
         rows_in = x_buf[...]
-        rows_grad = dy_buf[...]
+        rows_grad = dy_ref[...]
         act, dpre = gelu_pair(mxu(rows_in, inner_ref[span, :], NT), mxu(rows_grad, outer_ref[span, :], NT))
         act_buf[:, span] = act
         dpre_buf[:, span] = dpre
@@ -145,7 +168,7 @@
         return carry
 
     lax.fori_loop(0, inner_ref.shape[0] // chunk, part, 0)
-    x_buf[...] = times_gate(gate_buf[...], mxu(act_buf[...], outer_ref[...]))
+    x_buf[...] = times_gate(gate_ref[...], mxu(act_buf[...], outer_ref[...]))
     dy_buf[...] = mxu(dpre_buf[...], inner_ref[...]).astype(jnp.bfloat16)
     lanes = slot_lanes(slots, rows_ref.shape[1], offset, step)
     combine(cols_ref, lanes, step, x_buf, y_buf, True)
@@ -172,14 +195,14 @@
             ref[...] = sum_buf[slot].astype(jnp.bfloat16)
 
 
-def moe_front_kernel(offset, chunk, slots, rows_ref, gate_rows_ref, cols_ref, *rest):
-    u_refs, g_refs, rest = rest[:slots], rest[slots : 2 * slots], rest[2 * slots :]
+def moe_front_kernel(offset, chunk, slots, rows_ref, cols_ref, dy_ref, *rest):
+    u_refs, rest = rest[:slots], rest[slots:]
     inner_ref, outer_ref, start_ref, rest = rest[0], rest[1], rest[2], rest[3:]
     du_refs, rest = rest[:slots], rest[slots:]
-    x_ref, dy_ref, gate_ref, act_ref, dpre_ref, buf, sum_buf, sem = rest
+    x_ref, act_ref, dpre_ref, buf, sum_buf, sem = rest
     step = pl.program_id(0)
     fetch(start_ref, sum_buf, sem)
-    dispatch(rows_ref, gate_rows_ref, u_refs, g_refs, offset + step, x_ref, dy_ref, gate_ref)
+    dispatch(rows_ref, u_refs, offset + step, x_ref)
 
     def part(index, carry):
         span = pl.ds(pl.multiple_of(index * chunk, chunk), chunk)
@@ -247,49 +270,55 @@
     return units, steps, pairs, sums, part, inner, outer, grads, grads_spec
 
 
-def moe_full(rows, gate_rows, cols, u_all, g_all, weights, offset):
+def expert_block(array, offset):
+    return pl.BlockSpec((pl.Squeezed(),) + array.shape[1:], lambda e: (offset + e, 0, 0))
+
+
+def moe_full(rows, cols, early, u_all, weights, offset):
     slots, _, tokens = rows.shape
     width = u_all[0].shape[1]
     units, steps, pairs, sums, _, inner, outer, grads, grads_spec = moe_sizes(slots, tokens, weights, width)
-    operands = [rows, gate_rows, cols, *u_all, *g_all, weights, weights]
+    operands = [rows, cols, *early, *u_all, weights, weights]
     low, full = jnp.bfloat16, jnp.float32
     scratch = [pltpu.VMEM((pairs, width), low)] * 2 + [pltpu.VMEM((pairs, units), low)] * 2
-    scratch += [pltpu.VMEM((pairs, 128), full)] + [pltpu.VMEM(sums.shape, full)] * 2
+    scratch += [pltpu.VMEM(sums.shape, full)] * 2
     return moe_call(
         functools.partial(moe_full_kernel, offset, units // 3, slots), steps, operands,
-        [once(a) for a in operands[:-2]] + [inner, outer],
+        [once(rows), once(cols)] + [expert_block(a, offset) for a in early]
+        + [once(a) for a in u_all] + [inner, outer],
         [sums, sums, grads], [once(sums), once(sums), grads_spec], scratch,
-        steps * pairs * width * (12 * units + 8 * tokens),
-    )
-
-
-def moe_front(rows, gate_rows, cols, u_all, g_all, weights, offset, start):
+        steps * pairs * width * (12 * units + 6 * tokens),
+    )
+
+
+def moe_front(rows, cols, early, u_all, weights, offset, start):
     slots, _, tokens = rows.shape
     width = u_all[0].shape[1]
     units, steps, pairs, sums, part, inner, outer, _, _ = moe_sizes(slots, tokens, weights, width)
-    operands = [rows, gate_rows, cols, *u_all, *g_all, weights, weights, start]
+    operands = [rows, cols, early[0], *u_all, weights, weights, start]
     low, full = jnp.bfloat16, jnp.float32
-    kept = [((pairs, width), low), ((pairs, width), low), ((pairs, 128), full)]
-    kept += [((pairs, units), low), ((pairs, units), low)]
+    kept = [((pairs, width), low), ((pairs, units), low), ((pairs, units), low)]
     outs = [part] * slots + [jax.ShapeDtypeStruct((steps,) + shape, kind) for shape, kind in kept]
     specs = [once(part)] * slots
     specs += [pl.BlockSpec((pl.Squeezed(),) + shape, lambda e: (e, 0, 0)) for shape, _ in kept]
     return moe_call(
         functools.partial(moe_front_kernel, offset, units // 3, slots), steps, operands,
-        [once(a) for a in operands[:-3]] + [inner, outer, pl.BlockSpec(memory_space=pl.ANY)],
+        [once(rows), once(cols), expert_block(early[0], offset)]
+        + [once(a) for a in u_all] + [inner, outer, pl.BlockSpec(memory_space=pl.ANY)],
         outs, specs,
         [pltpu.VMEM((pairs, width), low), pltpu.VMEM(sums.shape, full), pltpu.SemaphoreType.DMA],
-        steps * pairs * width * (6 * units + 6 * tokens),
-    )
-
-
-def moe_rest(cols, kept, weights, offset, count, start):
+        steps * pairs * width * (6 * units + 4 * tokens),
+    )
+
+
+def moe_rest(cols, kept, early, weights, offset, count, start):
     slots, tokens, width = start.shape
     units, steps, pairs, sums, part, _, outer, grads, grads_spec = moe_sizes(slots, tokens, weights, width)
-    operands = [cols, *kept, weights, start]
+    operands = [cols, kept[0], *early, *kept[1:], weights, start]
     low, full = jnp.bfloat16, jnp.float32
     in_specs = [once(cols)]
-    in_specs += [pl.BlockSpec((pl.Squeezed(),) + a.shape[1:], lambda e: (e, 0, 0)) for a in kept]
+    in_specs += [expert_block(kept[0], 0)] + [expert_block(a, offset) for a in early]
+    in_specs += [expert_block(a, 0) for a in kept[1:]]
     return moe_call(
         functools.partial(moe_rest_kernel, offset, units // 3, slots, count), steps, operands,
         in_specs + [outer, pl.BlockSpec(memory_space=pl.ANY)],
@@ -360,41 +389,41 @@
         begin, end = key_range(marks_ref, index * block, block, blocks)
         seg_row = seg_ref[:, span].astype(jnp.float32)
         masks = head_masks(block)
+        queries = []
         for pair in range(HEADS // 2):
             lanes = slice(pair * 2 * HEAD, (pair + 1) * 2 * HEAD)
             query = joined_ref[span, lanes] * jnp.bfloat16(HEAD ** (-0.5))
-            queries = [jnp.where(m, query, jnp.zeros_like(query)) for m in masks]
-
-            def keys(at, state):
-                key_span = pl.ds(pl.multiple_of(at * block, block), block)
-                key_pair = joined_ref[key_span, D + pair * 2 * HEAD : D + (pair + 1) * 2 * HEAD]
-                seg_col = jnp.concatenate([column[key_span, :]] * (block // 128), axis=1)
-                same = seg_col == seg_row
-                out = []
-                for side in range(2):
-                    peak, total, acc = state[side]
-                    head = 2 * pair + side
-                    scores = jnp.where(same, mxu(key_pair, queries[side], NT), MASKED)
-                    new_peak = jnp.maximum(peak, jnp.max(scores, axis=0, keepdims=True))
-                    weights = jnp.exp(scores - new_peak)
-                    fix = jnp.exp(peak - new_peak)
-                    total = total * fix + jnp.sum(weights, axis=0, keepdims=True)
-                    value = value_t[head * HEAD : (head + 1) * HEAD, key_span]
-                    acc = acc * fix + mxu(value, weights.astype(jnp.bfloat16))
-                    out.append((new_peak, total, acc))
-                return tuple(out)
-
-            zero = (
-                jnp.full((1, block), MASKED, jnp.float32),
-                jnp.zeros((1, block), jnp.float32),
-                jnp.zeros((HEAD, block), jnp.float32),
-            )
-            done = lax.fori_loop(begin, end, keys, (zero, zero))
-            for side in range(2):
-                peak, total, acc = done[side]
-                head = 2 * pair + side
-                mixed_t_ref[head * HEAD : (head + 1) * HEAD, span] = (acc / total).astype(jnp.bfloat16)
-                logs_ref[head : head + 1, span] = peak + jnp.log(total)
+            queries.extend(jnp.where(m, query, jnp.zeros_like(query)) for m in masks)
+
+        def keys(at, state):
+            key_span = pl.ds(pl.multiple_of(at * block, block), block)
+            seg_col = jnp.concatenate([column[key_span, :]] * (block // 128), axis=1)
+            same = seg_col == seg_row
+            out = []
+            for head in range(HEADS):
+                first = D + head // 2 * 2 * HEAD
+                key_pair = joined_ref[key_span, first : first + 2 * HEAD]
+                peak, total, acc = state[head]
+                scores = jnp.where(same, mxu(key_pair, queries[head], NT), MASKED)
+                new_peak = jnp.maximum(peak, jnp.max(scores, axis=0, keepdims=True))
+                weights = jnp.exp(scores - new_peak)
+                fix = jnp.exp(peak - new_peak)
+                total = total * fix + jnp.sum(weights, axis=0, keepdims=True)
+                value = value_t[head * HEAD : (head + 1) * HEAD, key_span]
+                acc = acc * fix + mxu(value, weights.astype(jnp.bfloat16))
+                out.append((new_peak, total, acc))
+            return tuple(out)
+
+        zero = (
+            jnp.full((1, block), MASKED, jnp.float32),
+            jnp.zeros((1, block), jnp.float32),
+            jnp.zeros((HEAD, block), jnp.float32),
+        )
+        done = lax.fori_loop(begin, end, keys, (zero,) * HEADS)
+        for head in range(HEADS):
+            peak, total, acc = done[head]
+            mixed_t_ref[head * HEAD : (head + 1) * HEAD, span] = (acc / total).astype(jnp.bfloat16)
+            logs_ref[head : head + 1, span] = peak + jnp.log(total)
         mixed = jnp.transpose(mixed_t_ref[:, span].astype(jnp.float32)).astype(jnp.bfloat16)
         mixed_ref[span, :] = mixed
         hidden = x_ref[span, :].astype(jnp.float32) + mxu(mixed, proj_low)
@@ -475,45 +504,47 @@
         begin, end = key_range(marks_ref, index * block, block, blocks)
         seg_row = seg_ref[:, span].astype(jnp.float32)
         masks = head_masks(block)
-        query_grads = []
+        queries = []
+        out_grads = []
+        deltas = []
+        logs = []
         for pair in range(HEADS // 2):
             lanes = slice(pair * 2 * HEAD, (pair + 1) * 2 * HEAD)
             query = joined_ref[span, lanes] * jnp.bfloat16(HEAD ** (-0.5))
-            queries = [jnp.where(m, query, jnp.zeros_like(query)) for m in masks]
+            queries.extend(jnp.where(m, query, jnp.zeros_like(query)) for m in masks)
             grad_pair = mixed_grad[:, lanes]
-            out_grads = [jnp.where(m, grad_pair, jnp.zeros_like(grad_pair)) for m in masks]
-            deltas = []
-            logs = []
-            for side in range(2):
-                head = 2 * pair + side
-                deltas.append(jnp.sum(dots[head * HEAD : (head + 1) * HEAD], axis=0, keepdims=True))
-                logs.append(logs_ref[head : head + 1, span])
-
-            def keys(at, state):
-                key_span = pl.ds(pl.multiple_of(at * block, block), block)
-                key_pair = joined_ref[key_span, D + pair * 2 * HEAD : D + (pair + 1) * 2 * HEAD]
-                value_pair = joined_ref[key_span, 2 * D + pair * 2 * HEAD : 2 * D + (pair + 1) * 2 * HEAD]
-                seg_col = jnp.concatenate([column[key_span, :]] * (block // 128), axis=1)
-                same = seg_col == seg_row
-                out = []
+            out_grads.extend(jnp.where(m, grad_pair, jnp.zeros_like(grad_pair)) for m in masks)
+        for head in range(HEADS):
+            deltas.append(jnp.sum(dots[head * HEAD : (head + 1) * HEAD], axis=0, keepdims=True))
+            logs.append(logs_ref[head : head + 1, span])
+
+        def keys(at, state):
+            key_span = pl.ds(pl.multiple_of(at * block, block), block)
+            seg_col = jnp.concatenate([column[key_span, :]] * (block // 128), axis=1)
+            same = seg_col == seg_row
+            out = []
+            for pair in range(HEADS // 2):
+                first = pair * 2 * HEAD
+                lanes = slice(first, first + 2 * HEAD)
+                key_pair = joined_ref[key_span, D + first : D + first + 2 * HEAD]
+                value_pair = joined_ref[key_span, 2 * D + first : 2 * D + first + 2 * HEAD]
                 key_sum = key_grad[key_span, lanes]
                 value_sum = value_grad[key_span, lanes]
-                for side in range(2):
-                    head = 2 * pair + side
-                    scores = jnp.where(same, mxu(key_pair, queries[side], NT), MASKED)
-                    probs = jnp.exp(scores - logs[side])
-                    prob_grad = mxu(value_pair, out_grads[side], NT)
-                    score_grad = (probs * (prob_grad - deltas[side])).astype(jnp.bfloat16)
-                    value_sum = value_sum + mxu(probs.astype(jnp.bfloat16), out_grads[side])
-                    key_sum = key_sum + mxu(score_grad, queries[side])
+                for head in (2 * pair, 2 * pair + 1):
+                    scores = jnp.where(same, mxu(key_pair, queries[head], NT), MASKED)
+                    probs = jnp.exp(scores - logs[head])
+                    prob_grad = mxu(value_pair, out_grads[head], NT)
+                    score_grad = (probs * (prob_grad - deltas[head])).astype(jnp.bfloat16)
+                    value_sum = value_sum + mxu(probs.astype(jnp.bfloat16), out_grads[head])
+                    key_sum = key_sum + mxu(score_grad, queries[head])
                     key_t = key_t_ref[head * HEAD : (head + 1) * HEAD, key_span]
-                    out.append(state[side] + mxu(key_t, score_grad))
+                    out.append(state[head] + mxu(key_t, score_grad))
                 key_grad[key_span, lanes] = key_sum
                 value_grad[key_span, lanes] = value_sum
-                return tuple(out)
-
-            zero = jnp.zeros((HEAD, block), jnp.float32)
-            query_grads.extend(lax.fori_loop(begin, end, keys, (zero, zero)))
+            return tuple(out)
+
+        zero = jnp.zeros((HEAD, block), jnp.float32)
+        query_grads = lax.fori_loop(begin, end, keys, (zero,) * HEADS)
         query_grad_t = jnp.concatenate(query_grads, axis=0) * HEAD ** (-0.5)
         grads[span, :D] = jnp.transpose(query_grad_t).astype(jnp.bfloat16)
         return carry
@@ -669,10 +700,11 @@
     hidden_one = saved[-1]
     u_all = to_peers([moe_in] * groups, groups)
     second = local_count // 2
-    y_sums, du_sums, grads_first = moe_full(rows, gate_rows, cols, u_all, g_all, weights[0], 0)
-    outs = moe_front(rows, gate_rows, cols, u_all, g_all, weights[1], second, du_sums)
+    early = moe_early(rows, gate_rows, g_all)
+    y_sums, du_sums, grads_first = moe_full(rows, cols, early, u_all, weights[0], 0)
+    outs = moe_front(rows, cols, early, u_all, weights[1], second, du_sums)
     du_parts = to_peers(outs[:groups], groups)
-    *y_own, grads_second = moe_rest(cols, outs[groups:], weights[1], second, local_count, y_sums)
+    *y_own, grads_second = moe_rest(cols, outs[groups:], early, weights[1], second, local_count, y_sums)
     y_parts = to_peers(y_own, groups)
     moe_sum = sum(p.astype(jnp.float32) for p in y_parts)
     block_out = (hidden_one + moe_sum).astype(jnp.bfloat16)

time: 401 us -> 374 us (0.933)
  the two profiles are of different devices: /device:TPU:0 before, /device:TPU:18 now
where the time goes in v6:
time: 374 us; the launch traced here: 367 us
  Pallas kernels  180 us (48%)
  waiting for transfers between devices  88 us (24%)
  starting transfers between devices  44.7 us (12%)
  other arithmetic  21.4 us (6%)
  local copies, waits for them, and re-layouts  17.8 us (5%)
  between operations  14.6 us (4%)
    pallas_call x4, Pallas kernels, moe_call(): pl.pallas_call(kernel, out_shape=tuple(outs), grid_spec=pltpu.PrefetchSca...  125 us
    ppermute x15, waiting for transfers between devices, to_peers(): lax.ppermute(arrays[k], 'expert', [(i, i ^ k) for i in range(groups)])  47.8 us
    pallas_call x1, Pallas kernels, attend_back(): pl.pallas_call(functools.partial(attend_back_kernel, block, len(du_parts)...  29 us
    ppermute x15, starting transfers between devices, to_peers(): lax.ppermute(arrays[k], 'expert', [(i, i ^ k) for i in range(groups)])  24.8 us
    pallas_call x1, Pallas kernels, attend(): pl.pallas_call(functools.partial(attend_kernel, block), out_shape=(jax.Sh...  24.3 us
    ppermute x5, waiting for transfers between devices, butterfly_sum(): got = lax.ppermute(send, axis, [(i, i ^ bit) for i in range(size)])  21.6 us
    ppermute x5, waiting for transfers between devices, butterfly_sum(): got = lax.ppermute(value, axis, [(i, i ^ bit) for i in range(size)])  17.9 us
    ppermute x5, starting transfers between devices, butterfly_sum(): got = lax.ppermute(send, axis, [(i, i ^ bit) for i in range(size)])  12.6 us
  transfers between devices with their start and end apart: 29, of which 15 were waited for; matrix products, arithmetic and copies ran while one was open for 4% of the time, Pallas kernels for 49%

profile of v6, /device:TPU:18, one launch (start us, length us, event | category | flops | bytes accessed | tf_op | source)
XLA Modules:
  0.0 367.0 jit_solution(14495752559940814440)
XLA Ops:
  7.2 2.0 convert_bitcast_fusion
  9.3 0.8 pad_maximum_fusion.1
  10.1 1.8 copy.43
  11.9 0.9 convert_element_type.72
  12.9 1.1 fusion.5
  14.1 0.7 all-gather.3.cloned.1.call-update
  14.9 1.6 collective-permute-start.1
  17.0 1.4 collective-permute-start.2
  18.5 1.5 collective-permute-start.5
  20.5 1.5 collective-permute-start.3
  22.0 24.3 %attend.1 = (bf16[1024,1152]{1,0:T(8,128)(2,1)}, bf16[384,1024]{1,0:T(8,128)(2,1)S(1)}, bf16[1024,384]{1,0:T(8,128)(2,1)S(1)}, bf16[384,1024]{1,0:T(8,128)(2,1)S...) custom-call(s32[1024]{0:T(1024)S(1)} %bitcast.31, ...), custom_call_target="tpu_custom_call" | custom-call | flops 8589934592 | bytes 12582912 | tf_op jit(solution)/shard_map/attend/pallas_call | solution.py:446
  46.2 1.1 copy-done
  47.4 0.9 copy-done.13
  48.3 0.9 copy-done.14
  49.1 0.9 copy-done.15
  50.1 0.6 copy-done.16
  50.7 9.2 %collective-permute-start.8 = (bf16[1024,384]{1,0:T(8,128)(2,1)}, bf16[1024,384]{1,0:T(8,128)(2,1)}, u32[]{:S(2)}, u32[]{:S(2)}) collective-permute-start(bf16[1024,384]{1,0:T(8,128)(2,1)} %get-tuple-element.52.rest_0_), channel_id=1, source_target_pairs={{0,24},{8,16},{16,8},{24,0},{1,25},{9,17},{17,9},{25,1},{2,26},{10... | collective-permute-start | bytes 2359304 | tf_op jit(solution)/shard_map/ppermute | solution.py:604
  60.4 1.1 collective-permute-start.6
  61.4 0.7 fusion.6
  62.1 2.2 route.1
  64.3 9.6 %shard_map.340 = (bf16[4,1280,384]{2,1,0:T(8,128)(2,1)}, f32[4,1280,128]{2,1,0:T(8,128)}) custom-call(s32[4,4,1024]{2,1,0:T(4,128)} %get-tuple-element.49.rows_ref, f32[4,4,1024]{2,1,0:T(4,128)} %get-tuple-element.50.gate_rows_ref, bf16[1024,384]{1,0:T(8,128)(2,1)} %out_grad_ref.1, bf16[1024,384]{1,0:T(8,128)(2,1)} %collective-permute-done.3.rest_1_, ...), custom_call_target="tpu_custom_call" | custom-call | flops 4026531840 | bytes 41943040 | tf_op jit(solution)/shard_map/pallas_call | solution.py:245
  73.9 4.7 %collective-permute-done.8.rest_3_ = bf16[1024,384]{1,0:T(8,128)(2,1)} collective-permute-done((bf16[1024,384]{1,0:T(8,128)(2,1)}, bf16[1024,384]{1,0:T(8,128)(2,1)}, u32[]{:S(2)}, u32[]{:S(2)}) %collective-permute-start.8) | collective-permute-done | bytes 786464 | tf_op jit(solution)/shard_map/ppermute | solution.py:604
  78.6 14.1 %collective-permute-done.7.rest_2_ = bf16[1024,384]{1,0:T(8,128)(2,1)} collective-permute-done((bf16[1024,384]{1,0:T(8,128)(2,1)}, bf16[1024,384]{1,0:T(8,128)(2,1)}, u32[]{:S(2)}, u32[]{:S(2)}) %collective-permute-start.7) | collective-permute-done | bytes 786464 | tf_op jit(solution)/shard_map/ppermute | solution.py:604
  92.7 1.3 collective-permute-done.6.rest_1_
  94.0 49.6 %shard_map.341 = (f32[4,1024,384]{2,1,0:T(8,128)}, f32[4,1024,384]{2,1,0:T(8,128)}, bf16[1536,1536]{1,0:T(8,128)(2,1)}) custom-call(s32[4,4,1024]{2,1,0:T(4,128)} %get-tuple-element.49.rows_ref, s32[1024,128]{1,0:T(8,128)} %get-tuple-element.48.cols_ref, bf16[4,1280,384]{2,1,0:T(8,128)(2,1)} %get-tuple-element.51.dy_ref, ...), custom_call_target="tpu_custom_call" | custom-call | flops 24159191040 | bytes 41943040 | tf_op jit(solution)/shard_map/pallas_call | solution.py:245
  143.7 0.6 copy-done.30
  145.1 34.3 %shard_map.342 = (bf16[1024,384]{1,0:T(8,128)(2,1)}, bf16[1024,384]{1,0:T(8,128)(2,1)}, bf16[1024,384]{1,0:T(8,128)(2,1)}, bf16[1024,384]{1,0:T(8,128)(2,1)}, bf...) custom-call(s32[4,4,1024]{2,1,0:T(4,128)} %get-tuple-element.49.rows_ref, ...), custom_call_target="tpu_custom_call" | custom-call | flops 13086228480 | bytes 41943040 | tf_op jit(solution)/shard_map/pallas_call | solution.py:245
  180.0 1.4 collective-permute-start.13
  181.4 1.5 collective-permute-start.14
  183.0 31.5 %shard_map.343 = (bf16[1024,384]{1,0:T(8,128)(2,1)}, bf16[1024,384]{1,0:T(8,128)(2,1)}, bf16[1024,384]{1,0:T(8,128)(2,1)}, bf16[1024,384]{1,0:T(8,128)(2,1)}, bf16[1536,1536]{1,0:T(8,128)(2,1)}) custom-call(s32[1024,128]{1,0:T(8,128)} %get-tuple-element.48.cols_ref, bf16[2,1280,384]{2,1,0:T(8,128)(2,1)} %get-tuple-element.55.x_ref, ...), custom_call_target="tpu_custom_call" | custom-call | flops 11072962560 | bytes 41943040 | tf_op jit(solution)/shard_map/pallas_call | solution.py:245
  214.6 1.6 collective-permute-done.13.rest_2_
  216.3 29.0 %attend_back.1 = (f32[1024,384]{1,0:T(8,128)}, f32[768,896]{1,0:T(8,128)}) custom-call(s32[1024]{0:T(1024)S(1)} %bitcast.32, bf16[1024,384]{1,0:T(8,128)(2,1)S(1)} %copy-done.8, f32[6,384]{1,0:T(8,128)S(1)} %copy-done.5, f32[384,1152]{1,0:T(8,128)} %qkv_ref.3, f32[384,384]{1,0:T(8,128)S(1)} %copy-done.3, s32[1,1024]{1,0:T(1,128)S(1)} %copy-done.10, ...), custom_call_target="tpu_custom_call" | custom-call | flops 25769803776 | bytes 25165824 | tf_op jit(solution)/shard_map/attend_back/pallas_call | solution.py:580
  245.3 1.9 select_convert_fusion
  247.3 2.2 collective-permute-done.15
  249.6 2.0 convert_add_fusion
  251.6 8.1 %collective-permute-start.16 = (bf16[192,896]{1,0:T(8,128)(2,1)S(1)}, bf16[192,896]{1,0:T(8,128)(2,1)S(1)}, u32[]{:S(2)}, u32[]{:S(2)}) collective-permute-start(bf16[192,896]{1,0:T(8,128)(2,1)S(1)} %select_convert_fusion.1), channel_id=1, source_target_pairs={{0,8},{8,0},{16,24},{24,16},{1,9},{9,1},{17,25},{25,17},{2,10},{10... | collective-permute-start | bytes 1032200 | tf_op jit(solution)/shard_map/ppermute | solution.py:628
  259.7 8.3 %collective-permute-done.16 = bf16[192,896]{1,0:T(8,128)(2,1)S(1)} collective-permute-done((bf16[192,896]{1,0:T(8,128)(2,1)S(1)}, bf16[192,896]{1,0:T(8,128)(2,1)S(1)}, u32[]{:S(2)}, u32[]{:S(2)}) %collective-permute-start.16) | collective-permute-done | bytes 344096 | tf_op jit(solution)/shard_map/ppermute | solution.py:628
  268.2 2.0 collective-permute-start.17
  270.2 3.9 %collective-permute-done.17 = bf16[96,896]{1,0:T(8,128)(2,1)S(1)} collective-permute-done((bf16[96,896]{1,0:T(8,128)(2,1)S(1)}, bf16[96,896]{1,0:T(8,128)(2,1)S(1)}, u32[]{:S(2)}, u32[]{:S(2)}) %collective-permute-start.17) | collective-permute-done | bytes 172064 | tf_op jit(solution)/shard_map/ppermute | solution.py:628
  274.2 1.9 collective-permute-start.18
  276.0 2.7 collective-permute-done.18
  278.8 0.6 collective-permute-start.19
  279.4 4.4 %collective-permute-done.19 = bf16[24,896]{1,0:T(8,128)(2,1)S(1)} collective-permute-done((bf16[24,896]{1,0:T(8,128)(2,1)S(1)}, bf16[24,896]{1,0:T(8,128)(2,1)S(1)}, u32[]{:S(2)}, u32[]{:S(2)}) %collective-permute-start.19) | collective-permute-done | bytes 43040 | tf_op jit(solution)/shard_map/ppermute | solution.py:628
  283.8 0.7 collective-permute-start.20
  284.5 4.3 %collective-permute-done.20 = bf16[24,896]{1,0:T(8,128)(2,1)S(1)} collective-permute-done((bf16[24,896]{1,0:T(8,128)(2,1)S(1)}, bf16[24,896]{1,0:T(8,128)(2,1)S(1)}, u32[]{:S(2)}, u32[]{:S(2)}) %collective-permute-start.20) | collective-permute-done | bytes 43040 | tf_op jit(solution)/shard_map/ppermute | solution.py:636
  288.9 2.8 collective-permute-start.21
  291.7 2.5 collective-permute-done.21
  294.2 1.8 collective-permute-start.22
  296.1 5.3 %collective-permute-done.22 = bf16[96,896]{1,0:T(8,128)(2,1)S(1)} collective-permute-done((bf16[96,896]{1,0:T(8,128)(2,1)S(1)}, bf16[96,896]{1,0:T(8,128)(2,1)S(1)}, u32[]{:S(2)}, u32[]{:S(2)}) %collective-permute-start.22) | collective-permute-done | bytes 172064 | tf_op jit(solution)/shard_map/ppermute | solution.py:636
  301.5 1.7 collective-permute-start.23
  303.6 1.8 collective-permute-start.10
  305.4 1.3 collective-permute-start.11
  306.7 5.8 %collective-permute-done.23 = bf16[192,896]{1,0:T(8,128)(2,1)S(1)} collective-permute-done((bf16[192,896]{1,0:T(8,128)(2,1)S(1)}, bf16[192,896]{1,0:T(8,128)(2,1)S(1)}, u32[]{:S(2)}, u32[]{:S(2)}) %collective-permute-start.23) | collective-permute-done | bytes 344096 | tf_op jit(solution)/shard_map/ppermute | solution.py:636
  312.8 16.4 %collective-permute-done.9 = bf16[1024,384]{1,0:T(8,128)(2,1)S(1)} collective-permute-done((bf16[1024,384]{1,0:T(8,128)(2,1)S(1)}, bf16[1024,384]{1,0:T(8,128)(2,1)S(1)}, u32[]{:S(2)}, u32[]{:S(2)}) %collective-permute-start.9) | collective-permute-done | bytes 786464 | tf_op jit(solution)/shard_map/ppermute | solution.py:604
  329.2 9.6 %collective-permute-done.11 = bf16[1024,384]{1,0:T(8,128)(2,1)S(1)} collective-permute-done((bf16[1024,384]{1,0:T(8,128)(2,1)S(1)}, bf16[1024,384]{1,0:T(8,128)(2,1)S(1)}, u32[]{:S(2)}, u32[]{:S(2)}) %collective-permute-start.11) | collective-permute-done | bytes 786464 | tf_op jit(solution)/shard_map/ppermute | solution.py:604
  338.8 1.4 add_convert_fusion
  341.6 0.6 multiply_add_fusion.7
  342.3 1.4 multiply_add_fusion.6
  343.6 0.8 copy-done.20
  345.0 2.8 multiply_add_fusion
  347.8 1.9 concatenate.40
  350.3 2.1 concatenate.41
  352.9 1.1 maximum_convert_fusion.1
  354.9 5.4 %multiply_add_fusion.2 = (f32[192,4,384]{2,1,0:T(4,128)}, f32[192,4,384]{2,1,0:T(4,128)}, f32[192,4,384]{2,1,0:T(4,128)}, f32[192,4,384]{2,1,0:T(4,128)}, f32[192,4,384]{2,1,0:T(4,128)}, /*index=5*/f32[192,4,384]{2,1,0:T(4,128)}) fusion(f32[192,4,384]{2,1,0:T(4,128)S(1)} %copy-done.23, f32[192,4,384]{2,1,0:T(4,128)S(1)} %copy-done.18, ...), kind=kLoop, calls=%fused_computation.12 | loop fusion | flops 5308416 | bytes 16515072 | tf_op jit(solution)/shard_map/add | solution.py:646
  (132 shorter events, 8.3 us)
Async XLA Ops:
  7.2 86.8 %all-gather.5.cloned.1.call-start = ((), (), s32[]{:S(2)}) async-start(), calls=%async_computation.3 | async-start | bytes 5308416 | tf_op jit(solution)/shard_map/all_gather | solution.py:682
  12.8 2.0 copy-start.29
  12.9 2.0 copy-start.31
  12.9 5.6 %copy-start.34 = (bf16[1024,384]{1,0:T(8,128)(2,1)S(1)}, bf16[1024,384]{1,0:T(8,128)(2,1)}, u32[]{:S(2)}) copy-start(bf16[1024,384]{1,0:T(8,128)(2,1)} %out_grad_ref.1) | copy-start | bytes 2359300
  12.9 9.1 %copy-start.2 = (f32[384,384]{1,0:T(8,128)S(1)}, f32[384,384]{1,0:T(8,128)}, u32[]{:S(2)}) copy-start(f32[384,384]{1,0:T(8,128)} %proj_ref.3) | copy-start | bytes 1769476
  12.9 9.1 %copy-start.4 = (f32[6,384]{1,0:T(8,128)S(1)}, f32[6,384]{1,0:T(8,128)}, u32[]{:S(2)}) copy-start(f32[6,384]{1,0:T(8,128)} %norm_ref.3) | copy-start | bytes 27652
  12.9 9.1 %copy-start.7 = (bf16[1024,384]{1,0:T(8,128)(2,1)S(1)}, bf16[1024,384]{1,0:T(8,128)(2,1)}, u32[]{:S(2)}) copy-start(bf16[1024,384]{1,0:T(8,128)(2,1)} %x_ref.3) | copy-start | bytes 2359300
  12.9 9.0 %copy-start.9 = (s32[1,1024]{1,0:T(1,128)S(1)}, s32[1,1024]{1,0:T(1,128)}, u32[]{:S(2)}) copy-start(s32[1,1024]{1,0:T(1,128)} %seg_ref.3) | copy-start | bytes 12292
  12.9 9.0 %copy-start.11 = (s32[1024]{0:T(1024)S(1)}, s32[1024]{0:T(1024)}, u32[]{:S(2)}) copy-start(s32[1024]{0:T(1024)} %param.25) | copy-start | bytes 12292
  14.0 131.0 %all-gather.3.cloned.1.call-start = ((), (), s32[]{:S(2)}) async-start(), calls=%async_computation.2 | async-start | bytes 5308416 | tf_op jit(solution)/shard_map/all_gather | solution.py:683
  14.8 333.0 %reduce-scatter.3.cloned.1.call-start = ((), (), s32[]{:S(2)}) async-start(), calls=%async_computation.4 | async-start | bytes 5308416 | tf_op jit(solution)/shard_map/reduce_scatter | solution.py:713
  14.9 5.6 %collective-permute-start.1 = (f32[8,1024]{1,0:T(8,128)S(1)}, f32[8,1024]{1,0:T(8,128)S(1)}, u32[]{:S(2)}, u32[]{:S(2)}) collective-permute-start(f32[8,1024]{1,0:T(8,128)S(1)} %get-tuple-element.114), channel_id=1, source_target_pairs={{0,16},{8,24},{16,0},{24,8},{1,17},{9,25},{17,1},{25,9},{2,18},{10... | collective-permute-start | bytes 98312 | tf_op jit(solution)/shard_map/ppermute | solution.py:604
  16.5 34.2 %collective-permute-start = (f32[8,1024]{1,0:T(8,128)S(1)}, f32[8,1024]{1,0:T(8,128)S(1)}, u32[]{:S(2)}, u32[]{:S(2)}) collective-permute-start(f32[8,1024]{1,0:T(8,128)S(1)} %get-tuple-element.114), channel_id=1, source_target_pairs={{0,8},{8,0},{16,24},{24,16},{1,9},{9,1},{17,25},{25,17},{2,10},{10... | collective-permute-start | bytes 98312 | tf_op jit(solution)/shard_map/ppermute | solution.py:604
  17.0 42.8 %collective-permute-start.2 = (f32[8,1024]{1,0:T(8,128)S(1)}, f32[8,1024]{1,0:T(8,128)S(1)}, u32[]{:S(2)}, u32[]{:S(2)}) collective-permute-start(f32[8,1024]{1,0:T(8,128)S(1)} %get-tuple-element.114), channel_id=1, source_target_pairs={{0,24},{8,16},{16,8},{24,0},{1,25},{9,17},{17,9},{25,1},{2,26},{10... | collective-permute-start | bytes 98312 | tf_op jit(solution)/shard_map/ppermute | solution.py:604
  18.5 41.9 %collective-permute-start.5 = (bf16[1024,384]{1,0:T(8,128)(2,1)S(1)}, bf16[1024,384]{1,0:T(8,128)(2,1)S(1)}, u32[]{:S(2)}, u32[]{:S(2)}) collective-permute-start(bf16[1024,384]{1,0:T(8,128)(2,1)S(1)} %copy-done.34), channel_id=1, source_target_pairs={{0,24},{8,16},{16,8},{24,0},{1,25},{9,17},{17,9},{25,1},{2,26},{10... | collective-permute-start | bytes 2359304 | tf_op jit(solution)/shard_map/ppermute | solution.py:604
  19.9 44.3 %collective-permute-start.4 = (bf16[1024,384]{1,0:T(8,128)(2,1)S(1)}, bf16[1024,384]{1,0:T(8,128)(2,1)}, u32[]{:S(2)}, u32[]{:S(2)}) collective-permute-start(bf16[1024,384]{1,0:T(8,128)(2,1)S(1)} %copy-done.34), channel_id=1, source_target_pairs={{0,16},{8,24},{16,0},{24,8},{1,17},{9,25},{17,1},{25,9},{2,18},{10... | collective-permute-start | bytes 2359304 | tf_op jit(solution)/shard_map/ppermute | solution.py:604
  20.5 43.8 %collective-permute-start.3 = (bf16[1024,384]{1,0:T(8,128)(2,1)S(1)}, bf16[1024,384]{1,0:T(8,128)(2,1)}, u32[]{:S(2)}, u32[]{:S(2)}) collective-permute-start(bf16[1024,384]{1,0:T(8,128)(2,1)S(1)} %copy-done.34), channel_id=1, source_target_pairs={{0,8},{8,0},{16,24},{24,16},{1,9},{9,1},{17,25},{25,17},{2,10},{10... | collective-permute-start | bytes 2359304 | tf_op jit(solution)/shard_map/ppermute | solution.py:604
  46.2 1.1 copy-start
  47.4 0.9 copy-start.13
  48.3 0.9 copy-start.14
  49.1 0.9 copy-start.15
  50.7 27.9 %collective-permute-start.8 = (bf16[1024,384]{1,0:T(8,128)(2,1)}, bf16[1024,384]{1,0:T(8,128)(2,1)}, u32[]{:S(2)}, u32[]{:S(2)}) collective-permute-start(bf16[1024,384]{1,0:T(8,128)(2,1)} %get-tuple-element.52.rest_0_), channel_id=1, source_target_pairs={{0,24},{8,16},{16,8},{24,0},{1,25},{9,17},{17,9},{25,1},{2,26},{10... | collective-permute-start | bytes 2359304 | tf_op jit(solution)/shard_map/ppermute | solution.py:604
  59.8 32.9 %collective-permute-start.7 = (bf16[1024,384]{1,0:T(8,128)(2,1)}, bf16[1024,384]{1,0:T(8,128)(2,1)}, u32[]{:S(2)}, u32[]{:S(2)}) collective-permute-start(bf16[1024,384]{1,0:T(8,128)(2,1)} %get-tuple-element.52.rest_0_), channel_id=1, source_target_pairs={{0,16},{8,24},{16,0},{24,8},{1,17},{9,25},{17,1},{25,9},{2,18},{10... | collective-permute-start | bytes 2359304 | tf_op jit(solution)/shard_map/ppermute | solution.py:604
  60.4 3.9 %copy-start.38 = (bf16[1024,384]{1,0:T(8,128)(2,1)}, bf16[1024,384]{1,0:T(8,128)(2,1)S(1)}, u32[]{:S(2)}) copy-start(bf16[1024,384]{1,0:T(8,128)(2,1)S(1)} %collective-permute-done.5.rest_3_) | copy-start | bytes 2359300
  60.4 33.6 %collective-permute-start.6 = (bf16[1024,384]{1,0:T(8,128)(2,1)}, bf16[1024,384]{1,0:T(8,128)(2,1)}, u32[]{:S(2)}, u32[]{:S(2)}) collective-permute-start(bf16[1024,384]{1,0:T(8,128)(2,1)} %get-tuple-element.52.rest_0_), channel_id=1, source_target_pairs={{0,8},{8,0},{16,24},{24,16},{1,9},{9,1},{17,25},{25,17},{2,10},{10... | collective-permute-start | bytes 2359304 | tf_op jit(solution)/shard_map/ppermute | solution.py:604
  143.6 206.7 %reduce-scatter.5.cloned.1.call-start = ((), (), s32[]{:S(2)}) async-start(), calls=%async_computation.5 | async-start | bytes 5308416 | tf_op jit(solution)/shard_map/reduce_scatter | solution.py:713
  179.4 35.2 %collective-permute-start.12 = (bf16[1024,384]{1,0:T(8,128)(2,1)}, bf16[1024,384]{1,0:T(8,128)(2,1)}, u32[]{:S(2)}, u32[]{:S(2)}) collective-permute-start(bf16[1024,384]{1,0:T(8,128)(2,1)} %get-tuple-element.69), channel_id=1, source_target_pairs={{0,8},{8,0},{16,24},{24,16},{1,9},{9,1},{17,25},{25,17},{2,10},{10... | collective-permute-start | bytes 2359304 | tf_op jit(solution)/shard_map/ppermute | solution.py:604
  180.0 36.2 %collective-permute-start.13 = (bf16[1024,384]{1,0:T(8,128)(2,1)}, bf16[1024,384]{1,0:T(8,128)(2,1)}, u32[]{:S(2)}, u32[]{:S(2)}) collective-permute-start(bf16[1024,384]{1,0:T(8,128)(2,1)} %get-tuple-element.70), channel_id=1, source_target_pairs={{0,16},{8,24},{16,0},{24,8},{1,17},{9,25},{17,1},{25,9},{2,18},{10... | collective-permute-start | bytes 2359304 | tf_op jit(solution)/shard_map/ppermute | solution.py:604
  181.4 34.8 %collective-permute-start.14 = (bf16[1024,384]{1,0:T(8,128)(2,1)}, bf16[1024,384]{1,0:T(8,128)(2,1)}, u32[]{:S(2)}, u32[]{:S(2)}) collective-permute-start(bf16[1024,384]{1,0:T(8,128)(2,1)} %get-tuple-element.71), channel_id=1, source_target_pairs={{0,24},{8,16},{16,8},{24,0},{1,25},{9,17},{17,9},{25,1},{2,26},{10... | collective-permute-start | bytes 2359304 | tf_op jit(solution)/shard_map/ppermute | solution.py:604
  214.5 1.8 copy-start.3
  214.5 1.7 copy-start.5
  214.5 1.7 copy-start.6
  214.5 1.7 copy-start.8
  214.5 1.7 copy-start.10
  214.5 1.7 copy-start.12
  214.6 1.7 copy-start.17
  247.2 2.3 collective-permute-start.15
  251.6 16.4 %collective-permute-start.16 = (bf16[192,896]{1,0:T(8,128)(2,1)S(1)}, bf16[192,896]{1,0:T(8,128)(2,1)S(1)}, u32[]{:S(2)}, u32[]{:S(2)}) collective-permute-start(bf16[192,896]{1,0:T(8,128)(2,1)S(1)} %select_convert_fusion.1), channel_id=1, source_target_pairs={{0,8},{8,0},{16,24},{24,16},{1,9},{9,1},{17,25},{25,17},{2,10},{10... | collective-permute-start | bytes 1032200 | tf_op jit(solution)/shard_map/ppermute | solution.py:628
  268.2 5.9 %collective-permute-start.17 = (bf16[96,896]{1,0:T(8,128)(2,1)S(1)}, bf16[96,896]{1,0:T(8,128)(2,1)S(1)}, u32[]{:S(2)}, u32[]{:S(2)}) collective-permute-start(bf16[96,896]{1,0:T(8,128)(2,1)S(1)} %select_convert_fusion.2), channel_id=1, source_target_pairs={{0,16},{8,24},{16,0},{24,8},{1,17},{9,25},{17,1},{25,9},{2,18},{10... | collective-permute-start | bytes 516104 | tf_op jit(solution)/shard_map/ppermute | solution.py:628
  274.2 4.6 %collective-permute-start.18 = (bf16[48,896]{1,0:T(8,128)(2,1)S(1)}, bf16[48,896]{1,0:T(8,128)(2,1)S(1)}, u32[]{:S(2)}, u32[]{:S(2)}) collective-permute-start(bf16[48,896]{1,0:T(8,128)(2,1)S(1)} %select_convert_fusion.3), channel_id=1, source_target_pairs={{0,2},{1,3},{2,0},{3,1},{4,6},{5,7},{6,4},{7,5},{8,10},{9,11},{10,... | collective-permute-start | bytes 258056 | tf_op jit(solution)/shard_map/ppermute | solution.py:628
  278.8 24.4 %copy-start.37 = (bf16[1024,384]{1,0:T(8,128)(2,1)S(1)}, bf16[1024,384]{1,0:T(8,128)(2,1)}, u32[]{:S(2)}) copy-start(bf16[1024,384]{1,0:T(8,128)(2,1)} %get-tuple-element.60) | copy-start | bytes 2359300
  278.8 24.8 %copy-start.36 = (bf16[1024,384]{1,0:T(8,128)(2,1)S(1)}, bf16[1024,384]{1,0:T(8,128)(2,1)}, u32[]{:S(2)}) copy-start(bf16[1024,384]{1,0:T(8,128)(2,1)} %get-tuple-element.61) | copy-start | bytes 2359300
  278.8 26.6 %copy-start.35 = (bf16[1024,384]{1,0:T(8,128)(2,1)S(1)}, bf16[1024,384]{1,0:T(8,128)(2,1)}, u32[]{:S(2)}) copy-start(bf16[1024,384]{1,0:T(8,128)(2,1)} %get-tuple-element.62) | copy-start | bytes 2359300
  278.8 5.0 %collective-permute-start.19 = (bf16[24,896]{1,0:T(8,128)(2,1)S(1)}, bf16[24,896]{1,0:T(8,128)(2,1)S(1)}, u32[]{:S(2)}, u32[]{:S(2)}) collective-permute-start(bf16[24,896]{1,0:T(8,128)(2,1)S(1)} %select_convert_fusion.4), channel_id=1, source_target_pairs={{0,4},{1,5},{2,6},{3,7},{4,0},{5,1},{6,2},{7,3},{8,12},{9,13},{10,... | collective-permute-start | bytes 129032 | tf_op jit(solution)/shard_map/ppermute | solution.py:628
  283.8 5.0 %collective-permute-start.20 = (bf16[24,896]{1,0:T(8,128)(2,1)S(1)}, bf16[24,896]{1,0:T(8,128)(2,1)S(1)}, u32[]{:S(2)}, u32[]{:S(2)}) collective-permute-start(bf16[24,896]{1,0:T(8,128)(2,1)S(1)} %add_convert_fusion.1), channel_id=1, source_target_pairs={{0,4},{1,5},{2,6},{3,7},{4,0},{5,1},{6,2},{7,3},{8,12},{9,13},{10,... | collective-permute-start | bytes 129032 | tf_op jit(solution)/shard_map/ppermute | solution.py:636
  288.9 5.3 %collective-permute-start.21 = (bf16[48,896]{1,0:T(8,128)(2,1)S(1)}, bf16[48,896]{1,0:T(8,128)(2,1)S(1)}, u32[]{:S(2)}, u32[]{:S(2)}) collective-permute-start(bf16[48,896]{1,0:T(8,128)(2,1)S(1)} %pad_maximum_fusion.7), channel_id=1, source_target_pairs={{0,2},{1,3},{2,0},{3,1},{4,6},{5,7},{6,4},{7,5},{8,10},{9,11},{10,... | collective-permute-start | bytes 258056 | tf_op jit(solution)/shard_map/ppermute | solution.py:636
  294.2 7.2 %collective-permute-start.22 = (bf16[96,896]{1,0:T(8,128)(2,1)S(1)}, bf16[96,896]{1,0:T(8,128)(2,1)S(1)}, u32[]{:S(2)}, u32[]{:S(2)}) collective-permute-start(bf16[96,896]{1,0:T(8,128)(2,1)S(1)} %pad_maximum_fusion.5), channel_id=1, source_target_pairs={{0,16},{8,24},{16,0},{24,8},{1,17},{9,25},{17,1},{25,9},{2,18},{10... | collective-permute-start | bytes 516104 | tf_op jit(solution)/shard_map/ppermute | solution.py:636
  301.5 11.0 %collective-permute-start.23 = (bf16[192,896]{1,0:T(8,128)(2,1)S(1)}, bf16[192,896]{1,0:T(8,128)(2,1)S(1)}, u32[]{:S(2)}, u32[]{:S(2)}) collective-permute-start(bf16[192,896]{1,0:T(8,128)(2,1)S(1)} %pad_maximum_fusion.3), channel_id=1, source_target_pairs={{0,8},{8,0},{16,24},{24,16},{1,9},{9,1},{17,25},{25,17},{2,10},{10... | collective-permute-start | bytes 1032200 | tf_op jit(solution)/shard_map/ppermute | solution.py:636
  303.2 26.0 %collective-permute-start.9 = (bf16[1024,384]{1,0:T(8,128)(2,1)S(1)}, bf16[1024,384]{1,0:T(8,128)(2,1)S(1)}, u32[]{:S(2)}, u32[]{:S(2)}) collective-permute-start(bf16[1024,384]{1,0:T(8,128)(2,1)S(1)} %copy-done.37), channel_id=1, source_target_pairs={{0,8},{8,0},{16,24},{24,16},{1,9},{9,1},{17,25},{25,17},{2,10},{10... | collective-permute-start | bytes 2359304 | tf_op jit(solution)/shard_map/ppermute | solution.py:604
  303.6 25.6 %collective-permute-start.10 = (bf16[1024,384]{1,0:T(8,128)(2,1)S(1)}, bf16[1024,384]{1,0:T(8,128)(2,1)S(1)}, u32[]{:S(2)}, u32[]{:S(2)}) collective-permute-start(bf16[1024,384]{1,0:T(8,128)(2,1)S(1)} %copy-done.36), channel_id=1, source_target_pairs={{0,16},{8,24},{16,0},{24,8},{1,17},{9,25},{17,1},{25,9},{2,18},{10... | collective-permute-start | bytes 2359304 | tf_op jit(solution)/shard_map/ppermute | solution.py:604
  305.4 33.4 %copy-start.1 = (f32[1024,384]{1,0:T(8,128)S(1)}, f32[1024,384]{1,0:T(8,128)}, u32[]{:S(2)}) copy-start(f32[1024,384]{1,0:T(8,128)} %copy-done) | copy-start | bytes 4718596
  305.4 33.4 %copy-start.26 = (bf16[1024,384]{1,0:T(8,128)(2,1)S(1)}, bf16[1024,384]{1,0:T(8,128)(2,1)}, u32[]{:S(2)}) copy-start(bf16[1024,384]{1,0:T(8,128)(2,1)} %get-tuple-element.59) | copy-start | bytes 2359300
  305.4 33.4 %collective-permute-start.11 = (bf16[1024,384]{1,0:T(8,128)(2,1)S(1)}, bf16[1024,384]{1,0:T(8,128)(2,1)S(1)}, u32[]{:S(2)}, u32[]{:S(2)}) collective-permute-start(bf16[1024,384]{1,0:T(8,128)(2,1)S(1)} %copy-done.35), channel_id=1, source_target_pairs={{0,24},{8,16},{16,8},{24,0},{1,25},{9,17},{17,9},{25,1},{2,26},{10... | collective-permute-start | bytes 2359304 | tf_op jit(solution)/shard_map/ppermute | solution.py:604
  312.7 27.5 %collective-permute-start.24 = (bf16[384,896]{1,0:T(8,128)(2,1)S(1)}, bf16[384,896]{1,0:T(8,128)(2,1)S(1)}, u32[]{:S(2)}, u32[]{:S(2)}) collective-permute-start(bf16[384,896]{1,0:T(8,128)(2,1)S(1)} %pad_maximum_fusion.2), channel_id=1, source_target_pairs={{0,1},{1,0},{2,3},{3,2},{4,5},{5,4},{6,7},{7,6},{8,9},{9,8},{10,11... | collective-permute-start | bytes 2064392 | tf_op jit(solution)/shard_map/ppermute | solution.py:636
  340.7 1.5 copy-start.27
  340.7 1.5 copy-start.28
  340.9 2.8 copy-start.22
  342.3 2.2 copy-start.20
  342.3 2.7 copy-start.21
  350.3 3.7 %copy-start.24 = (f32[192,4,384]{2,1,0:T(4,128)S(1)}, f32[192,4,384]{2,1,0:T(4,128)}, u32[]{:S(2)}) copy-start(f32[192,4,384]{2,1,0:T(4,128)} %param.36) | copy-start | bytes 3538948
  350.3 3.7 %copy-start.25 = (f32[192,4,384]{2,1,0:T(4,128)S(1)}, f32[192,4,384]{2,1,0:T(4,128)}, u32[]{:S(2)}) copy-start(f32[192,4,384]{2,1,0:T(4,128)} %param.35) | copy-start | bytes 3538948
  352.9 1.3 copy-start.18
  352.9 1.6 copy-start.19
  352.9 2.0 copy-start.23
  (4 other events, 2.9 us)
Sparse Core Ops, SparseCore 0:
  14.2 51.0 all-gather.4
  67.5 49.9 all-gather.2
  143.7 52.4 reduce-scatter.2
  214.7 52.3 reduce-scatter.4
